TPU v7x, 32 devices: a whole 2x2x4 slice. The times are simulated.
32 devices in a mesh: cube: 16 (over z, y, x), cores: 2 (over core).
Axes of the slice: x: 2, y: 2, z: 4, core: 2. Of those that a mesh axis runs over, the one named last changes fastest.
Arguments:
- rhs: float32 [4, 8192, 256], P(None, ('cube', 'cores')), may hold values from -6 to 6
- dinv: float32 [4, 8192, 512], P(None, ('cube', 'cores')), may hold values from -1 to 2.5, as said below
- own_update: float32 [4, 8192, 512], P(None, ('cube', 'cores')), may hold values from -0.125 to 0.125
- partner_update: float32 [4, 8192, 512], P(None, ('cube', 'cores')), may hold values from -0.125 to 0.125
- cot_solved: float32 [4, 8192, 256], P(None, ('cube', 'cores')), may hold values from -6 to 6
- cot_top: float32 [8192, 256], P(('cube', 'cores')), may hold values from -6 to 6
- elem_map: int32 [16, 512], P('cube'), may hold values from 0 to 511, each once within a row
Outputs:
- solved: float32 [4, 8192, 256], P(None, ('cube', 'cores'))
- top_update: float32 [8192, 256], P(('cube', 'cores'))
- grad_rhs: float32 [4, 8192, 256], P(None, ('cube', 'cores'))
- element_grad: float32 [4, 512, 8192], P(None, 'cube', 'cores')
Inputs may be any that keep to these rules, and one draw needn't show every extreme that they name: Each row of elem_map is a permutation of 0 .. 511. Each block of dinv is the inverse of a well conditioned diagonal block.
All inputs are finite; a program needn't handle non-finite values.
Results may differ from a plain program's by a relative error of at most 0.00012.
Values sent between devices are 32-bit elements; how exact they have to be, the bound alone decides.
No kernel may reach another device: no remote copies, remote signals or barrier semaphores. Data moves between devices by JAX's collectives and lax.ppermute only.
A program may use at most 64 MiB of HBM per device.

v0:
```python
import functools
import types

import jax
import jax.numpy as jnp
from jax import lax
from jax.experimental import pallas as pl
from jax.experimental.pallas import tpu as pltpu
from jax.sharding import PartitionSpec as P

F32, BF16 = jnp.float32, jnp.bfloat16
VMEM = pltpu.VMEM
NEAR = 4


def partner(x, distance):
    return lax.ppermute(x, "cube", [(i, i ^ 1 << distance) for i in range(lax.axis_size("cube"))])


def swap(x):
    return lax.ppermute(x, "cores", [(0, 1), (1, 0)])


def split(x):
    hi = x.astype(BF16)
    return hi, (x - hi.astype(F32)).astype(BF16)


def dot(a, b):
    return lax.dot_general(a, b, (((1,), (0,)), ((), ())), preferred_element_type=F32)


def mul(hi, lo, v):
    n = v.shape[1]
    vh, vl = split(v)
    t = dot(hi, jnp.concatenate([vh, vl], axis=1))
    return t[:, :n] + t[:, n:] + dot(lo, vh)


def mul_t(v, hi, lo):
    n = v.shape[0]
    vh, vl = split(v)
    t = dot(jnp.concatenate([vh, vl], axis=0), hi)
    return t[:n] + t[n:] + dot(vh, lo)


class Sequence:
    def __init__(self):
        self.last = None

    def __call__(self, kernel, args, outs, scratch=(), limit=8, hbm=()):
        args = list(args)
        if self.last is not None:
            args[0] = after(args[0], self.last)
        for i in hbm:
            args[i] = pltpu.with_memory_space_constraint(args[i], pltpu.HBM)
        res = pl.pallas_call(
            kernel,
            out_shape=tuple(outs),
            in_specs=[pl.BlockSpec(memory_space=pltpu.HBM if i in hbm else VMEM) for i in range(len(args))],
            out_specs=tuple(pl.BlockSpec(memory_space=VMEM) for _ in outs),
            scratch_shapes=list(scratch),
            compiler_params=pltpu.CompilerParams(vmem_limit_bytes=limit << 20),
        )(*args)
        self.last = res[0]
        return res

    def named(self, kernel, args, outs, **more):
        def body(*refs):
            ins, rest = refs[: len(args)], refs[len(args) :]
            kernel(
                types.SimpleNamespace(**dict(zip(args, ins))),
                types.SimpleNamespace(**dict(zip(outs, rest))),
                *rest[len(outs) :],
            )

        return dict(zip(outs, self(body, args.values(), outs.values(), **more)))


def shape(*s, dtype=F32):
    return jax.ShapeDtypeStruct(s, dtype)


def after(x, *others):
    return lax.optimization_barrier((x, *others))[0]


def halves(h):
    c = lax.axis_index("cores")
    return pl.multiple_of(c * h, h), pl.multiple_of((1 - c) * h, h)


def whole(m_ref, t_ref, level, hi_ref, lo_ref):
    h = hi_ref.shape[0] // 2
    for ref, off in zip((m_ref, t_ref), halves(h)):
        hi, lo = split(ref[...] if level is None else ref[level])
        hi_ref[pl.ds(off, h), :] = hi
        lo_ref[pl.ds(off, h), :] = lo


def take_kernel(last, far_ref, dinv_ref, pf_ref, d0_ref, sem):
    copies = [
        pltpu.make_async_copy(far_ref.at[last], pf_ref, sem.at[0]),
        pltpu.make_async_copy(dinv_ref.at[0], d0_ref, sem.at[1]),
    ]
    for copy in copies:
        copy.start()
    for copy in copies:
        copy.wait()


def first_kernel(refs, outs):
    h, k = refs.top.shape[0], refs.top.shape[1] // 2
    mine, theirs = halves(k)
    row_mine, row_theirs = halves(h)
    whole(refs.pf, refs.pf_t, None, outs.ph, outs.pl)
    outs.wm[...] = refs.top[:, pl.ds(mine, k)].T
    outs.w[:, pl.ds(row_mine, h)] = outs.wm[...]
    outs.w[:, pl.ds(row_theirs, h)] = refs.top_t[:, pl.ds(mine, k)].T
    outs.y[...] = mul_t(outs.w[...], outs.ph[...], outs.pl[...])
    whole(refs.d0, refs.d0_t, None, outs.dh, outs.dl)
    for level in range(refs.rhs.shape[0]):
        outs.rows[level, pl.ds(row_mine, h), :] = refs.rhs[level, :, pl.ds(mine, k)]
        outs.rows[level, pl.ds(row_theirs, h), :] = refs.rhs_t[level, :, pl.ds(mine, k)]
    outs.s[...] = mul(outs.dh[...], outs.dl[...], outs.rows[0])
    outs.wt[...] = refs.top[:, pl.ds(theirs, k)].T


def prep_kernel(new, refs, outs, buf, sem):
    copies = [
        pltpu.make_async_copy(getattr(refs, name).at[level], buf.at[i], sem.at[i])
        for i, (name, level) in enumerate(new)
    ]
    for copy in copies:
        copy.start()
    for i, (name, level) in enumerate(new):
        copies[i].wait()
        hi, lo = getattr(outs, f"{name}{level}h"), getattr(outs, f"{name}{level}l")
        h = hi.shape[0] // 2
        mine, theirs = halves(h)
        for v, off in ((buf[i], mine), (getattr(refs, name + "_t")[level], theirs)):
            v_hi, v_lo = split(v)
            hi[pl.ds(off, h), :] = v_hi
            lo[pl.ds(off, h), :] = v_lo


def own_kernel(lb, refs, outs):
    outs.a[...] = mul(refs.ph[...], refs.pl[...], refs.s[...])
    h, k = refs.cot.shape[1], refs.cot.shape[2] // 2
    mine, _ = halves(k)
    for ref, off in zip((refs.cot, refs.cot_t), halves(h)):
        outs.b[:, pl.ds(off, h)] = ref[lb, :, pl.ds(mine, k)].T
    outs.b[...] += mul_t(refs.w[...], refs.qh[...], refs.ql[...])


def fwd_next(level, refs, outs):
    u = refs.a[...] + mul(refs.ph[...], refs.pl[...], refs.sp[...])
    outs.s[...] = mul(refs.dh[...], refs.dl[...], refs.rows[level] - u)


def bwd_next(refs, outs):
    outs.w[...] = -mul_t(refs.b[...] + refs.yp[...], refs.dh[...], refs.dl[...])
    outs.y[...] = mul_t(outs.w[...], refs.ph[...], refs.pl[...])
    h = outs.wm.shape[1]
    mine, theirs = halves(h)
    outs.wm[...] = outs.w[:, pl.ds(mine, h)]
    outs.ws[...] = outs.w[:, pl.ds(theirs, h)]


def bwd_last(refs, outs):
    w = refs.b[...] + refs.yp[...]
    outs.g[...] = -mul_t(w, refs.dh[...], refs.dl[...])
    h = outs.gm.shape[1]
    mine, theirs = halves(h)
    outs.gm[...] = outs.g[:, pl.ds(mine, h)]
    outs.gs[...] = outs.g[:, pl.ds(theirs, h)]


def fwd_last(refs, outs):
    outs.u[...] = refs.a[...] + mul(refs.ph[...], refs.pl[...], refs.sp[...])
    h = outs.um.shape[0]
    mine, theirs = halves(h)
    outs.um[...] = outs.u[pl.ds(mine, h), :]
    outs.us[...] = outs.u[pl.ds(theirs, h), :]


def outer_kernel(batch, by_near, map_ref, *refs):
    ins, outs = refs[: 4 * batch], refs[4 * batch :]
    r = ins[0].shape[0]
    e = outs[0].shape[2]
    target = map_ref[...] ^ (lax.axis_index("cube") * e)
    pick = jnp.where(lax.broadcasted_iota(jnp.int32, (r, r), 0) == target, 1.0, 0.0).astype(BF16)
    for i in range(batch):
        s_ref, st_ref, wm_ref, wt_ref = ins[4 * i : 4 * i + 4]
        sh, sl = split(jnp.concatenate([s_ref[...], st_ref[...]], axis=1))
        ph = dot(pick, sh).astype(BF16)
        plo = dot(pick, sl).astype(BF16)
        wh, wl = split(jnp.concatenate([wm_ref[...], wt_ref[...]], axis=0))
        o = dot(ph, wh) + dot(ph, wl) + dot(plo, wh)
        for j, out in enumerate(outs):
            for q in range(out.shape[1]):
                at = (j + NEAR * q if by_near else q + NEAR * j) * e
                out[i, q] = o[at : at + e]


def turn_kernel(n_in, *refs):
    ins, outs = refs[:n_in], refs[n_in:]
    for q, out in enumerate(outs):
        for j, ref in enumerate(ins):
            for i in range(ref.shape[0]):
                out[i, j] = ref[i, q]


def results_kernel(*refs):
    solved_ref, grad_ref = refs[-2:]
    levels, h, k = solved_ref.shape
    k //= 2
    mine, _ = halves(h)
    own, other = (pl.ds(x, k) for x in halves(k))
    for level in range(levels):
        s_ref, st_ref, gm_ref, gt_ref = refs[4 * level : 4 * level + 4]
        solved_ref[level, :, own] = s_ref[pl.ds(mine, h), :]
        solved_ref[level, :, other] = st_ref[pl.ds(mine, h), :]
        grad_ref[level, :, own] = -gm_ref[...].T
        grad_ref[level, :, other] = -gt_ref[...].T


def join_kernel(m_ref, t_ref, o_ref):
    k = m_ref.shape[1]
    own, other = (pl.ds(x, k) for x in halves(k))
    o_ref[:, own] = m_ref[...]
    o_ref[:, other] = t_ref[...]


def place_kernel(plan, *refs):
    o_ref, sem = refs[-2:]
    me = lax.axis_index("cube")
    h = refs[0].shape[-1]
    copies = []
    for i, (array, index, level, source) in enumerate(plan):
        col = pl.multiple_of((me ^ source) * h, h)
        copies.append(
            pltpu.make_async_copy(refs[array].at[index], o_ref.at[level, :, pl.ds(col, h)], sem.at[i])
        )
    for copy in copies:
        copy.start()
    for copy in copies:
        copy.wait()


def place(run, blocks, plan, out, so_far=None):
    more = [] if so_far is None else [so_far]
    res = pl.pallas_call(
        functools.partial(place_kernel, plan),
        out_shape=out,
        in_specs=[pl.BlockSpec(memory_space=pl.ANY)] * (len(blocks) + len(more)),
        out_specs=pl.BlockSpec(memory_space=pl.ANY),
        scratch_shapes=[pltpu.SemaphoreType.DMA((len(plan),))],
        input_output_aliases={len(blocks): 0} if more else {},
        compiler_params=pltpu.CompilerParams(vmem_limit_bytes=1 << 20),
    )(after(blocks[0], run.last), *blocks[1:], *more)
    run.last = res
    return res


def local(rhs, dinv, own, far, cot, top, elem_map):
    levels, h, k = rhs.shape
    r, kh = 2 * h, k // 2
    n = lax.axis_size("cube")
    base = n.bit_length() - 1 - levels
    last = levels - 1
    run = Sequence()
    vec, vec_t, half_t, front = shape(r, kh), shape(kh, r), shape(kh, h), shape(r, r, dtype=BF16)

    top_t = swap(top)
    pf, d0 = run(
        functools.partial(take_kernel, last),
        [far, dinv],
        [shape(h, r)] * 2,
        [pltpu.SemaphoreType.DMA((2,))],
        hbm=(0, 1),
    )
    pf_t, d0_t = swap(pf), swap(d0)
    rhs_t, cot_t = swap(rhs), swap(cot)
    x = run.named(
        first_kernel,
        {"pf": pf, "pf_t": pf_t, "d0": d0, "d0_t": d0_t, "top": top, "top_t": top_t, "rhs": rhs, "rhs_t": rhs_t},
        {
            "s": vec, "y": vec_t, "w": vec_t, "wm": half_t, "wt": half_t, "rows": shape(levels, r, kh),
            "ph": front, "pl": front, "dh": front, "dl": front,
        },
    )
    raw = {"far": far, "own": own, "dinv": dinv}
    raw.update({name + "_t": swap(after(v, top_t, pf_t, d0_t, rhs_t, cot_t)) for name, v in raw.items()})
    parts = {f"far{last}h": x["ph"], f"far{last}l": x["pl"], "dinv0h": x["dh"], "dinv0l": x["dl"]}
    rows = x["rows"]
    s, st, wm, wt = ([None] * levels for _ in range(4))
    s[0], w, y, wm[last], wt[last] = x["s"], x["w"], x["y"], x["wm"], x["wt"]
    st[0] = swap(s[0])

    nears, fars = range(NEAR), range(n // NEAR)

    def outer(batch, by_near):
        one = shape(len(batch), len(fars if by_near else nears), r // n, h)
        return run(
            functools.partial(outer_kernel, len(batch), by_near),
            [elem_map, *(v for q in batch for v in (s[q], st[q], wm[q], wt[q]))],
            [one] * len(nears if by_near else fars),
            limit=12,
        )

    def exchange(arrays, step):
        return [
            arrays[0],
            *(lax.ppermute(v, "cube", [(i, i ^ j * step) for i in range(n)]) for j, v in enumerate(arrays) if j),
        ]

    def turn(arrays):
        batch, count, e, width = arrays[0].shape
        return run(
            functools.partial(turn_kernel, len(arrays)), arrays, [shape(batch, len(arrays), e, width)] * count
        )

    early, late = list(range(1, levels - 1)), [0, last]
    for t in range(levels):
        lf, lb = t, last - t
        yp = partner(y, base + lb)
        if t < last:
            sp = partner(s[lf], base + lf)
        if t == 0:
            new = [(name, q) for name in raw if "_t" not in name for q in range(levels)]
            new = [q for q in new if f"{q[0]}{q[1]}h" not in parts]
            parts.update(
                run.named(
                    functools.partial(prep_kernel, new),
                    {"far_t": raw["far_t"], "own_t": raw["own_t"], "dinv_t": raw["dinv_t"],
                     "far": far, "own": own, "dinv": dinv},
                    {f"{name}{level}{e}": front for name, level in new for e in "hl"},
                    scratch=[VMEM((len(new), h, r), F32), pltpu.SemaphoreType.DMA((len(new),))],
                    hbm=(3, 4, 5),
                )
            )
        x = run.named(
            functools.partial(own_kernel, lb),
            {
                "s": s[lf], "w": w, "cot": cot, "cot_t": cot_t,
                "ph": parts[f"own{lf}h"], "pl": parts[f"own{lf}l"],
                "qh": parts[f"own{lb}h"], "ql": parts[f"own{lb}l"],
            },
            {"a": vec, "b": vec_t},
        )
        a, b = x["a"], x["b"]
        if t == levels - 2:
            crossed = exchange(outer(early, False), NEAR)
        if t < last:
            x = run.named(
                bwd_next,
                {
                    "b": b, "yp": yp,
                    **{p + e: parts[f"{q}{e}"] for e in "hl" for p, q in (("d", f"dinv{lb}"), ("p", f"far{lb - 1}"))},
                },
                {"y": vec_t, "w": vec_t, "wm": half_t, "ws": half_t},
            )
            w, y, wm[lb - 1], wt[lb - 1] = x["w"], x["y"], x["wm"], swap(x["ws"])
            x = run.named(
                functools.partial(fwd_next, t + 1),
                {
                    "a": a, "sp": sp, "rows": rows,
                    **{p + e: parts[f"{q}{e}"] for e in "hl" for p, q in (("p", f"far{lf}"), ("d", f"dinv{lf + 1}"))},
                },
                {"s": vec},
            )
            s[t + 1] = x["s"]
            st[t + 1] = swap(s[t + 1])
    late_in = turn(exchange(outer(late, True), 1))
    late_in = exchange(late_in, NEAR)
    g = run.named(
        bwd_last,
        {"b": b, "yp": yp, "dh": parts["dinv0h"], "dl": parts["dinv0l"]},
        {"g": vec_t, "gm": half_t, "gs": half_t},
    )
    gms, gts = [g["gm"], *wm[:last]], [swap(g["gs"]), *wt[:last]]
    early_in = exchange(turn(crossed), 1)
    sp = partner(after(s[last], *crossed), base + last)
    solved, grads = run(
        results_kernel,
        [v for q in range(levels) for v in (s[q], st[q], gms[q], gts[q])],
        [shape(levels, h, k), shape(levels, h, k)],
    )
    out = shape(levels, r // n, n * h)
    plan = [(m, (i, f), lv, m + NEAR * f) for m in nears for f in fars for i, lv in enumerate(early)]
    element_grad = place(run, early_in, plan, out)
    u = run.named(
        fwd_last,
        {"a": a, "sp": sp, "ph": parts[f"far{last}h"], "pl": parts[f"far{last}l"]},
        {"u": vec, "um": shape(h, kh), "us": shape(h, kh)},
    )
    top_update, = run(join_kernel, [u["um"], swap(u["us"])], [shape(h, k)])
    plan = [(f, (i, m), lv, m + NEAR * f) for m in nears for f in fars for i, lv in enumerate(late)]
    element_grad = place(run, late_in, plan, out, element_grad)
    return solved, top_update, grads, element_grad


def solution(mesh):
    rows = P(None, ("cube", "cores"), None)
    return jax.shard_map(
        local,
        mesh=mesh,
        in_specs=(rows, rows, rows, rows, rows, P(("cube", "cores"), None), P("cube", None)),
        out_specs=(rows, P(("cube", "cores"), None), rows, P(None, "cube", "cores")),
        check_vma=False,
    )
```

profile of v0, /device:TPU:8, one launch (start us, length us, event | category | flops | bytes accessed | tf_op | source)
XLA Modules:
  0.0 113.7 jit_solution(6306840693994869777)
XLA Ops:
  0.7 0.5 collective-permute-start.4
  1.2 1.3 %shard_map.102 = (f32[256,512]{1,0:T(8,128)S(1)}, f32[256,512]{1,0:T(8,128)S(1)}) custom-call(f32[4,256,512]{2,1,0:T(8,128)} %refs_3_.1, f32[4,256,512]{2,1,0:T(8,128)} %refs_5_.1), custom_call_target="tpu_custom_call" | custom-call | tf_op jit(solution)/shard_map/pallas_call | solution.py:57
  2.6 0.1 collective-permute-start
  2.7 0.5 collective-permute-start.1
  3.2 0.1 collective-permute-start.2
  3.2 3.5 %collective-permute-done.2.refs_5_ = f32[256,256]{1,0:T(8,128)S(1)} collective-permute-done((f32[256,256]{1,0:T(8,128)S(1)}, f32[256,256]{1,0:T(8,128)S(1)}, u32[]{:S(2)}, u32[]{:S(2)}) %collective-permute-start.2) | collective-permute-done | bytes 262176 | tf_op jit(solution)/shard_map/ppermute | solution.py:21
  6.8 0.2 collective-permute-start.5
  7.0 0.4 collective-permute-start.6
  7.4 0.1 collective-permute-start.7
  7.5 1.0 shard_map.103
  8.5 2.7 %collective-permute-start.8 = (f32[128,512]{1,0:T(8,128)S(1)}, f32[128,512]{1,0:T(8,128)S(1)}, u32[]{:S(2)}, u32[]{:S(2)}) collective-permute-start(f32[128,512]{1,0:T(8,128)S(1)} %get-tuple-element.119), channel_id=1, source_target_pairs={{0,16},{2,18},{4,20},{6,22},{8,24},{10,26},{12,28},{14,30},{16,0},... | collective-permute-start | bytes 786440 | tf_op jit(solution)/shard_map/ppermute | solution.py:17
  11.2 1.5 %collective-permute-start.9 = (f32[512,128]{1,0:T(8,128)S(1)}, f32[512,128]{1,0:T(8,128)S(1)}, u32[]{:S(2)}, u32[]{:S(2)}) collective-permute-start(f32[512,128]{1,0:T(8,128)S(1)} %get-tuple-element.158.refs_0_), channel_id=1, source_target_pairs={{0,2},{2,0},{4,6},{6,4},{8,10},{10,8},{12,14},{14,12},{16,18},{18,... | collective-permute-start | bytes 786440 | tf_op jit(solution)/shard_map/ppermute | solution.py:17
  12.7 1.5 %collective-permute-done.6.refs_1_ = f32[4,256,512]{2,1,0:T(8,128)S(1)} collective-permute-done((f32[4,256,512]{2,1,0:T(8,128)}, f32[4,256,512]{2,1,0:T(8,128)S(1)}, u32[]{:S(2)}, u32[]{:S(2)}) %collective-permute-start.6) | collective-permute-done | bytes 2097184 | tf_op jit(solution)/shard_map/ppermute | solution.py:21
  14.2 3.0 %collective-permute-done.7.refs_2_ = f32[4,256,512]{2,1,0:T(8,128)S(1)} collective-permute-done((f32[4,256,512]{2,1,0:T(8,128)}, f32[4,256,512]{2,1,0:T(8,128)S(1)}, u32[]{:S(2)}, u32[]{:S(2)}) %collective-permute-start.7) | collective-permute-done | bytes 2097184 | tf_op jit(solution)/shard_map/ppermute | solution.py:21
  17.2 3.0 %shard_map.104 = (bf16[512,512]{1,0:T(8,128)(2,1)S(1)}, bf16[512,512]{1,0:T(8,128)(2,1)S(1)}, bf16[512,512]{1,0:T(8,128)(2,1)S(1)}, bf16[512,512]{1,0:T(8,128)(2...) custom-call(f32[4,256,512]{2,1,0:T(8,128)S(1)} %collective-permute-d, ...), custom_call_target="tpu_custom_call" | custom-call | tf_op jit(solution)/shard_map/pallas_call | solution.py:57
  20.2 0.6 shard_map.105
  20.9 1.9 %collective-permute-done.8.refs_1_ = f32[128,512]{1,0:T(8,128)S(1)} collective-permute-done((f32[128,512]{1,0:T(8,128)S(1)}, f32[128,512]{1,0:T(8,128)S(1)}, u32[]{:S(2)}, u32[]{:S(2)}) %collective-permute-start.8) | collective-permute-done | bytes 262176 | tf_op jit(solution)/shard_map/ppermute | solution.py:17
  22.8 0.8 shard_map.106
  23.6 1.3 %collective-permute-start.10 = (f32[128,512]{1,0:T(8,128)S(1)}, f32[128,512]{1,0:T(8,128)S(1)}, u32[]{:S(2)}, u32[]{:S(2)}) collective-permute-start(f32[128,512]{1,0:T(8,128)S(1)} %get-tuple-element.124), channel_id=1, source_target_pairs={{0,8},{2,10},{4,12},{6,14},{8,0},{10,2},{12,4},{14,6},{16,24},{18,... | collective-permute-start | bytes 786440 | tf_op jit(solution)/shard_map/ppermute | solution.py:17
  24.9 0.8 shard_map.107.refs_0_.refs_4_
  25.7 1.6 %collective-permute-start.11 = (f32[512,128]{1,0:T(8,128)S(1)}, f32[512,128]{1,0:T(8,128)S(1)}, u32[]{:S(2)}, u32[]{:S(2)}) collective-permute-start(f32[512,128]{1,0:T(8,128)S(1)} %shard_map.107.refs_0_.refs_4_), channel_id=1, source_target_pairs={{0,4},{2,6},{4,0},{6,2},{8,12},{10,14},{12,8},{14,10},{16,20},{18,... | collective-permute-start | bytes 786440 | tf_op jit(solution)/shard_map/ppermute | solution.py:17
  27.4 0.6 shard_map.108
  28.0 0.6 collective-permute-start.15
  28.6 3.3 %collective-permute-done.10.refs_1_ = f32[128,512]{1,0:T(8,128)S(1)} collective-permute-done((f32[128,512]{1,0:T(8,128)S(1)}, f32[128,512]{1,0:T(8,128)S(1)}, u32[]{:S(2)}, u32[]{:S(2)}) %collective-permute-start.10) | collective-permute-done | bytes 262176 | tf_op jit(solution)/shard_map/ppermute | solution.py:17
  31.9 0.7 shard_map.109
  32.7 0.9 collective-permute-done.11.refs_1_
  33.5 0.8 shard_map.110.refs_0_.refs_4_.refs_8_
  34.4 1.4 %collective-permute-start.20 = (f32[128,512]{1,0:T(8,128)S(1)}, f32[128,512]{1,0:T(8,128)S(1)}, u32[]{:S(2)}, u32[]{:S(2)}) collective-permute-start(f32[128,512]{1,0:T(8,128)S(1)} %get-tuple-element.143), channel_id=1, source_target_pairs={{0,4},{2,6},{4,0},{6,2},{8,12},{10,14},{12,8},{14,10},{16,20},{18,... | collective-permute-start | bytes 786440 | tf_op jit(solution)/shard_map/ppermute | solution.py:17
  35.8 1.2 %collective-permute-start.21 = (f32[512,128]{1,0:T(8,128)S(1)}, f32[512,128]{1,0:T(8,128)S(1)}, u32[]{:S(2)}, u32[]{:S(2)}) collective-permute-start(f32[512,128]{1,0:T(8,128)S(1)} %shard_map.110.refs_0_.refs_4_.refs_8_), channel_id=1, source_target_pairs={{0,8},{2,10},{4,12},{6,14},{8,0},{10,2},{12,4},{14,6},{16,24},{18,... | collective-permute-start | bytes 786440 | tf_op jit(solution)/shard_map/ppermute | solution.py:17
  37.0 0.6 shard_map.111
  37.7 0.6 collective-permute-start.19
  38.2 0.1 collective-permute-done.13.refs_3_.refs_11_
  38.3 1.3 %shard_map.112 = (f32[2,4,32,256]{3,2,1,0:T(8,128)S(1)}, f32[2,4,32,256]{3,2,1,0:T(8,128)S(1)}, f32[2,4,32,256]{3,2,1,0:T(8,128)S(1)}, f32[2,4,32,256]{3,2,1,0:T(8,128)S(1)}) custom-call(s32[1,512]{1,0:T(1,128)S(1)} %copy-done.3, f32[512,128]{1,0:T(8,128)S(1)} %shard_map.107.refs_0_.refs_4_, f32[512,128]{1,0:T(8,128)S(1)} %collective-permute-done.12.refs_1_.refs_5_, ...), custom_call_target="tpu_custom_call" | custom-call | tf_op jit(solution)/shard_map/pallas_call | solution.py:57
  39.6 3.5 %collective-permute-done.20.refs_1_ = f32[128,512]{1,0:T(8,128)S(1)} collective-permute-done((f32[128,512]{1,0:T(8,128)S(1)}, f32[128,512]{1,0:T(8,128)S(1)}, u32[]{:S(2)}, u32[]{:S(2)}) %collective-permute-start.20) | collective-permute-done | bytes 262176 | tf_op jit(solution)/shard_map/ppermute | solution.py:17
  43.2 0.8 shard_map.114
  43.9 0.3 collective-permute-done.21.refs_1_
  44.2 0.8 shard_map.115.refs_0_.refs_4_.refs_12_
  45.1 1.2 %collective-permute-start.16 = (f32[2,4,32,256]{3,2,1,0:T(8,128)S(1)}, f32[2,4,32,256]{3,2,1,0:T(8,128)S(1)}, u32[]{:S(2)}, u32[]{:S(2)}) collective-permute-start(f32[2,4,32,256]{3,2,1,0:T(8,128)S(1)} %get-tuple-element.154), channel_id=1, source_target_pairs={{0,8},{2,10},{4,12},{6,14},{8,0},{10,2},{12,4},{14,6},{16,24},{18,... | collective-permute-start | bytes 786440 | tf_op jit(solution)/shard_map/ppermute | solution.py:315
  46.3 0.2 collective-permute-start.22
  46.5 3.4 %collective-permute-start.17 = (f32[2,4,32,256]{3,2,1,0:T(8,128)S(1)}, f32[2,4,32,256]{3,2,1,0:T(8,128)S(1)}, u32[]{:S(2)}, u32[]{:S(2)}) collective-permute-start(f32[2,4,32,256]{3,2,1,0:T(8,128)S(1)} %get-tuple-element.155), channel_id=1, source_target_pairs={{0,16},{2,18},{4,20},{6,22},{8,24},{10,26},{12,28},{14,30},{16,0},... | collective-permute-start | bytes 786440 | tf_op jit(solution)/shard_map/ppermute | solution.py:315
  49.9 0.6 shard_map.116
  50.6 1.5 %shard_map.117 = (f32[2,4,32,256]{3,2,1,0:T(8,128)S(1)}, f32[2,4,32,256]{3,2,1,0:T(8,128)S(1)}, f32[2,4,32,256]{3,2,1,0:T(8,128)S(1)}, f32[2,4,32,256]{3,2,1,0:T(8,128)S(1)}) custom-call(s32[1,512]{1,0:T(1,128)S(1)} %copy-done.3, f32[512,128]{1,0:T(8,128)S(1)} %get-tuple-element.158.refs_0_, f32[512,128]{1,0:T(8,128)S(1)} %collective-permute-done.19.refs_1_, ...), custom_call_target="tpu_custom_call" | custom-call | tf_op jit(solution)/shard_map/pallas_call | solution.py:57
  52.1 1.6 %collective-permute-start.24 = (f32[2,4,32,256]{3,2,1,0:T(8,128)S(1)}, f32[2,4,32,256]{3,2,1,0:T(8,128)S(1)}, u32[]{:S(2)}, u32[]{:S(2)}) collective-permute-start(f32[2,4,32,256]{3,2,1,0:T(8,128)S(1)} %get-tuple-element.173), channel_id=1, source_target_pairs={{0,2},{2,0},{4,6},{6,4},{8,10},{10,8},{12,14},{14,12},{16,18},{18,... | collective-permute-start | bytes 786440 | tf_op jit(solution)/shard_map/ppermute | solution.py:315
  53.6 1.1 collective-permute-start.25
  54.7 3.4 %collective-permute-done.16.refs_1_ = f32[2,4,32,256]{3,2,1,0:T(8,128)S(1)} collective-permute-done((f32[2,4,32,256]{3,2,1,0:T(8,128)S(1)}, f32[2,4,32,256]{3,2,1,0:T(8,128)S(1)}, u32[]{:S(2)}, u32[]{:S(2)}) %collective-permute-start.16) | collective-permute-done | bytes 262176 | tf_op jit(solution)/shard_map/ppermute | solution.py:315
  58.1 2.0 %collective-permute-start.26 = (f32[2,4,32,256]{3,2,1,0:T(8,128)S(1)}, f32[2,4,32,256]{3,2,1,0:T(8,128)S(1)}, u32[]{:S(2)}, u32[]{:S(2)}) collective-permute-start(f32[2,4,32,256]{3,2,1,0:T(8,128)S(1)} %get-tuple-element.175), channel_id=1, source_target_pairs={{0,6},{2,4},{4,2},{6,0},{8,14},{10,12},{12,10},{14,8},{16,22},{18,... | collective-permute-start | bytes 786440 | tf_op jit(solution)/shard_map/ppermute | solution.py:315
  60.1 7.7 %collective-permute-done.17.refs_2_ = f32[2,4,32,256]{3,2,1,0:T(8,128)S(1)} collective-permute-done((f32[2,4,32,256]{3,2,1,0:T(8,128)S(1)}, f32[2,4,32,256]{3,2,1,0:T(8,128)S(1)}, u32[]{:S(2)}, u32[]{:S(2)}) %collective-permute-start.17) | collective-permute-done | bytes 262176 | tf_op jit(solution)/shard_map/ppermute | solution.py:315
  67.8 1.5 %collective-permute-start.27 = (f32[128,512]{1,0:T(8,128)S(1)}, f32[128,512]{1,0:T(8,128)S(1)}, u32[]{:S(2)}, u32[]{:S(2)}) collective-permute-start(f32[128,512]{1,0:T(8,128)S(1)} %get-tuple-element.161), channel_id=1, source_target_pairs={{0,2},{2,0},{4,6},{6,4},{8,10},{10,8},{12,14},{14,12},{16,18},{18,... | collective-permute-start | bytes 786440 | tf_op jit(solution)/shard_map/ppermute | solution.py:17
  69.3 3.6 %collective-permute-done.18.refs_3_ = f32[2,4,32,256]{3,2,1,0:T(8,128)S(1)} collective-permute-done((f32[2,4,32,256]{3,2,1,0:T(8,128)S(1)}, f32[2,4,32,256]{3,2,1,0:T(8,128)S(1)}, u32[]{:S(2)}, u32[]{:S(2)}) %collective-permute-start.18) | collective-permute-done | bytes 262176 | tf_op jit(solution)/shard_map/ppermute | solution.py:315
  72.9 1.6 %collective-permute-start.29 = (f32[2,4,32,256]{3,2,1,0:T(8,128)S(1)}, f32[2,4,32,256]{3,2,1,0:T(8,128)S(1)}, u32[]{:S(2)}, u32[]{:S(2)}) collective-permute-start(f32[2,4,32,256]{3,2,1,0:T(8,128)S(1)} %get-tuple-element.184), channel_id=1, source_target_pairs={{0,2},{2,0},{4,6},{6,4},{8,10},{10,8},{12,14},{14,12},{16,18},{18,... | collective-permute-start | bytes 786440 | tf_op jit(solution)/shard_map/ppermute | solution.py:315
  74.5 1.1 collective-permute-start.30
  75.5 0.9 collective-permute-start.31
  76.6 1.1 shard_map.119
  77.7 4.5 %collective-permute-done.29.refs_1_ = f32[2,4,32,256]{3,2,1,0:T(8,128)S(1)} collective-permute-done((f32[2,4,32,256]{3,2,1,0:T(8,128)S(1)}, f32[2,4,32,256]{3,2,1,0:T(8,128)S(1)}, u32[]{:S(2)}, u32[]{:S(2)}) %collective-permute-start.29) | collective-permute-done | bytes 262176 | tf_op jit(solution)/shard_map/ppermute | solution.py:315
  82.2 5.3 %collective-permute-done.30.refs_2_ = f32[2,4,32,256]{3,2,1,0:T(8,128)S(1)} collective-permute-done((f32[2,4,32,256]{3,2,1,0:T(8,128)S(1)}, f32[2,4,32,256]{3,2,1,0:T(8,128)S(1)}, u32[]{:S(2)}, u32[]{:S(2)}) %collective-permute-start.30) | collective-permute-done | bytes 262176 | tf_op jit(solution)/shard_map/ppermute | solution.py:315
  87.6 2.5 %collective-permute-start.36 = (f32[2,4,32,256]{3,2,1,0:T(8,128)S(1)}, f32[2,4,32,256]{3,2,1,0:T(8,128)S(1)}, u32[]{:S(2)}, u32[]{:S(2)}) collective-permute-start(f32[2,4,32,256]{3,2,1,0:T(8,128)S(1)} %get-tuple-element.197), channel_id=1, source_target_pairs={{0,24},{2,26},{4,28},{6,30},{8,16},{10,18},{12,20},{14,22},{16,8},... | collective-permute-start | bytes 786440 | tf_op jit(solution)/shard_map/ppermute | solution.py:315
  90.0 1.6 %shard_map.120 = (f32[4,256,256]{2,1,0:T(8,128)}, f32[4,256,256]{2,1,0:T(8,128)}) custom-call(f32[512,128]{1,0:T(8,128)S(1)} %get-tuple-element.158.refs_0_, f32[512,128]{1,0:T(8,128)S(1)} %collective-permute-done.19.refs_1_, f32[128,256]{1,0:T(8,128)S(1)} %get-tuple-element.180.refs_2_, f32[128,256]{1,0:T(8,128)S(1)} %collective-permute-done.28.refs_3_, ...), custom_call_target="tpu_custom_call" | custom-call | tf_op jit(solution)/shard_map/pallas_call | solution.py:57
  91.7 1.2 %shard_map.121.refs_4_ = f32[4,32,4096]{2,1,0:T(8,128)} custom-call(f32[2,4,32,256]{3,2,1,0:T(8,128)S(1)} %get-tuple-element.183.refs_0_, f32[2,4,32,256]{3,2,1,0:T(8,128)S(1)} %collective-permute-done.29.refs_1_, f32[2,4,32,256]{3,2,1,0:T(8,128)S(1)} %collective-permute-done.30.refs_2_, f32[2,4,32,256]{3,2,1,0:T(8,128)S(1)} %collective-permute-done.31.refs_3_), custom_call_target="tpu_custom_call" | custom-call | tf_op jit(solution)/shard_map/pallas_call | solution.py:253
  92.9 1.2 %shard_map.122 = (f32[512,128]{1,0:T(8,128)}, f32[256,128]{1,0:T(8,128)S(1)}, f32[256,128]{1,0:T(8,128)S(1)}) custom-call(f32[512,128]{1,0:T(8,128)S(1)} %get-tuple-element.187.refs_0_, f32[512,128]{1,0:T(8,128)S(1)} %collective-permute-done.32.refs_1_, bf16[512,512]{1,0:T(8,128)(2,1)S(1)} %get-tuple-element.189.refs_2_, ...), custom_call_target="tpu_custom_call" | custom-call | tf_op jit(solution)/shard_map/pallas_call | solution.py:57
  94.1 1.3 %collective-permute-done.33.t_ref = f32[256,128]{1,0:T(8,128)S(1)} collective-permute-done((f32[256,128]{1,0:T(8,128)S(1)}, f32[256,128]{1,0:T(8,128)S(1)}, u32[]{:S(2)}, u32[]{:S(2)}) %collective-permute-start.33) | collective-permute-done | bytes 131104 | tf_op jit(solution)/shard_map/ppermute | solution.py:21
  95.5 0.7 shard_map.123
  96.2 9.3 %collective-permute-done.35.refs_2_ = f32[2,4,32,256]{3,2,1,0:T(8,128)S(1)} collective-permute-done((f32[2,4,32,256]{3,2,1,0:T(8,128)S(1)}, f32[2,4,32,256]{3,2,1,0:T(8,128)S(1)}, u32[]{:S(2)}, u32[]{:S(2)}) %collective-permute-start.35) | collective-permute-done | bytes 262176 | tf_op jit(solution)/shard_map/ppermute | solution.py:315
  105.6 6.7 %collective-permute-done.36.refs_3_ = f32[2,4,32,256]{3,2,1,0:T(8,128)S(1)} collective-permute-done((f32[2,4,32,256]{3,2,1,0:T(8,128)S(1)}, f32[2,4,32,256]{3,2,1,0:T(8,128)S(1)}, u32[]{:S(2)}, u32[]{:S(2)}) %collective-permute-start.36) | collective-permute-done | bytes 262176 | tf_op jit(solution)/shard_map/ppermute | solution.py:315
  112.3 1.2 %shard_map.124 = f32[4,32,4096]{2,1,0:T(8,128)} custom-call(f32[2,4,32,256]{3,2,1,0:T(8,128)S(1)} %get-tuple-element.194.refs_0_, f32[2,4,32,256]{3,2,1,0:T(8,128)S(1)} %collective-permute-done.34.refs_1_, f32[2,4,32,256]{3,2,1,0:T(8,128)S(1)} %collective-permute-done.35.refs_2_, ...), custom_call_target="tpu_custom_call", output_to_operand_aliasing={{}: (4, {})} | custom-call | tf_op jit(solution)/shard_map/pallas_call | solution.py:253
  (43 shorter events, 0.5 us)
Async XLA Ops:
  0.6 6.9 %copy-start.1 = (f32[4,256,256]{2,1,0:T(8,128)S(1)}, f32[4,256,256]{2,1,0:T(8,128)}, u32[]{:S(2)}) copy-start(f32[4,256,256]{2,1,0:T(8,128)} %refs_6_.1) | copy-start | bytes 3145732
  0.6 6.1 %copy-start.4 = (f32[4,256,512]{2,1,0:T(8,128)S(1)}, f32[4,256,512]{2,1,0:T(8,128)}, u32[]{:S(2)}) copy-start(f32[4,256,512]{2,1,0:T(8,128)} %refs_3_.1) | copy-start | bytes 6291460
  0.7 2.5 %copy-start.2 = (f32[256,256]{1,0:T(8,128)S(1)}, f32[256,256]{1,0:T(8,128)}, u32[]{:S(2)}) copy-start(f32[256,256]{1,0:T(8,128)} %refs_4_.2) | copy-start | bytes 786436
  0.7 6.1 %collective-permute-start.3 = (f32[4,256,256]{2,1,0:T(8,128)}, f32[4,256,256]{2,1,0:T(8,128)S(1)}, u32[]{:S(2)}, u32[]{:S(2)}) collective-permute-start(f32[4,256,256]{2,1,0:T(8,128)} %refs_6_.1), channel_id=1, source_target_pairs={{0,1},{1,0},{2,3},{3,2},{4,5},{5,4},{6,7},{7,6},{8,9},{9,8},{10,11... | collective-permute-start | bytes 3145736 | tf_op jit(solution)/shard_map/ppermute | solution.py:21
  0.7 6.0 %collective-permute-start.4 = (f32[4,256,256]{2,1,0:T(8,128)}, f32[4,256,256]{2,1,0:T(8,128)S(1)}, u32[]{:S(2)}, u32[]{:S(2)}) collective-permute-start(f32[4,256,256]{2,1,0:T(8,128)} %refs_2_.7), channel_id=1, source_target_pairs={{0,1},{1,0},{2,3},{3,2},{4,5},{5,4},{6,7},{7,6},{8,9},{9,8},{10,11... | collective-permute-start | bytes 3145736 | tf_op jit(solution)/shard_map/ppermute | solution.py:21
  2.6 4.2 %collective-permute-start = (f32[256,512]{1,0:T(8,128)S(1)}, f32[256,512]{1,0:T(8,128)S(1)}, u32[]{:S(2)}, u32[]{:S(2)}) collective-permute-start(f32[256,512]{1,0:T(8,128)S(1)} %get-tuple-element.102.refs_0_), channel_id=1, source_target_pairs={{0,1},{1,0},{2,3},{3,2},{4,5},{5,4},{6,7},{7,6},{8,9},{9,8},{10,11... | collective-permute-start | bytes 1572872 | tf_op jit(solution)/shard_map/ppermute | solution.py:21
  2.7 4.1 %collective-permute-start.1 = (f32[256,512]{1,0:T(8,128)S(1)}, f32[256,512]{1,0:T(8,128)S(1)}, u32[]{:S(2)}, u32[]{:S(2)}) collective-permute-start(f32[256,512]{1,0:T(8,128)S(1)} %get-tuple-element.103.refs_2_), channel_id=1, source_target_pairs={{0,1},{1,0},{2,3},{3,2},{4,5},{5,4},{6,7},{7,6},{8,9},{9,8},{10,11... | collective-permute-start | bytes 1572872 | tf_op jit(solution)/shard_map/ppermute | solution.py:21
  3.2 3.6 %collective-permute-start.2 = (f32[256,256]{1,0:T(8,128)S(1)}, f32[256,256]{1,0:T(8,128)S(1)}, u32[]{:S(2)}, u32[]{:S(2)}) collective-permute-start(f32[256,256]{1,0:T(8,128)S(1)} %copy-done.2), channel_id=1, source_target_pairs={{0,1},{1,0},{2,3},{3,2},{4,5},{5,4},{6,7},{7,6},{8,9},{9,8},{10,11... | collective-permute-start | bytes 786440 | tf_op jit(solution)/shard_map/ppermute | solution.py:21
  6.8 5.9 %collective-permute-start.5 = (f32[4,256,512]{2,1,0:T(8,128)S(1)}, f32[4,256,512]{2,1,0:T(8,128)S(1)}, u32[]{:S(2)}, u32[]{:S(2)}) collective-permute-start(f32[4,256,512]{2,1,0:T(8,128)S(1)} %copy-done.4), channel_id=1, source_target_pairs={{0,1},{1,0},{2,3},{3,2},{4,5},{5,4},{6,7},{7,6},{8,9},{9,8},{10,11... | collective-permute-start | bytes 6291464 | tf_op jit(solution)/shard_map/ppermute | solution.py:21
  7.0 7.2 %collective-permute-start.6 = (f32[4,256,512]{2,1,0:T(8,128)}, f32[4,256,512]{2,1,0:T(8,128)S(1)}, u32[]{:S(2)}, u32[]{:S(2)}) collective-permute-start(f32[4,256,512]{2,1,0:T(8,128)} %refs_4_.3), channel_id=1, source_target_pairs={{0,1},{1,0},{2,3},{3,2},{4,5},{5,4},{6,7},{7,6},{8,9},{9,8},{10,11... | collective-permute-start | bytes 6291464 | tf_op jit(solution)/shard_map/ppermute | solution.py:21
  7.4 9.9 %collective-permute-start.7 = (f32[4,256,512]{2,1,0:T(8,128)}, f32[4,256,512]{2,1,0:T(8,128)S(1)}, u32[]{:S(2)}, u32[]{:S(2)}) collective-permute-start(f32[4,256,512]{2,1,0:T(8,128)} %refs_5_.1), channel_id=1, source_target_pairs={{0,1},{1,0},{2,3},{3,2},{4,5},{5,4},{6,7},{7,6},{8,9},{9,8},{10,11... | collective-permute-start | bytes 6291464 | tf_op jit(solution)/shard_map/ppermute | solution.py:21
  8.5 14.3 %collective-permute-start.8 = (f32[128,512]{1,0:T(8,128)S(1)}, f32[128,512]{1,0:T(8,128)S(1)}, u32[]{:S(2)}, u32[]{:S(2)}) collective-permute-start(f32[128,512]{1,0:T(8,128)S(1)} %get-tuple-element.119), channel_id=1, source_target_pairs={{0,16},{2,18},{4,20},{6,22},{8,24},{10,26},{12,28},{14,30},{16,0},... | collective-permute-start | bytes 786440 | tf_op jit(solution)/shard_map/ppermute | solution.py:17
  11.2 9.0 %copy-start = (f32[4,256,256]{2,1,0:T(8,128)S(1)}, f32[4,256,256]{2,1,0:T(8,128)}, u32[]{:S(2)}) copy-start(f32[4,256,256]{2,1,0:T(8,128)} %refs_2_.7) | copy-start | bytes 3145732
  11.2 13.7 %collective-permute-start.9 = (f32[512,128]{1,0:T(8,128)S(1)}, f32[512,128]{1,0:T(8,128)S(1)}, u32[]{:S(2)}, u32[]{:S(2)}) collective-permute-start(f32[512,128]{1,0:T(8,128)S(1)} %get-tuple-element.158.refs_0_), channel_id=1, source_target_pairs={{0,2},{2,0},{4,6},{6,4},{8,10},{10,8},{12,14},{14,12},{16,18},{18,... | collective-permute-start | bytes 786440 | tf_op jit(solution)/shard_map/ppermute | solution.py:17
  23.6 8.3 %collective-permute-start.10 = (f32[128,512]{1,0:T(8,128)S(1)}, f32[128,512]{1,0:T(8,128)S(1)}, u32[]{:S(2)}, u32[]{:S(2)}) collective-permute-start(f32[128,512]{1,0:T(8,128)S(1)} %get-tuple-element.124), channel_id=1, source_target_pairs={{0,8},{2,10},{4,12},{6,14},{8,0},{10,2},{12,4},{14,6},{16,24},{18,... | collective-permute-start | bytes 786440 | tf_op jit(solution)/shard_map/ppermute | solution.py:17
  25.7 7.8 %collective-permute-start.11 = (f32[512,128]{1,0:T(8,128)S(1)}, f32[512,128]{1,0:T(8,128)S(1)}, u32[]{:S(2)}, u32[]{:S(2)}) collective-permute-start(f32[512,128]{1,0:T(8,128)S(1)} %shard_map.107.refs_0_.refs_4_), channel_id=1, source_target_pairs={{0,4},{2,6},{4,0},{6,2},{8,12},{10,14},{12,8},{14,10},{16,20},{18,... | collective-permute-start | bytes 786440 | tf_op jit(solution)/shard_map/ppermute | solution.py:17
  27.4 10.3 %collective-permute-start.12 = (f32[512,128]{1,0:T(8,128)S(1)}, f32[512,128]{1,0:T(8,128)S(1)}, u32[]{:S(2)}, u32[]{:S(2)}) collective-permute-start(f32[512,128]{1,0:T(8,128)S(1)} %shard_map.107.refs_0_.refs_4_), channel_id=1, source_target_pairs={{0,1},{1,0},{2,3},{3,2},{4,5},{5,4},{6,7},{7,6},{8,9},{9,8},{10,11... | collective-permute-start | bytes 786440 | tf_op jit(solution)/shard_map/ppermute | solution.py:21
  28.0 8.9 %collective-permute-start.15 = (f32[128,256]{1,0:T(8,128)S(1)}, f32[128,256]{1,0:T(8,128)S(1)}, u32[]{:S(2)}, u32[]{:S(2)}) collective-permute-start(f32[128,256]{1,0:T(8,128)S(1)} %get-tuple-element.152), channel_id=1, source_target_pairs={{0,1},{1,0},{2,3},{3,2},{4,5},{5,4},{6,7},{7,6},{8,9},{9,8},{10,11... | collective-permute-start | bytes 393224 | tf_op jit(solution)/shard_map/ppermute | solution.py:21
  34.4 4.0 %collective-permute-start.14 = (f32[512,128]{1,0:T(8,128)S(1)}, f32[512,128]{1,0:T(8,128)S(1)}, u32[]{:S(2)}, u32[]{:S(2)}) collective-permute-start(f32[512,128]{1,0:T(8,128)S(1)} %shard_map.110.refs_0_.refs_4_.refs_8_), channel_id=1, source_target_pairs={{0,1},{1,0},{2,3},{3,2},{4,5},{5,4},{6,7},{7,6},{8,9},{9,8},{10,11... | collective-permute-start | bytes 786440 | tf_op jit(solution)/shard_map/ppermute | solution.py:21
  34.4 8.7 %collective-permute-start.20 = (f32[128,512]{1,0:T(8,128)S(1)}, f32[128,512]{1,0:T(8,128)S(1)}, u32[]{:S(2)}, u32[]{:S(2)}) collective-permute-start(f32[128,512]{1,0:T(8,128)S(1)} %get-tuple-element.143), channel_id=1, source_target_pairs={{0,4},{2,6},{4,0},{6,2},{8,12},{10,14},{12,8},{14,10},{16,20},{18,... | collective-permute-start | bytes 786440 | tf_op jit(solution)/shard_map/ppermute | solution.py:17
  35.8 8.4 %collective-permute-start.21 = (f32[512,128]{1,0:T(8,128)S(1)}, f32[512,128]{1,0:T(8,128)S(1)}, u32[]{:S(2)}, u32[]{:S(2)}) collective-permute-start(f32[512,128]{1,0:T(8,128)S(1)} %shard_map.110.refs_0_.refs_4_.refs_8_), channel_id=1, source_target_pairs={{0,8},{2,10},{4,12},{6,14},{8,0},{10,2},{12,4},{14,6},{16,24},{18,... | collective-permute-start | bytes 786440 | tf_op jit(solution)/shard_map/ppermute | solution.py:17
  37.0 1.3 %collective-permute-start.13 = (f32[128,256]{1,0:T(8,128)S(1)}, f32[128,256]{1,0:T(8,128)S(1)}, u32[]{:S(2)}, u32[]{:S(2)}) collective-permute-start(f32[128,256]{1,0:T(8,128)S(1)} %get-tuple-element.150), channel_id=1, source_target_pairs={{0,1},{1,0},{2,3},{3,2},{4,5},{5,4},{6,7},{7,6},{8,9},{9,8},{10,11... | collective-permute-start | bytes 393224 | tf_op jit(solution)/shard_map/ppermute | solution.py:21
  37.0 1.4 %copy-start.3 = (s32[1,512]{1,0:T(1,128)S(1)}, s32[1,512]{1,0:T(1,128)}, u32[]{:S(2)}) copy-start(s32[1,512]{1,0:T(1,128)} %map_ref.1) | copy-start | bytes 6148
  37.7 12.8 %collective-permute-start.19 = (f32[512,128]{1,0:T(8,128)S(1)}, f32[512,128]{1,0:T(8,128)S(1)}, u32[]{:S(2)}, u32[]{:S(2)}) collective-permute-start(f32[512,128]{1,0:T(8,128)S(1)} %get-tuple-element.158.refs_0_), channel_id=1, source_target_pairs={{0,1},{1,0},{2,3},{3,2},{4,5},{5,4},{6,7},{7,6},{8,9},{9,8},{10,11... | collective-permute-start | bytes 786440 | tf_op jit(solution)/shard_map/ppermute | solution.py:21
  45.0 5.6 %collective-permute-start.23 = (f32[512,128]{1,0:T(8,128)S(1)}, f32[512,128]{1,0:T(8,128)S(1)}, u32[]{:S(2)}, u32[]{:S(2)}) collective-permute-start(f32[512,128]{1,0:T(8,128)S(1)} %shard_map.115.refs_0_.refs_4_.refs_12_), channel_id=1, source_target_pairs={{0,1},{1,0},{2,3},{3,2},{4,5},{5,4},{6,7},{7,6},{8,9},{9,8},{10,11... | collective-permute-start | bytes 786440 | tf_op jit(solution)/shard_map/ppermute | solution.py:21
  45.1 13.0 %collective-permute-start.16 = (f32[2,4,32,256]{3,2,1,0:T(8,128)S(1)}, f32[2,4,32,256]{3,2,1,0:T(8,128)S(1)}, u32[]{:S(2)}, u32[]{:S(2)}) collective-permute-start(f32[2,4,32,256]{3,2,1,0:T(8,128)S(1)} %get-tuple-element.154), channel_id=1, source_target_pairs={{0,8},{2,10},{4,12},{6,14},{8,0},{10,2},{12,4},{14,6},{16,24},{18,... | collective-permute-start | bytes 786440 | tf_op jit(solution)/shard_map/ppermute | solution.py:315
  46.3 4.3 %collective-permute-start.22 = (f32[128,256]{1,0:T(8,128)S(1)}, f32[128,256]{1,0:T(8,128)S(1)}, u32[]{:S(2)}, u32[]{:S(2)}) collective-permute-start(f32[128,256]{1,0:T(8,128)S(1)} %get-tuple-element.169), channel_id=1, source_target_pairs={{0,1},{1,0},{2,3},{3,2},{4,5},{5,4},{6,7},{7,6},{8,9},{9,8},{10,11... | collective-permute-start | bytes 393224 | tf_op jit(solution)/shard_map/ppermute | solution.py:21
  46.5 21.3 %collective-permute-start.17 = (f32[2,4,32,256]{3,2,1,0:T(8,128)S(1)}, f32[2,4,32,256]{3,2,1,0:T(8,128)S(1)}, u32[]{:S(2)}, u32[]{:S(2)}) collective-permute-start(f32[2,4,32,256]{3,2,1,0:T(8,128)S(1)} %get-tuple-element.155), channel_id=1, source_target_pairs={{0,16},{2,18},{4,20},{6,22},{8,24},{10,26},{12,28},{14,30},{16,0},... | collective-permute-start | bytes 786440 | tf_op jit(solution)/shard_map/ppermute | solution.py:315
  50.5 22.3 %collective-permute-start.18 = (f32[2,4,32,256]{3,2,1,0:T(8,128)S(1)}, f32[2,4,32,256]{3,2,1,0:T(8,128)S(1)}, u32[]{:S(2)}, u32[]{:S(2)}) collective-permute-start(f32[2,4,32,256]{3,2,1,0:T(8,128)S(1)} %get-tuple-element.156), channel_id=1, source_target_pairs={{0,24},{2,26},{4,28},{6,30},{8,16},{10,18},{12,20},{14,22},{16,8},... | collective-permute-start | bytes 786440 | tf_op jit(solution)/shard_map/ppermute | solution.py:315
  52.1 22.4 %collective-permute-start.24 = (f32[2,4,32,256]{3,2,1,0:T(8,128)S(1)}, f32[2,4,32,256]{3,2,1,0:T(8,128)S(1)}, u32[]{:S(2)}, u32[]{:S(2)}) collective-permute-start(f32[2,4,32,256]{3,2,1,0:T(8,128)S(1)} %get-tuple-element.173), channel_id=1, source_target_pairs={{0,2},{2,0},{4,6},{6,4},{8,10},{10,8},{12,14},{14,12},{16,18},{18,... | collective-permute-start | bytes 786440 | tf_op jit(solution)/shard_map/ppermute | solution.py:315
  53.6 21.9 %collective-permute-start.25 = (f32[2,4,32,256]{3,2,1,0:T(8,128)S(1)}, f32[2,4,32,256]{3,2,1,0:T(8,128)S(1)}, u32[]{:S(2)}, u32[]{:S(2)}) collective-permute-start(f32[2,4,32,256]{3,2,1,0:T(8,128)S(1)} %get-tuple-element.174), channel_id=1, source_target_pairs={{0,4},{2,6},{4,0},{6,2},{8,12},{10,14},{12,8},{14,10},{16,20},{18,... | collective-permute-start | bytes 786440 | tf_op jit(solution)/shard_map/ppermute | solution.py:315
  58.1 18.4 %collective-permute-start.26 = (f32[2,4,32,256]{3,2,1,0:T(8,128)S(1)}, f32[2,4,32,256]{3,2,1,0:T(8,128)S(1)}, u32[]{:S(2)}, u32[]{:S(2)}) collective-permute-start(f32[2,4,32,256]{3,2,1,0:T(8,128)S(1)} %get-tuple-element.175), channel_id=1, source_target_pairs={{0,6},{2,4},{4,2},{6,0},{8,14},{10,12},{12,10},{14,8},{16,22},{18,... | collective-permute-start | bytes 786440 | tf_op jit(solution)/shard_map/ppermute | solution.py:315
  67.8 8.8 %collective-permute-start.27 = (f32[128,512]{1,0:T(8,128)S(1)}, f32[128,512]{1,0:T(8,128)S(1)}, u32[]{:S(2)}, u32[]{:S(2)}) collective-permute-start(f32[128,512]{1,0:T(8,128)S(1)} %get-tuple-element.161), channel_id=1, source_target_pairs={{0,2},{2,0},{4,6},{6,4},{8,10},{10,8},{12,14},{14,12},{16,18},{18,... | collective-permute-start | bytes 786440 | tf_op jit(solution)/shard_map/ppermute | solution.py:17
  72.9 9.3 %collective-permute-start.29 = (f32[2,4,32,256]{3,2,1,0:T(8,128)S(1)}, f32[2,4,32,256]{3,2,1,0:T(8,128)S(1)}, u32[]{:S(2)}, u32[]{:S(2)}) collective-permute-start(f32[2,4,32,256]{3,2,1,0:T(8,128)S(1)} %get-tuple-element.184), channel_id=1, source_target_pairs={{0,2},{2,0},{4,6},{6,4},{8,10},{10,8},{12,14},{14,12},{16,18},{18,... | collective-permute-start | bytes 786440 | tf_op jit(solution)/shard_map/ppermute | solution.py:315
  74.5 13.1 %collective-permute-start.30 = (f32[2,4,32,256]{3,2,1,0:T(8,128)S(1)}, f32[2,4,32,256]{3,2,1,0:T(8,128)S(1)}, u32[]{:S(2)}, u32[]{:S(2)}) collective-permute-start(f32[2,4,32,256]{3,2,1,0:T(8,128)S(1)} %get-tuple-element.185), channel_id=1, source_target_pairs={{0,4},{2,6},{4,0},{6,2},{8,12},{10,14},{12,8},{14,10},{16,20},{18,... | collective-permute-start | bytes 786440 | tf_op jit(solution)/shard_map/ppermute | solution.py:315
  75.5 16.2 %collective-permute-start.31 = (f32[2,4,32,256]{3,2,1,0:T(8,128)S(1)}, f32[2,4,32,256]{3,2,1,0:T(8,128)S(1)}, u32[]{:S(2)}, u32[]{:S(2)}) collective-permute-start(f32[2,4,32,256]{3,2,1,0:T(8,128)S(1)} %get-tuple-element.186), channel_id=1, source_target_pairs={{0,6},{2,4},{4,2},{6,0},{8,14},{10,12},{12,10},{14,8},{16,22},{18,... | collective-permute-start | bytes 786440 | tf_op jit(solution)/shard_map/ppermute | solution.py:315
  76.5 16.5 %collective-permute-start.32 = (f32[512,128]{1,0:T(8,128)S(1)}, f32[512,128]{1,0:T(8,128)S(1)}, u32[]{:S(2)}, u32[]{:S(2)}) collective-permute-start(f32[512,128]{1,0:T(8,128)S(1)} %shard_map.115.refs_0_.refs_4_.refs_12_), channel_id=1, source_target_pairs={{0,16},{2,18},{4,20},{6,22},{8,24},{10,26},{12,28},{14,30},{16,0},... | collective-permute-start | bytes 786440 | tf_op jit(solution)/shard_map/ppermute | solution.py:17
  77.7 9.9 %collective-permute-start.28 = (f32[128,256]{1,0:T(8,128)S(1)}, f32[128,256]{1,0:T(8,128)S(1)}, u32[]{:S(2)}, u32[]{:S(2)}) collective-permute-start(f32[128,256]{1,0:T(8,128)S(1)} %get-tuple-element.181), channel_id=1, source_target_pairs={{0,1},{1,0},{2,3},{3,2},{4,5},{5,4},{6,7},{7,6},{8,9},{9,8},{10,11... | collective-permute-start | bytes 393224 | tf_op jit(solution)/shard_map/ppermute | solution.py:21
  82.2 14.0 %collective-permute-start.34 = (f32[2,4,32,256]{3,2,1,0:T(8,128)S(1)}, f32[2,4,32,256]{3,2,1,0:T(8,128)S(1)}, u32[]{:S(2)}, u32[]{:S(2)}) collective-permute-start(f32[2,4,32,256]{3,2,1,0:T(8,128)S(1)} %get-tuple-element.195), channel_id=1, source_target_pairs={{0,8},{2,10},{4,12},{6,14},{8,0},{10,2},{12,4},{14,6},{16,24},{18,... | collective-permute-start | bytes 786440 | tf_op jit(solution)/shard_map/ppermute | solution.py:315
  87.6 18.0 %collective-permute-start.35 = (f32[2,4,32,256]{3,2,1,0:T(8,128)S(1)}, f32[2,4,32,256]{3,2,1,0:T(8,128)S(1)}, u32[]{:S(2)}, u32[]{:S(2)}) collective-permute-start(f32[2,4,32,256]{3,2,1,0:T(8,128)S(1)} %get-tuple-element.196), channel_id=1, source_target_pairs={{0,16},{2,18},{4,20},{6,22},{8,24},{10,26},{12,28},{14,30},{16,0},... | collective-permute-start | bytes 786440 | tf_op jit(solution)/shard_map/ppermute | solution.py:315
  87.6 24.7 %collective-permute-start.36 = (f32[2,4,32,256]{3,2,1,0:T(8,128)S(1)}, f32[2,4,32,256]{3,2,1,0:T(8,128)S(1)}, u32[]{:S(2)}, u32[]{:S(2)}) collective-permute-start(f32[2,4,32,256]{3,2,1,0:T(8,128)S(1)} %get-tuple-element.197), channel_id=1, source_target_pairs={{0,24},{2,26},{4,28},{6,30},{8,16},{10,18},{12,20},{14,22},{16,8},... | collective-permute-start | bytes 786440 | tf_op jit(solution)/shard_map/ppermute | solution.py:315
  94.1 1.3 %collective-permute-start.33 = (f32[256,128]{1,0:T(8,128)S(1)}, f32[256,128]{1,0:T(8,128)S(1)}, u32[]{:S(2)}, u32[]{:S(2)}) collective-permute-start(f32[256,128]{1,0:T(8,128)S(1)} %get-tuple-element.192), channel_id=1, source_target_pairs={{0,1},{1,0},{2,3},{3,2},{4,5},{5,4},{6,7},{7,6},{8,9},{9,8},{10,11... | collective-permute-start | bytes 393224 | tf_op jit(solution)/shard_map/ppermute | solution.py:21
where the time goes:
time: 114 us
  waiting for transfers between devices  60.1 us (53%)
  starting transfers between devices  29.9 us (26%)
  Pallas kernels  22.6 us (20%)
    ppermute x12, waiting for transfers between devices, exchange(): lax.ppermute(v, 'cube', [(i, i ^ j * step) for i in range(n)])  40.6 us
    pallas_call x21, Pallas kernels, __call__(): pl.pallas_call(kernel, out_shape=tuple(outs), in_specs=[pl.BlockSpec(memo...  20.1 us
    ppermute x12, starting transfers between devices, exchange(): lax.ppermute(v, 'cube', [(i, i ^ j * step) for i in range(n)])  15.3 us
    ppermute x8, starting transfers between devices, partner(): lax.ppermute(x, 'cube', [(i, i ^ 1 << distance) for i in range(lax.axis_s...  11.2 us
    ppermute x8, waiting for transfers between devices, partner(): lax.ppermute(x, 'cube', [(i, i ^ 1 << distance) for i in range(lax.axis_s...  9.92 us
    ppermute x17, waiting for transfers between devices, swap(): return lax.ppermute(x, 'cores', [(0, 1), (1, 0)])  9.52 us
    ppermute x17, starting transfers between devices, swap(): return lax.ppermute(x, 'cores', [(0, 1), (1, 0)])  3.4 us
    pallas_call x2, Pallas kernels, place(): pl.pallas_call(functools.partial(place_kernel, plan), out_shape=out, in_s...  2.45 us
  transfers between devices with their start and end apart: 37, of which 17 were waited for; matrix products, arithmetic and copies ran while one was open for 0% of the time, Pallas kernels for 19%

commit v1 on v0

--- a/solution.py
+++ b/solution.py
@@ -19,6 +19,14 @@
 
 def swap(x):
     return lax.ppermute(x, "cores", [(0, 1), (1, 0)])
+
+
+def both(x):
+    return lax.all_gather(x, "cores")
+
+
+def other(ref):
+    return ref[1 - lax.axis_index("cores")] if len(ref.shape) == 3 else ref[...]
 
 
 def split(x):
@@ -62,7 +70,7 @@
             scratch_shapes=list(scratch),
             compiler_params=pltpu.CompilerParams(vmem_limit_bytes=limit << 20),
         )(*args)
-        self.last = res[0]
+        self.last = res[-1]
         return res
 
     def named(self, kernel, args, outs, **more):
@@ -192,10 +200,10 @@
     pick = jnp.where(lax.broadcasted_iota(jnp.int32, (r, r), 0) == target, 1.0, 0.0).astype(BF16)
     for i in range(batch):
         s_ref, st_ref, wm_ref, wt_ref = ins[4 * i : 4 * i + 4]
-        sh, sl = split(jnp.concatenate([s_ref[...], st_ref[...]], axis=1))
+        sh, sl = split(jnp.concatenate([s_ref[...], other(st_ref)], axis=1))
         ph = dot(pick, sh).astype(BF16)
         plo = dot(pick, sl).astype(BF16)
-        wh, wl = split(jnp.concatenate([wm_ref[...], wt_ref[...]], axis=0))
+        wh, wl = split(jnp.concatenate([wm_ref[...], other(wt_ref)], axis=0))
         o = dot(ph, wh) + dot(ph, wl) + dot(plo, wh)
         for j, out in enumerate(outs):
             for q in range(out.shape[1]):
@@ -216,20 +224,21 @@
     levels, h, k = solved_ref.shape
     k //= 2
     mine, _ = halves(h)
-    own, other = (pl.ds(x, k) for x in halves(k))
+    own, theirs = (pl.ds(x, k) for x in halves(k))
     for level in range(levels):
         s_ref, st_ref, gm_ref, gt_ref = refs[4 * level : 4 * level + 4]
         solved_ref[level, :, own] = s_ref[pl.ds(mine, h), :]
-        solved_ref[level, :, other] = st_ref[pl.ds(mine, h), :]
+        st = st_ref if len(st_ref.shape) == 2 else st_ref.at[1 - lax.axis_index("cores")]
+        solved_ref[level, :, theirs] = st[pl.ds(mine, h), :]
         grad_ref[level, :, own] = -gm_ref[...].T
-        grad_ref[level, :, other] = -gt_ref[...].T
+        grad_ref[level, :, theirs] = -other(gt_ref).T
 
 
 def join_kernel(m_ref, t_ref, o_ref):
     k = m_ref.shape[1]
-    own, other = (pl.ds(x, k) for x in halves(k))
+    own, theirs = (pl.ds(x, k) for x in halves(k))
     o_ref[:, own] = m_ref[...]
-    o_ref[:, other] = t_ref[...]
+    o_ref[:, theirs] = other(t_ref)
 
 
 def place_kernel(plan, *refs):
@@ -361,7 +370,7 @@
                 },
                 {"y": vec_t, "w": vec_t, "wm": half_t, "ws": half_t},
             )
-            w, y, wm[lb - 1], wt[lb - 1] = x["w"], x["y"], x["wm"], swap(x["ws"])
+            w, y, wm[lb - 1], wt[lb - 1] = x["w"], x["y"], x["wm"], (both if t == levels - 2 else swap)(x["ws"])
             x = run.named(
                 functools.partial(fwd_next, t + 1),
                 {
@@ -371,31 +380,31 @@
                 {"s": vec},
             )
             s[t + 1] = x["s"]
-            st[t + 1] = swap(s[t + 1])
-    late_in = turn(exchange(outer(late, True), 1))
-    late_in = exchange(late_in, NEAR)
+            st[t + 1] = (swap if t == 0 else both)(s[t + 1])
+    late_out = exchange(outer(late, True), 1)
+    early_in = exchange(turn(crossed), 1)
+    late_in = exchange(turn(late_out), NEAR)
+    sp = partner(after(s[last], *crossed), base + last)
+    out = shape(levels, r // n, n * h)
+    plan = [(m, (i, f), lv, m + NEAR * f) for m in nears for f in fars for i, lv in enumerate(early)]
+    element_grad = place(run, early_in, plan, out)
     g = run.named(
         bwd_last,
         {"b": b, "yp": yp, "dh": parts["dinv0h"], "dl": parts["dinv0l"]},
         {"g": vec_t, "gm": half_t, "gs": half_t},
     )
-    gms, gts = [g["gm"], *wm[:last]], [swap(g["gs"]), *wt[:last]]
-    early_in = exchange(turn(crossed), 1)
-    sp = partner(after(s[last], *crossed), base + last)
+    gms, gts = [g["gm"], *wm[:last]], [both(g["gs"]), *wt[:last]]
     solved, grads = run(
         results_kernel,
         [v for q in range(levels) for v in (s[q], st[q], gms[q], gts[q])],
         [shape(levels, h, k), shape(levels, h, k)],
     )
-    out = shape(levels, r // n, n * h)
-    plan = [(m, (i, f), lv, m + NEAR * f) for m in nears for f in fars for i, lv in enumerate(early)]
-    element_grad = place(run, early_in, plan, out)
     u = run.named(
         fwd_last,
         {"a": a, "sp": sp, "ph": parts[f"far{last}h"], "pl": parts[f"far{last}l"]},
         {"u": vec, "um": shape(h, kh), "us": shape(h, kh)},
     )
-    top_update, = run(join_kernel, [u["um"], swap(u["us"])], [shape(h, k)])
+    top_update, = run(join_kernel, [u["um"], both(u["us"])], [shape(h, k)])
     plan = [(f, (i, m), lv, m + NEAR * f) for m in nears for f in fars for i, lv in enumerate(late)]
     element_grad = place(run, late_in, plan, out, element_grad)
     return solved, top_update, grads, element_grad

time: 114 us -> 110 us (0.965)
  waiting for transfers between devices: 60.1 us -> 37.8 us
  blocking collectives: 0 us -> 10.5 us
  starting transfers between devices: 29.9 us -> 37.5 us
    ppermute x12, waiting for transfers between devices: 40.6 us -> 24.4 us  [exchange(): lax.ppermute(v, 'cube', [(i, i ^ j * step) for i in range(n)])]
    all_gather x0 -> x5, blocking collectives: none -> 10.5 us  [both(): return lax.all_gather(x, 'cores')]
    ppermute x12, starting transfers between devices: 15.3 us -> 20 us  [exchange(): lax.ppermute(v, 'cube', [(i, i ^ j * step) for i in range(n)])]
    ppermute x8, waiting for transfers between devices: 9.92 us -> 5.31 us  [partner(): lax.ppermute(x, 'cube', [(i, i ^ 1 << distance) for i in range(lax.axis_s...]
    ppermute x8, starting transfers between devices: 11.2 us -> 14.5 us  [partner(): lax.ppermute(x, 'cube', [(i, i ^ 1 << distance) for i in range(lax.axis_s...]
    ppermute x17 -> x12, waiting for transfers between devices: 9.52 us -> 8.07 us  [swap(): return lax.ppermute(x, 'cores', [(0, 1), (1, 0)])]
    ppermute x17 -> x12, starting transfers between devices: 3.4 us -> 2.95 us  [swap(): return lax.ppermute(x, 'cores', [(0, 1), (1, 0)])]
  transfers between devices with their start and end apart: 37 -> 32, of which waited for: 17 -> 11; matrix products, arithmetic and copies ran while one was open for 0% -> 0% of each run, Pallas kernels for 19% -> 19%
where the time goes in v1:
time: 110 us; the launch traced here: 109 us
  waiting for transfers between devices  37.8 us (34%)
  starting transfers between devices  37.5 us (34%)
  Pallas kernels  22.4 us (20%)
  blocking collectives  10.5 us (10%)
    ppermute x12, waiting for transfers between devices, exchange(): lax.ppermute(v, 'cube', [(i, i ^ j * step) for i in range(n)])  24.4 us
    ppermute x12, starting transfers between devices, exchange(): lax.ppermute(v, 'cube', [(i, i ^ j * step) for i in range(n)])  20 us
    pallas_call x21, Pallas kernels, __call__(): pl.pallas_call(kernel, out_shape=tuple(outs), in_specs=[pl.BlockSpec(memo...  19.9 us
    ppermute x8, starting transfers between devices, partner(): lax.ppermute(x, 'cube', [(i, i ^ 1 << distance) for i in range(lax.axis_s...  14.5 us
    all_gather x5, blocking collectives, both(): return lax.all_gather(x, 'cores')  10.5 us
    ppermute x12, waiting for transfers between devices, swap(): return lax.ppermute(x, 'cores', [(0, 1), (1, 0)])  8.07 us
    ppermute x8, waiting for transfers between devices, partner(): lax.ppermute(x, 'cube', [(i, i ^ 1 << distance) for i in range(lax.axis_s...  5.31 us
    ppermute x12, starting transfers between devices, swap(): return lax.ppermute(x, 'cores', [(0, 1), (1, 0)])  2.95 us
  transfers between devices with their start and end apart: 32, of which 11 were waited for; matrix products, arithmetic and copies ran while one was open for 0% of the time, Pallas kernels for 19%

profile of v1, /device:TPU:8, one launch (start us, length us, event | category | flops | bytes accessed | tf_op | source)
XLA Modules:
  0.0 109.3 jit_solution(11009644418967346849)
XLA Ops:
  0.7 0.5 collective-permute-start.4
  1.2 1.3 %shard_map.102 = (f32[256,512]{1,0:T(8,128)S(1)}, f32[256,512]{1,0:T(8,128)S(1)}) custom-call(f32[4,256,512]{2,1,0:T(8,128)} %refs_3_.1, f32[4,256,512]{2,1,0:T(8,128)} %refs_5_.1), custom_call_target="tpu_custom_call" | custom-call | tf_op jit(solution)/shard_map/pallas_call | solution.py:65
  2.7 0.5 collective-permute-start.1
  3.2 3.5 %collective-permute-done.2.refs_5_ = f32[256,256]{1,0:T(8,128)S(1)} collective-permute-done((f32[256,256]{1,0:T(8,128)S(1)}, f32[256,256]{1,0:T(8,128)S(1)}, u32[]{:S(2)}, u32[]{:S(2)}) %collective-permute-start.2) | collective-permute-done | bytes 262176 | tf_op jit(solution)/shard_map/ppermute | solution.py:21
  6.8 0.2 collective-permute-start.5
  7.0 0.4 collective-permute-start.6
  7.4 0.1 collective-permute-start.7
  7.5 1.0 shard_map.103
  8.5 2.7 %collective-permute-start.8 = (f32[128,512]{1,0:T(8,128)S(1)}, f32[128,512]{1,0:T(8,128)S(1)}, u32[]{:S(2)}, u32[]{:S(2)}) collective-permute-start(f32[128,512]{1,0:T(8,128)S(1)} %get-tuple-element.119), channel_id=1, source_target_pairs={{0,16},{2,18},{4,20},{6,22},{8,24},{10,26},{12,28},{14,30},{16,0},... | collective-permute-start | bytes 786440 | tf_op jit(solution)/shard_map/ppermute | solution.py:17
  11.2 1.5 %collective-permute-start.9 = (f32[512,128]{1,0:T(8,128)S(1)}, f32[512,128]{1,0:T(8,128)S(1)}, u32[]{:S(2)}, u32[]{:S(2)}) collective-permute-start(f32[512,128]{1,0:T(8,128)S(1)} %get-tuple-element.183.refs_0_), channel_id=1, source_target_pairs={{0,2},{2,0},{4,6},{6,4},{8,10},{10,8},{12,14},{14,12},{16,18},{18,... | collective-permute-start | bytes 786440 | tf_op jit(solution)/shard_map/ppermute | solution.py:17
  12.7 1.5 %collective-permute-done.6.refs_1_ = f32[4,256,512]{2,1,0:T(8,128)S(1)} collective-permute-done((f32[4,256,512]{2,1,0:T(8,128)}, f32[4,256,512]{2,1,0:T(8,128)S(1)}, u32[]{:S(2)}, u32[]{:S(2)}) %collective-permute-start.6) | collective-permute-done | bytes 2097184 | tf_op jit(solution)/shard_map/ppermute | solution.py:21
  14.2 3.0 %collective-permute-done.7.refs_2_ = f32[4,256,512]{2,1,0:T(8,128)S(1)} collective-permute-done((f32[4,256,512]{2,1,0:T(8,128)}, f32[4,256,512]{2,1,0:T(8,128)S(1)}, u32[]{:S(2)}, u32[]{:S(2)}) %collective-permute-start.7) | collective-permute-done | bytes 2097184 | tf_op jit(solution)/shard_map/ppermute | solution.py:21
  17.2 3.0 %shard_map.104 = (bf16[512,512]{1,0:T(8,128)(2,1)S(1)}, bf16[512,512]{1,0:T(8,128)(2,1)S(1)}, bf16[512,512]{1,0:T(8,128)(2,1)S(1)}, bf16[512,512]{1,0:T(8,128)(2...) custom-call(f32[4,256,512]{2,1,0:T(8,128)S(1)} %collective-permute-d, ...), custom_call_target="tpu_custom_call" | custom-call | tf_op jit(solution)/shard_map/pallas_call | solution.py:65
  20.2 0.6 shard_map.105
  20.9 1.9 %collective-permute-done.8.refs_1_ = f32[128,512]{1,0:T(8,128)S(1)} collective-permute-done((f32[128,512]{1,0:T(8,128)S(1)}, f32[128,512]{1,0:T(8,128)S(1)}, u32[]{:S(2)}, u32[]{:S(2)}) %collective-permute-start.8) | collective-permute-done | bytes 262176 | tf_op jit(solution)/shard_map/ppermute | solution.py:17
  22.8 0.8 shard_map.106
  23.6 1.3 %collective-permute-start.10 = (f32[128,512]{1,0:T(8,128)S(1)}, f32[128,512]{1,0:T(8,128)S(1)}, u32[]{:S(2)}, u32[]{:S(2)}) collective-permute-start(f32[128,512]{1,0:T(8,128)S(1)} %get-tuple-element.138), channel_id=1, source_target_pairs={{0,8},{2,10},{4,12},{6,14},{8,0},{10,2},{12,4},{14,6},{16,24},{18,... | collective-permute-start | bytes 786440 | tf_op jit(solution)/shard_map/ppermute | solution.py:17
  24.9 0.8 shard_map.107.refs_0_.refs_4_
  25.7 1.6 %collective-permute-start.11 = (f32[512,128]{1,0:T(8,128)S(1)}, f32[512,128]{1,0:T(8,128)S(1)}, u32[]{:S(2)}, u32[]{:S(2)}) collective-permute-start(f32[512,128]{1,0:T(8,128)S(1)} %shard_map.107.refs_0_.refs_4_), channel_id=1, source_target_pairs={{0,4},{2,6},{4,0},{6,2},{8,12},{10,14},{12,8},{14,10},{16,20},{18,... | collective-permute-start | bytes 786440 | tf_op jit(solution)/shard_map/ppermute | solution.py:17
  27.4 0.5 collective-permute-start.12
  27.9 0.6 shard_map.108
  28.5 3.4 %collective-permute-done.10.refs_1_ = f32[128,512]{1,0:T(8,128)S(1)} collective-permute-done((f32[128,512]{1,0:T(8,128)S(1)}, f32[128,512]{1,0:T(8,128)S(1)}, u32[]{:S(2)}, u32[]{:S(2)}) %collective-permute-start.10) | collective-permute-done | bytes 262176 | tf_op jit(solution)/shard_map/ppermute | solution.py:17
  31.9 0.7 shard_map.109
  32.7 1.6 %collective-permute-start.15 = (f32[128,512]{1,0:T(8,128)S(1)}, f32[128,512]{1,0:T(8,128)S(1)}, u32[]{:S(2)}, u32[]{:S(2)}) collective-permute-start(f32[128,512]{1,0:T(8,128)S(1)} %get-tuple-element.154), channel_id=1, source_target_pairs={{0,4},{2,6},{4,0},{6,2},{8,12},{10,14},{12,8},{14,10},{16,20},{18,... | collective-permute-start | bytes 786440 | tf_op jit(solution)/shard_map/ppermute | solution.py:17
  34.3 0.8 shard_map.110.refs_0_.refs_4_.refs_8_
  35.1 0.9 collective-permute-start.16
  36.0 0.5 collective-permute-start.13
  36.5 2.2 %all-gather = f32[1024,128]{1,0:T(8,128)S(1)} all-gather(f32[512,128]{1,0:T(8,128)S(1)} %shard_map.110.refs_0_.refs_4_.refs_8_), channel_id=2, replica_groups=mesh['cube'=16,'cores'=2] {'cores'}, dimensions={0}, use_global_device_ids=true | all-gather | bytes 786432 | tf_op jit(solution)/shard_map/all_gather | solution.py:25
  38.7 0.6 shard_map.111
  39.4 1.3 %shard_map.112 = (f32[2,4,32,256]{3,2,1,0:T(8,128)S(1)}, f32[2,4,32,256]{3,2,1,0:T(8,128)S(1)}, f32[2,4,32,256]{3,2,1,0:T(8,128)S(1)}, f32[2,4,32,256]{3,2,1,0:T(8,128)S(1)}) custom-call(s32[1,512]{1,0:T(1,128)S(1)} %copy-done.3, f32[512,128]{1,0:T(8,128)S(1)} %shard_map.107.refs_0_.refs_4_, f32[512,128]{1,0:T(8,128)S(1)} %collective-permute-done.12.refs_1_.refs_5_, ...), custom_call_target="tpu_custom_call" | custom-call | tf_op jit(solution)/shard_map/pallas_call | solution.py:65
  40.6 3.2 %collective-permute-start.20 = (f32[2,4,32,256]{3,2,1,0:T(8,128)S(1)}, f32[2,4,32,256]{3,2,1,0:T(8,128)S(1)}, u32[]{:S(2)}, u32[]{:S(2)}) collective-permute-start(f32[2,4,32,256]{3,2,1,0:T(8,128)S(1)} %get-tuple-element.152), channel_id=1, source_target_pairs={{0,24},{2,26},{4,28},{6,30},{8,16},{10,18},{12,20},{14,22},{16,8},... | collective-permute-start | bytes 786440 | tf_op jit(solution)/shard_map/ppermute | solution.py:324
  43.8 1.2 %collective-permute-start.18 = (f32[2,4,32,256]{3,2,1,0:T(8,128)S(1)}, f32[2,4,32,256]{3,2,1,0:T(8,128)S(1)}, u32[]{:S(2)}, u32[]{:S(2)}) collective-permute-start(f32[2,4,32,256]{3,2,1,0:T(8,128)S(1)} %get-tuple-element.167), channel_id=1, source_target_pairs={{0,8},{2,10},{4,12},{6,14},{8,0},{10,2},{12,4},{14,6},{16,24},{18,... | collective-permute-start | bytes 786440 | tf_op jit(solution)/shard_map/ppermute | solution.py:324
  45.0 0.4 collective-permute-start.19
  45.3 0.7 shard_map.113
  46.1 0.8 shard_map.114.refs_0_.refs_4_.refs_12_
  46.9 2.2 %all-gather.2 = f32[1024,128]{1,0:T(8,128)S(1)} all-gather(f32[512,128]{1,0:T(8,128)S(1)} %shard_map.114.refs_0_.refs_4_.refs_12_), channel_id=4, replica_groups=mesh['cube'=16,'cores'=2] {'cores'}, dimensions={0}, use_global_device_ids=true | all-gather | bytes 786432 | tf_op jit(solution)/shard_map/all_gather | solution.py:25
  49.1 0.6 shard_map.115
  49.7 2.2 %all-gather.1 = f32[256,256]{1,0:T(8,128)S(1)} all-gather(f32[128,256]{1,0:T(8,128)S(1)} %get-tuple-element.155), channel_id=3, replica_groups=mesh['cube'=16,'cores'=2] {'cores'}, dimensions={0}, use_global_device_ids=true | all-gather | bytes 393216 | tf_op jit(solution)/shard_map/all_gather | solution.py:25
  51.9 1.3 %shard_map.116 = (f32[2,4,32,256]{3,2,1,0:T(8,128)S(1)}, f32[2,4,32,256]{3,2,1,0:T(8,128)S(1)}, f32[2,4,32,256]{3,2,1,0:T(8,128)S(1)}, f32[2,4,32,256]{3,2,1,0:T(8,128)S(1)}) custom-call(s32[1,512]{1,0:T(1,128)S(1)} %copy-done.3, f32[512,128]{1,0:T(8,128)S(1)} %get-tuple-element.183.refs_0_, f32[512,128]{1,0:T(8,128)S(1)} %collective-permute-done.17.refs_1_, ...), custom_call_target="tpu_custom_call" | custom-call | tf_op jit(solution)/shard_map/pallas_call | solution.py:65
  53.2 1.6 %collective-permute-start.21 = (f32[2,4,32,256]{3,2,1,0:T(8,128)S(1)}, f32[2,4,32,256]{3,2,1,0:T(8,128)S(1)}, u32[]{:S(2)}, u32[]{:S(2)}) collective-permute-start(f32[2,4,32,256]{3,2,1,0:T(8,128)S(1)} %get-tuple-element.173), channel_id=1, source_target_pairs={{0,2},{2,0},{4,6},{6,4},{8,10},{10,8},{12,14},{14,12},{16,18},{18,... | collective-permute-start | bytes 786440 | tf_op jit(solution)/shard_map/ppermute | solution.py:324
  54.7 1.2 %collective-permute-start.22 = (f32[2,4,32,256]{3,2,1,0:T(8,128)S(1)}, f32[2,4,32,256]{3,2,1,0:T(8,128)S(1)}, u32[]{:S(2)}, u32[]{:S(2)}) collective-permute-start(f32[2,4,32,256]{3,2,1,0:T(8,128)S(1)} %get-tuple-element.174), channel_id=1, source_target_pairs={{0,4},{2,6},{4,0},{6,2},{8,12},{10,14},{12,8},{14,10},{16,20},{18,... | collective-permute-start | bytes 786440 | tf_op jit(solution)/shard_map/ppermute | solution.py:324
  55.9 1.9 %collective-permute-done.18.refs_1_ = f32[2,4,32,256]{3,2,1,0:T(8,128)S(1)} collective-permute-done((f32[2,4,32,256]{3,2,1,0:T(8,128)S(1)}, f32[2,4,32,256]{3,2,1,0:T(8,128)S(1)}, u32[]{:S(2)}, u32[]{:S(2)}) %collective-permute-start.18) | collective-permute-done | bytes 262176 | tf_op jit(solution)/shard_map/ppermute | solution.py:324
  57.8 2.4 %collective-permute-start.23 = (f32[2,4,32,256]{3,2,1,0:T(8,128)S(1)}, f32[2,4,32,256]{3,2,1,0:T(8,128)S(1)}, u32[]{:S(2)}, u32[]{:S(2)}) collective-permute-start(f32[2,4,32,256]{3,2,1,0:T(8,128)S(1)} %get-tuple-element.165), channel_id=1, source_target_pairs={{0,6},{2,4},{4,2},{6,0},{8,14},{10,12},{12,10},{14,8},{16,22},{18,... | collective-permute-start | bytes 786440 | tf_op jit(solution)/shard_map/ppermute | solution.py:324
  60.2 6.3 %collective-permute-done.19.refs_2_ = f32[2,4,32,256]{3,2,1,0:T(8,128)S(1)} collective-permute-done((f32[2,4,32,256]{3,2,1,0:T(8,128)S(1)}, f32[2,4,32,256]{3,2,1,0:T(8,128)S(1)}, u32[]{:S(2)}, u32[]{:S(2)}) %collective-permute-start.19) | collective-permute-done | bytes 262176 | tf_op jit(solution)/shard_map/ppermute | solution.py:324
  66.6 1.6 %collective-permute-start.24 = (f32[2,4,32,256]{3,2,1,0:T(8,128)S(1)}, f32[2,4,32,256]{3,2,1,0:T(8,128)S(1)}, u32[]{:S(2)}, u32[]{:S(2)}) collective-permute-start(f32[2,4,32,256]{3,2,1,0:T(8,128)S(1)} %get-tuple-element.177), channel_id=1, source_target_pairs={{0,2},{2,0},{4,6},{6,4},{8,10},{10,8},{12,14},{14,12},{16,18},{18,... | collective-permute-start | bytes 786440 | tf_op jit(solution)/shard_map/ppermute | solution.py:324
  68.1 0.5 collective-permute-start.25
  68.6 1.5 %collective-permute-start.26 = (f32[2,4,32,256]{3,2,1,0:T(8,128)S(1)}, f32[2,4,32,256]{3,2,1,0:T(8,128)S(1)}, u32[]{:S(2)}, u32[]{:S(2)}) collective-permute-start(f32[2,4,32,256]{3,2,1,0:T(8,128)S(1)} %get-tuple-element.171), channel_id=1, source_target_pairs={{0,6},{2,4},{4,2},{6,0},{8,14},{10,12},{12,10},{14,8},{16,22},{18,... | collective-permute-start | bytes 786440 | tf_op jit(solution)/shard_map/ppermute | solution.py:324
  70.1 1.5 %collective-permute-start.27 = (f32[128,512]{1,0:T(8,128)S(1)}, f32[128,512]{1,0:T(8,128)S(1)}, u32[]{:S(2)}, u32[]{:S(2)}) collective-permute-start(f32[128,512]{1,0:T(8,128)S(1)} %get-tuple-element.180), channel_id=1, source_target_pairs={{0,2},{2,0},{4,6},{6,4},{8,10},{10,8},{12,14},{14,12},{16,18},{18,... | collective-permute-start | bytes 786440 | tf_op jit(solution)/shard_map/ppermute | solution.py:17
  71.6 3.4 %collective-permute-start.28 = (f32[512,128]{1,0:T(8,128)S(1)}, f32[512,128]{1,0:T(8,128)S(1)}, u32[]{:S(2)}, u32[]{:S(2)}) collective-permute-start(f32[512,128]{1,0:T(8,128)S(1)} %shard_map.114.refs_0_.refs_4_.refs_12_), channel_id=1, source_target_pairs={{0,16},{2,18},{4,20},{6,22},{8,24},{10,26},{12,28},{14,30},{16,0},... | collective-permute-start | bytes 786440 | tf_op jit(solution)/shard_map/ppermute | solution.py:17
  75.1 0.8 collective-permute-done.24.refs_1_
  75.9 2.1 %collective-permute-start.29 = (f32[2,4,32,256]{3,2,1,0:T(8,128)S(1)}, f32[2,4,32,256]{3,2,1,0:T(8,128)S(1)}, u32[]{:S(2)}, u32[]{:S(2)}) collective-permute-start(f32[2,4,32,256]{3,2,1,0:T(8,128)S(1)} %get-tuple-element.197), channel_id=1, source_target_pairs={{0,8},{2,10},{4,12},{6,14},{8,0},{10,2},{12,4},{14,6},{16,24},{18,... | collective-permute-start | bytes 786440 | tf_op jit(solution)/shard_map/ppermute | solution.py:324
  78.0 2.7 %collective-permute-done.25.refs_2_ = f32[2,4,32,256]{3,2,1,0:T(8,128)S(1)} collective-permute-done((f32[2,4,32,256]{3,2,1,0:T(8,128)S(1)}, f32[2,4,32,256]{3,2,1,0:T(8,128)S(1)}, u32[]{:S(2)}, u32[]{:S(2)}) %collective-permute-start.25) | collective-permute-done | bytes 262176 | tf_op jit(solution)/shard_map/ppermute | solution.py:324
  80.7 3.4 %collective-permute-start.30 = (f32[2,4,32,256]{3,2,1,0:T(8,128)S(1)}, f32[2,4,32,256]{3,2,1,0:T(8,128)S(1)}, u32[]{:S(2)}, u32[]{:S(2)}) collective-permute-start(f32[2,4,32,256]{3,2,1,0:T(8,128)S(1)} %get-tuple-element.198), channel_id=1, source_target_pairs={{0,16},{2,18},{4,20},{6,22},{8,24},{10,26},{12,28},{14,30},{16,0},... | collective-permute-start | bytes 786440 | tf_op jit(solution)/shard_map/ppermute | solution.py:324
  84.1 1.1 %collective-permute-start.31 = (f32[2,4,32,256]{3,2,1,0:T(8,128)S(1)}, f32[2,4,32,256]{3,2,1,0:T(8,128)S(1)}, u32[]{:S(2)}, u32[]{:S(2)}) collective-permute-start(f32[2,4,32,256]{3,2,1,0:T(8,128)S(1)} %get-tuple-element.175), channel_id=1, source_target_pairs={{0,24},{2,26},{4,28},{6,30},{8,16},{10,18},{12,20},{14,22},{16,8},... | collective-permute-start | bytes 786440 | tf_op jit(solution)/shard_map/ppermute | solution.py:324
  85.2 1.2 %shard_map.119.refs_4_ = f32[4,32,4096]{2,1,0:T(8,128)} custom-call(f32[2,4,32,256]{3,2,1,0:T(8,128)S(1)} %get-tuple-element.176.refs_0_, f32[2,4,32,256]{3,2,1,0:T(8,128)S(1)} %collective-permute-done.24.refs_1_, f32[2,4,32,256]{3,2,1,0:T(8,128)S(1)} %collective-permute-done.25.refs_2_, f32[2,4,32,256]{3,2,1,0:T(8,128)S(1)} %collective-permute-done.26.refs_3_), custom_call_target="tpu_custom_call" | custom-call | tf_op jit(solution)/shard_map/pallas_call | solution.py:262
  86.5 1.1 %shard_map.120 = (f32[128,512]{1,0:T(8,128)}, f32[128,256]{1,0:T(8,128)S(1)}, f32[128,256]{1,0:T(8,128)S(1)}) custom-call(f32[128,512]{1,0:T(8,128)S(1)} %get-tuple-element.179.refs_0_, f32[128,512]{1,0:T(8,128)S(1)} %collective-permute-done.27.refs_1_, bf16[512,512]{1,0:T(8,128)(2,1)S(1)} %get-tuple-element.181.refs_2_, ...), custom_call_target="tpu_custom_call" | custom-call | tf_op jit(solution)/shard_map/pallas_call | solution.py:65
  87.6 2.0 %all-gather.3 = f32[256,256]{1,0:T(8,128)S(1)} all-gather(f32[128,256]{1,0:T(8,128)S(1)} %get-tuple-element.182), channel_id=5, replica_groups=mesh['cube'=16,'cores'=2] {'cores'}, dimensions={0}, use_global_device_ids=true | all-gather | bytes 393216 | tf_op jit(solution)/shard_map/all_gather | solution.py:25
  89.5 1.6 %shard_map.121 = (f32[4,256,256]{2,1,0:T(8,128)}, f32[4,256,256]{2,1,0:T(8,128)}) custom-call(f32[512,128]{1,0:T(8,128)S(1)} %get-tuple-element.183.refs_0_, f32[512,128]{1,0:T(8,128)S(1)} %collective-permute-done.17.refs_1_, f32[128,256]{1,0:T(8,128)S(1)} %get-tuple-element.184.refs_2_, f32[2,128,256]{2,1,0:T(8,128)S(1)} %bitcast.12, ...), custom_call_target="tpu_custom_call" | custom-call | tf_op jit(solution)/shard_map/pallas_call | solution.py:65
  91.2 1.2 %shard_map.122 = (f32[512,128]{1,0:T(8,128)}, f32[256,128]{1,0:T(8,128)S(1)}, f32[256,128]{1,0:T(8,128)S(1)}) custom-call(f32[512,128]{1,0:T(8,128)S(1)} %get-tuple-element.188.refs_0_, f32[512,128]{1,0:T(8,128)S(1)} %collective-permute-done.28.refs_1_, bf16[512,512]{1,0:T(8,128)(2,1)S(1)} %get-tuple-element.190.refs_2_, ...), custom_call_target="tpu_custom_call" | custom-call | tf_op jit(solution)/shard_map/pallas_call | solution.py:65
  92.4 2.0 %all-gather.4 = f32[512,128]{1,0:T(8,128)S(1)} all-gather(f32[256,128]{1,0:T(8,128)S(1)} %get-tuple-element.193), channel_id=6, replica_groups=mesh['cube'=16,'cores'=2] {'cores'}, dimensions={0}, use_global_device_ids=true | all-gather | bytes 393216 | tf_op jit(solution)/shard_map/all_gather | solution.py:25
  94.4 0.7 shard_map.123
  95.1 5.5 %collective-permute-done.30.refs_2_ = f32[2,4,32,256]{3,2,1,0:T(8,128)S(1)} collective-permute-done((f32[2,4,32,256]{3,2,1,0:T(8,128)S(1)}, f32[2,4,32,256]{3,2,1,0:T(8,128)S(1)}, u32[]{:S(2)}, u32[]{:S(2)}) %collective-permute-start.30) | collective-permute-done | bytes 262176 | tf_op jit(solution)/shard_map/ppermute | solution.py:324
  100.6 7.2 %collective-permute-done.31.refs_3_ = f32[2,4,32,256]{3,2,1,0:T(8,128)S(1)} collective-permute-done((f32[2,4,32,256]{3,2,1,0:T(8,128)S(1)}, f32[2,4,32,256]{3,2,1,0:T(8,128)S(1)}, u32[]{:S(2)}, u32[]{:S(2)}) %collective-permute-start.31) | collective-permute-done | bytes 262176 | tf_op jit(solution)/shard_map/ppermute | solution.py:324
  107.9 1.2 %shard_map.124 = f32[4,32,4096]{2,1,0:T(8,128)} custom-call(f32[2,4,32,256]{3,2,1,0:T(8,128)S(1)} %get-tuple-element.196.refs_0_, f32[2,4,32,256]{3,2,1,0:T(8,128)S(1)} %collective-permute-done.29.refs_1_, f32[2,4,32,256]{3,2,1,0:T(8,128)S(1)} %collective-permute-done.30.refs_2_, ...), custom_call_target="tpu_custom_call", output_to_operand_aliasing={{}: (4, {})} | custom-call | tf_op jit(solution)/shard_map/pallas_call | solution.py:262
  (38 shorter events, 0.5 us)
Async XLA Ops:
  0.6 6.9 %copy-start.1 = (f32[4,256,256]{2,1,0:T(8,128)S(1)}, f32[4,256,256]{2,1,0:T(8,128)}, u32[]{:S(2)}) copy-start(f32[4,256,256]{2,1,0:T(8,128)} %refs_6_.1) | copy-start | bytes 3145732
  0.6 6.1 %copy-start.4 = (f32[4,256,512]{2,1,0:T(8,128)S(1)}, f32[4,256,512]{2,1,0:T(8,128)}, u32[]{:S(2)}) copy-start(f32[4,256,512]{2,1,0:T(8,128)} %refs_3_.1) | copy-start | bytes 6291460
  0.7 2.5 %copy-start.2 = (f32[256,256]{1,0:T(8,128)S(1)}, f32[256,256]{1,0:T(8,128)}, u32[]{:S(2)}) copy-start(f32[256,256]{1,0:T(8,128)} %refs_4_.2) | copy-start | bytes 786436
  0.7 6.1 %collective-permute-start.3 = (f32[4,256,256]{2,1,0:T(8,128)}, f32[4,256,256]{2,1,0:T(8,128)S(1)}, u32[]{:S(2)}, u32[]{:S(2)}) collective-permute-start(f32[4,256,256]{2,1,0:T(8,128)} %refs_6_.1), channel_id=1, source_target_pairs={{0,1},{1,0},{2,3},{3,2},{4,5},{5,4},{6,7},{7,6},{8,9},{9,8},{10,11... | collective-permute-start | bytes 3145736 | tf_op jit(solution)/shard_map/ppermute | solution.py:21
  0.7 6.0 %collective-permute-start.4 = (f32[4,256,256]{2,1,0:T(8,128)}, f32[4,256,256]{2,1,0:T(8,128)S(1)}, u32[]{:S(2)}, u32[]{:S(2)}) collective-permute-start(f32[4,256,256]{2,1,0:T(8,128)} %refs_2_.7), channel_id=1, source_target_pairs={{0,1},{1,0},{2,3},{3,2},{4,5},{5,4},{6,7},{7,6},{8,9},{9,8},{10,11... | collective-permute-start | bytes 3145736 | tf_op jit(solution)/shard_map/ppermute | solution.py:21
  2.6 4.2 %collective-permute-start = (f32[256,512]{1,0:T(8,128)S(1)}, f32[256,512]{1,0:T(8,128)S(1)}, u32[]{:S(2)}, u32[]{:S(2)}) collective-permute-start(f32[256,512]{1,0:T(8,128)S(1)} %get-tuple-element.102.refs_0_), channel_id=1, source_target_pairs={{0,1},{1,0},{2,3},{3,2},{4,5},{5,4},{6,7},{7,6},{8,9},{9,8},{10,11... | collective-permute-start | bytes 1572872 | tf_op jit(solution)/shard_map/ppermute | solution.py:21
  2.7 4.1 %collective-permute-start.1 = (f32[256,512]{1,0:T(8,128)S(1)}, f32[256,512]{1,0:T(8,128)S(1)}, u32[]{:S(2)}, u32[]{:S(2)}) collective-permute-start(f32[256,512]{1,0:T(8,128)S(1)} %get-tuple-element.103.refs_2_), channel_id=1, source_target_pairs={{0,1},{1,0},{2,3},{3,2},{4,5},{5,4},{6,7},{7,6},{8,9},{9,8},{10,11... | collective-permute-start | bytes 1572872 | tf_op jit(solution)/shard_map/ppermute | solution.py:21
  3.2 3.6 %collective-permute-start.2 = (f32[256,256]{1,0:T(8,128)S(1)}, f32[256,256]{1,0:T(8,128)S(1)}, u32[]{:S(2)}, u32[]{:S(2)}) collective-permute-start(f32[256,256]{1,0:T(8,128)S(1)} %copy-done.2), channel_id=1, source_target_pairs={{0,1},{1,0},{2,3},{3,2},{4,5},{5,4},{6,7},{7,6},{8,9},{9,8},{10,11... | collective-permute-start | bytes 786440 | tf_op jit(solution)/shard_map/ppermute | solution.py:21
  6.8 5.9 %collective-permute-start.5 = (f32[4,256,512]{2,1,0:T(8,128)S(1)}, f32[4,256,512]{2,1,0:T(8,128)S(1)}, u32[]{:S(2)}, u32[]{:S(2)}) collective-permute-start(f32[4,256,512]{2,1,0:T(8,128)S(1)} %copy-done.4), channel_id=1, source_target_pairs={{0,1},{1,0},{2,3},{3,2},{4,5},{5,4},{6,7},{7,6},{8,9},{9,8},{10,11... | collective-permute-start | bytes 6291464 | tf_op jit(solution)/shard_map/ppermute | solution.py:21
  7.0 7.2 %collective-permute-start.6 = (f32[4,256,512]{2,1,0:T(8,128)}, f32[4,256,512]{2,1,0:T(8,128)S(1)}, u32[]{:S(2)}, u32[]{:S(2)}) collective-permute-start(f32[4,256,512]{2,1,0:T(8,128)} %refs_4_.3), channel_id=1, source_target_pairs={{0,1},{1,0},{2,3},{3,2},{4,5},{5,4},{6,7},{7,6},{8,9},{9,8},{10,11... | collective-permute-start | bytes 6291464 | tf_op jit(solution)/shard_map/ppermute | solution.py:21
  7.4 9.9 %collective-permute-start.7 = (f32[4,256,512]{2,1,0:T(8,128)}, f32[4,256,512]{2,1,0:T(8,128)S(1)}, u32[]{:S(2)}, u32[]{:S(2)}) collective-permute-start(f32[4,256,512]{2,1,0:T(8,128)} %refs_5_.1), channel_id=1, source_target_pairs={{0,1},{1,0},{2,3},{3,2},{4,5},{5,4},{6,7},{7,6},{8,9},{9,8},{10,11... | collective-permute-start | bytes 6291464 | tf_op jit(solution)/shard_map/ppermute | solution.py:21
  8.5 14.3 %collective-permute-start.8 = (f32[128,512]{1,0:T(8,128)S(1)}, f32[128,512]{1,0:T(8,128)S(1)}, u32[]{:S(2)}, u32[]{:S(2)}) collective-permute-start(f32[128,512]{1,0:T(8,128)S(1)} %get-tuple-element.119), channel_id=1, source_target_pairs={{0,16},{2,18},{4,20},{6,22},{8,24},{10,26},{12,28},{14,30},{16,0},... | collective-permute-start | bytes 786440 | tf_op jit(solution)/shard_map/ppermute | solution.py:17
  11.2 13.7 %collective-permute-start.9 = (f32[512,128]{1,0:T(8,128)S(1)}, f32[512,128]{1,0:T(8,128)S(1)}, u32[]{:S(2)}, u32[]{:S(2)}) collective-permute-start(f32[512,128]{1,0:T(8,128)S(1)} %get-tuple-element.183.refs_0_), channel_id=1, source_target_pairs={{0,2},{2,0},{4,6},{6,4},{8,10},{10,8},{12,14},{14,12},{16,18},{18,... | collective-permute-start | bytes 786440 | tf_op jit(solution)/shard_map/ppermute | solution.py:17
  12.7 7.5 %copy-start = (f32[4,256,256]{2,1,0:T(8,128)S(1)}, f32[4,256,256]{2,1,0:T(8,128)}, u32[]{:S(2)}) copy-start(f32[4,256,256]{2,1,0:T(8,128)} %refs_2_.7) | copy-start | bytes 3145732
  23.6 8.3 %collective-permute-start.10 = (f32[128,512]{1,0:T(8,128)S(1)}, f32[128,512]{1,0:T(8,128)S(1)}, u32[]{:S(2)}, u32[]{:S(2)}) collective-permute-start(f32[128,512]{1,0:T(8,128)S(1)} %get-tuple-element.138), channel_id=1, source_target_pairs={{0,8},{2,10},{4,12},{6,14},{8,0},{10,2},{12,4},{14,6},{16,24},{18,... | collective-permute-start | bytes 786440 | tf_op jit(solution)/shard_map/ppermute | solution.py:17
  25.7 8.5 %collective-permute-start.11 = (f32[512,128]{1,0:T(8,128)S(1)}, f32[512,128]{1,0:T(8,128)S(1)}, u32[]{:S(2)}, u32[]{:S(2)}) collective-permute-start(f32[512,128]{1,0:T(8,128)S(1)} %shard_map.107.refs_0_.refs_4_), channel_id=1, source_target_pairs={{0,4},{2,6},{4,0},{6,2},{8,12},{10,14},{12,8},{14,10},{16,20},{18,... | collective-permute-start | bytes 786440 | tf_op jit(solution)/shard_map/ppermute | solution.py:17
  27.4 8.6 %collective-permute-start.14 = (f32[128,256]{1,0:T(8,128)S(1)}, f32[128,256]{1,0:T(8,128)S(1)}, u32[]{:S(2)}, u32[]{:S(2)}) collective-permute-start(f32[128,256]{1,0:T(8,128)S(1)} %get-tuple-element.123), channel_id=1, source_target_pairs={{0,1},{1,0},{2,3},{3,2},{4,5},{5,4},{6,7},{7,6},{8,9},{9,8},{10,11... | collective-permute-start | bytes 393224 | tf_op jit(solution)/shard_map/ppermute | solution.py:21
  27.4 11.9 %collective-permute-start.12 = (f32[512,128]{1,0:T(8,128)S(1)}, f32[512,128]{1,0:T(8,128)S(1)}, u32[]{:S(2)}, u32[]{:S(2)}) collective-permute-start(f32[512,128]{1,0:T(8,128)S(1)} %shard_map.107.refs_0_.refs_4_), channel_id=1, source_target_pairs={{0,1},{1,0},{2,3},{3,2},{4,5},{5,4},{6,7},{7,6},{8,9},{9,8},{10,11... | collective-permute-start | bytes 786440 | tf_op jit(solution)/shard_map/ppermute | solution.py:21
  32.7 12.3 %collective-permute-start.15 = (f32[128,512]{1,0:T(8,128)S(1)}, f32[128,512]{1,0:T(8,128)S(1)}, u32[]{:S(2)}, u32[]{:S(2)}) collective-permute-start(f32[128,512]{1,0:T(8,128)S(1)} %get-tuple-element.154), channel_id=1, source_target_pairs={{0,4},{2,6},{4,0},{6,2},{8,12},{10,14},{12,8},{14,10},{16,20},{18,... | collective-permute-start | bytes 786440 | tf_op jit(solution)/shard_map/ppermute | solution.py:17
  35.1 11.0 %collective-permute-start.16 = (f32[512,128]{1,0:T(8,128)S(1)}, f32[512,128]{1,0:T(8,128)S(1)}, u32[]{:S(2)}, u32[]{:S(2)}) collective-permute-start(f32[512,128]{1,0:T(8,128)S(1)} %shard_map.110.refs_0_.refs_4_.refs_8_), channel_id=1, source_target_pairs={{0,8},{2,10},{4,12},{6,14},{8,0},{10,2},{12,4},{14,6},{16,24},{18,... | collective-permute-start | bytes 786440 | tf_op jit(solution)/shard_map/ppermute | solution.py:17
  36.0 15.9 %collective-permute-start.17 = (f32[512,128]{1,0:T(8,128)S(1)}, f32[512,128]{1,0:T(8,128)S(1)}, u32[]{:S(2)}, u32[]{:S(2)}) collective-permute-start(f32[512,128]{1,0:T(8,128)S(1)} %get-tuple-element.183.refs_0_), channel_id=1, source_target_pairs={{0,1},{1,0},{2,3},{3,2},{4,5},{5,4},{6,7},{7,6},{8,9},{9,8},{10,11... | collective-permute-start | bytes 786440 | tf_op jit(solution)/shard_map/ppermute | solution.py:21
  36.0 3.3 %collective-permute-start.13 = (f32[128,256]{1,0:T(8,128)S(1)}, f32[128,256]{1,0:T(8,128)S(1)}, u32[]{:S(2)}, u32[]{:S(2)}) collective-permute-start(f32[128,256]{1,0:T(8,128)S(1)} %get-tuple-element.143), channel_id=1, source_target_pairs={{0,1},{1,0},{2,3},{3,2},{4,5},{5,4},{6,7},{7,6},{8,9},{9,8},{10,11... | collective-permute-start | bytes 393224 | tf_op jit(solution)/shard_map/ppermute | solution.py:21
  38.7 0.7 copy-start.3
  40.6 25.9 %collective-permute-start.20 = (f32[2,4,32,256]{3,2,1,0:T(8,128)S(1)}, f32[2,4,32,256]{3,2,1,0:T(8,128)S(1)}, u32[]{:S(2)}, u32[]{:S(2)}) collective-permute-start(f32[2,4,32,256]{3,2,1,0:T(8,128)S(1)} %get-tuple-element.152), channel_id=1, source_target_pairs={{0,24},{2,26},{4,28},{6,30},{8,16},{10,18},{12,20},{14,22},{16,8},... | collective-permute-start | bytes 786440 | tf_op jit(solution)/shard_map/ppermute | solution.py:324
  43.8 14.0 %collective-permute-start.18 = (f32[2,4,32,256]{3,2,1,0:T(8,128)S(1)}, f32[2,4,32,256]{3,2,1,0:T(8,128)S(1)}, u32[]{:S(2)}, u32[]{:S(2)}) collective-permute-start(f32[2,4,32,256]{3,2,1,0:T(8,128)S(1)} %get-tuple-element.167), channel_id=1, source_target_pairs={{0,8},{2,10},{4,12},{6,14},{8,0},{10,2},{12,4},{14,6},{16,24},{18,... | collective-permute-start | bytes 786440 | tf_op jit(solution)/shard_map/ppermute | solution.py:324
  45.0 21.5 %collective-permute-start.19 = (f32[2,4,32,256]{3,2,1,0:T(8,128)S(1)}, f32[2,4,32,256]{3,2,1,0:T(8,128)S(1)}, u32[]{:S(2)}, u32[]{:S(2)}) collective-permute-start(f32[2,4,32,256]{3,2,1,0:T(8,128)S(1)} %get-tuple-element.168), channel_id=1, source_target_pairs={{0,16},{2,18},{4,20},{6,22},{8,24},{10,26},{12,28},{14,30},{16,0},... | collective-permute-start | bytes 786440 | tf_op jit(solution)/shard_map/ppermute | solution.py:324
  53.2 15.5 %collective-permute-start.21 = (f32[2,4,32,256]{3,2,1,0:T(8,128)S(1)}, f32[2,4,32,256]{3,2,1,0:T(8,128)S(1)}, u32[]{:S(2)}, u32[]{:S(2)}) collective-permute-start(f32[2,4,32,256]{3,2,1,0:T(8,128)S(1)} %get-tuple-element.173), channel_id=1, source_target_pairs={{0,2},{2,0},{4,6},{6,4},{8,10},{10,8},{12,14},{14,12},{16,18},{18,... | collective-permute-start | bytes 786440 | tf_op jit(solution)/shard_map/ppermute | solution.py:324
  54.7 15.4 %collective-permute-start.22 = (f32[2,4,32,256]{3,2,1,0:T(8,128)S(1)}, f32[2,4,32,256]{3,2,1,0:T(8,128)S(1)}, u32[]{:S(2)}, u32[]{:S(2)}) collective-permute-start(f32[2,4,32,256]{3,2,1,0:T(8,128)S(1)} %get-tuple-element.174), channel_id=1, source_target_pairs={{0,4},{2,6},{4,0},{6,2},{8,12},{10,14},{12,8},{14,10},{16,20},{18,... | collective-permute-start | bytes 786440 | tf_op jit(solution)/shard_map/ppermute | solution.py:324
  57.8 13.9 %collective-permute-start.23 = (f32[2,4,32,256]{3,2,1,0:T(8,128)S(1)}, f32[2,4,32,256]{3,2,1,0:T(8,128)S(1)}, u32[]{:S(2)}, u32[]{:S(2)}) collective-permute-start(f32[2,4,32,256]{3,2,1,0:T(8,128)S(1)} %get-tuple-element.165), channel_id=1, source_target_pairs={{0,6},{2,4},{4,2},{6,0},{8,14},{10,12},{12,10},{14,8},{16,22},{18,... | collective-permute-start | bytes 786440 | tf_op jit(solution)/shard_map/ppermute | solution.py:324
  66.6 9.3 %collective-permute-start.24 = (f32[2,4,32,256]{3,2,1,0:T(8,128)S(1)}, f32[2,4,32,256]{3,2,1,0:T(8,128)S(1)}, u32[]{:S(2)}, u32[]{:S(2)}) collective-permute-start(f32[2,4,32,256]{3,2,1,0:T(8,128)S(1)} %get-tuple-element.177), channel_id=1, source_target_pairs={{0,2},{2,0},{4,6},{6,4},{8,10},{10,8},{12,14},{14,12},{16,18},{18,... | collective-permute-start | bytes 786440 | tf_op jit(solution)/shard_map/ppermute | solution.py:324
  68.1 12.6 %collective-permute-start.25 = (f32[2,4,32,256]{3,2,1,0:T(8,128)S(1)}, f32[2,4,32,256]{3,2,1,0:T(8,128)S(1)}, u32[]{:S(2)}, u32[]{:S(2)}) collective-permute-start(f32[2,4,32,256]{3,2,1,0:T(8,128)S(1)} %get-tuple-element.178), channel_id=1, source_target_pairs={{0,4},{2,6},{4,0},{6,2},{8,12},{10,14},{12,8},{14,10},{16,20},{18,... | collective-permute-start | bytes 786440 | tf_op jit(solution)/shard_map/ppermute | solution.py:324
  68.6 15.4 %collective-permute-start.26 = (f32[2,4,32,256]{3,2,1,0:T(8,128)S(1)}, f32[2,4,32,256]{3,2,1,0:T(8,128)S(1)}, u32[]{:S(2)}, u32[]{:S(2)}) collective-permute-start(f32[2,4,32,256]{3,2,1,0:T(8,128)S(1)} %get-tuple-element.171), channel_id=1, source_target_pairs={{0,6},{2,4},{4,2},{6,0},{8,14},{10,12},{12,10},{14,8},{16,22},{18,... | collective-permute-start | bytes 786440 | tf_op jit(solution)/shard_map/ppermute | solution.py:324
  70.1 16.3 %collective-permute-start.27 = (f32[128,512]{1,0:T(8,128)S(1)}, f32[128,512]{1,0:T(8,128)S(1)}, u32[]{:S(2)}, u32[]{:S(2)}) collective-permute-start(f32[128,512]{1,0:T(8,128)S(1)} %get-tuple-element.180), channel_id=1, source_target_pairs={{0,2},{2,0},{4,6},{6,4},{8,10},{10,8},{12,14},{14,12},{16,18},{18,... | collective-permute-start | bytes 786440 | tf_op jit(solution)/shard_map/ppermute | solution.py:17
  71.6 19.6 %collective-permute-start.28 = (f32[512,128]{1,0:T(8,128)S(1)}, f32[512,128]{1,0:T(8,128)S(1)}, u32[]{:S(2)}, u32[]{:S(2)}) collective-permute-start(f32[512,128]{1,0:T(8,128)S(1)} %shard_map.114.refs_0_.refs_4_.refs_12_), channel_id=1, source_target_pairs={{0,16},{2,18},{4,20},{6,22},{8,24},{10,26},{12,28},{14,30},{16,0},... | collective-permute-start | bytes 786440 | tf_op jit(solution)/shard_map/ppermute | solution.py:17
  75.9 19.2 %collective-permute-start.29 = (f32[2,4,32,256]{3,2,1,0:T(8,128)S(1)}, f32[2,4,32,256]{3,2,1,0:T(8,128)S(1)}, u32[]{:S(2)}, u32[]{:S(2)}) collective-permute-start(f32[2,4,32,256]{3,2,1,0:T(8,128)S(1)} %get-tuple-element.197), channel_id=1, source_target_pairs={{0,8},{2,10},{4,12},{6,14},{8,0},{10,2},{12,4},{14,6},{16,24},{18,... | collective-permute-start | bytes 786440 | tf_op jit(solution)/shard_map/ppermute | solution.py:324
  80.7 19.9 %collective-permute-start.30 = (f32[2,4,32,256]{3,2,1,0:T(8,128)S(1)}, f32[2,4,32,256]{3,2,1,0:T(8,128)S(1)}, u32[]{:S(2)}, u32[]{:S(2)}) collective-permute-start(f32[2,4,32,256]{3,2,1,0:T(8,128)S(1)} %get-tuple-element.198), channel_id=1, source_target_pairs={{0,16},{2,18},{4,20},{6,22},{8,24},{10,26},{12,28},{14,30},{16,0},... | collective-permute-start | bytes 786440 | tf_op jit(solution)/shard_map/ppermute | solution.py:324
  84.1 23.8 %collective-permute-start.31 = (f32[2,4,32,256]{3,2,1,0:T(8,128)S(1)}, f32[2,4,32,256]{3,2,1,0:T(8,128)S(1)}, u32[]{:S(2)}, u32[]{:S(2)}) collective-permute-start(f32[2,4,32,256]{3,2,1,0:T(8,128)S(1)} %get-tuple-element.175), channel_id=1, source_target_pairs={{0,24},{2,26},{4,28},{6,30},{8,16},{10,18},{12,20},{14,22},{16,8},... | collective-permute-start | bytes 786440 | tf_op jit(solution)/shard_map/ppermute | solution.py:324

commit v2 on v1

--- a/solution.py
+++ b/solution.py
@@ -152,13 +152,16 @@
             lo[pl.ds(off, h), :] = v_lo
 
 
-def own_kernel(lb, refs, outs):
-    outs.a[...] = mul(refs.ph[...], refs.pl[...], refs.s[...])
+def fwd_own(refs, outs):
+    outs.a[...] = mul(refs.h[...], refs.l[...], refs.s[...])
+
+
+def bwd_own(level, refs, outs):
     h, k = refs.cot.shape[1], refs.cot.shape[2] // 2
     mine, _ = halves(k)
     for ref, off in zip((refs.cot, refs.cot_t), halves(h)):
-        outs.b[:, pl.ds(off, h)] = ref[lb, :, pl.ds(mine, k)].T
-    outs.b[...] += mul_t(refs.w[...], refs.qh[...], refs.ql[...])
+        outs.b[:, pl.ds(off, h)] = ref[level, :, pl.ds(mine, k)].T
+    outs.b[...] += mul_t(refs.w[...], refs.h[...], refs.l[...])
 
 
 def fwd_next(level, refs, outs):
@@ -331,60 +334,64 @@
         )
 
     early, late = list(range(1, levels - 1)), [0, last]
-    for t in range(levels):
-        lf, lb = t, last - t
-        yp = partner(y, base + lb)
-        if t < last:
-            sp = partner(s[lf], base + lf)
-        if t == 0:
-            new = [(name, q) for name in raw if "_t" not in name for q in range(levels)]
-            new = [q for q in new if f"{q[0]}{q[1]}h" not in parts]
-            parts.update(
-                run.named(
-                    functools.partial(prep_kernel, new),
-                    {"far_t": raw["far_t"], "own_t": raw["own_t"], "dinv_t": raw["dinv_t"],
-                     "far": far, "own": own, "dinv": dinv},
-                    {f"{name}{level}{e}": front for name, level in new for e in "hl"},
-                    scratch=[VMEM((len(new), h, r), F32), pltpu.SemaphoreType.DMA((len(new),))],
-                    hbm=(3, 4, 5),
-                )
-            )
+    yp = partner(y, base + last)
+    sp = partner(s[0], base)
+    new = [(name, q) for name in raw if "_t" not in name for q in range(levels)]
+    new = [q for q in new if f"{q[0]}{q[1]}h" not in parts]
+    parts.update(
+        run.named(
+            functools.partial(prep_kernel, new),
+            {
+                "far_t": raw["far_t"], "own_t": raw["own_t"], "dinv_t": raw["dinv_t"],
+                "far": far, "own": own, "dinv": dinv,
+            },
+            {f"{name}{level}{e}": front for name, level in new for e in "hl"},
+            scratch=[VMEM((len(new), h, r), F32), pltpu.SemaphoreType.DMA((len(new),))],
+            hbm=(3, 4, 5),
+        )
+    )
+
+    def pick(**fronts):
+        return {p + e: parts[f"{q}{e}"] for p, q in fronts.items() for e in "hl"}
+
+    def own_a(t):
+        fronts = {e: parts[f"own{t}{e}"] for e in "hl"}
+        return run.named(fwd_own, {"s": s[t], **fronts}, {"a": vec})["a"]
+
+    def own_b(t):
+        fronts = {e: parts[f"own{t}{e}"] for e in "hl"}
+        args = {"w": w, "cot": cot, "cot_t": cot_t, **fronts}
+        return run.named(functools.partial(bwd_own, t), args, {"b": vec_t})["b"]
+
+    for t in range(last):
+        lb = last - t
+        if t == last - 1:
+            crossed = exchange(outer(early, False), NEAR)
         x = run.named(
-            functools.partial(own_kernel, lb),
-            {
-                "s": s[lf], "w": w, "cot": cot, "cot_t": cot_t,
-                "ph": parts[f"own{lf}h"], "pl": parts[f"own{lf}l"],
-                "qh": parts[f"own{lb}h"], "ql": parts[f"own{lb}l"],
-            },
-            {"a": vec, "b": vec_t},
-        )
-        a, b = x["a"], x["b"]
-        if t == levels - 2:
-            crossed = exchange(outer(early, False), NEAR)
-        if t < last:
-            x = run.named(
-                bwd_next,
-                {
-                    "b": b, "yp": yp,
-                    **{p + e: parts[f"{q}{e}"] for e in "hl" for p, q in (("d", f"dinv{lb}"), ("p", f"far{lb - 1}"))},
-                },
-                {"y": vec_t, "w": vec_t, "wm": half_t, "ws": half_t},
-            )
-            w, y, wm[lb - 1], wt[lb - 1] = x["w"], x["y"], x["wm"], (both if t == levels - 2 else swap)(x["ws"])
-            x = run.named(
-                functools.partial(fwd_next, t + 1),
-                {
-                    "a": a, "sp": sp, "rows": rows,
-                    **{p + e: parts[f"{q}{e}"] for e in "hl" for p, q in (("p", f"far{lf}"), ("d", f"dinv{lf + 1}"))},
-                },
-                {"s": vec},
-            )
-            s[t + 1] = x["s"]
-            st[t + 1] = (swap if t == 0 else both)(s[t + 1])
+            functools.partial(fwd_next, t + 1),
+            {"a": own_a(t), "sp": sp, "rows": rows, **pick(p=f"far{t}", d=f"dinv{t + 1}")},
+            {"s": vec},
+        )
+        s[t + 1] = x["s"]
+        sp = partner(s[t + 1], base + t + 1)
+        st[t + 1] = (both if t == last - 1 else swap)(s[t + 1])
+        x = run.named(
+            bwd_next,
+            {"b": own_b(lb), "yp": yp, **pick(d=f"dinv{lb}", p=f"far{lb - 1}")},
+            {"y": vec_t, "w": vec_t, "wm": half_t, "ws": half_t},
+        )
+        w, y, wm[lb - 1], wt[lb - 1] = x["w"], x["y"], x["wm"], (both if t == last - 1 else swap)(x["ws"])
+        yp = partner(y, base + lb - 1)
     late_out = exchange(outer(late, True), 1)
+    a = own_a(last)
+    b = own_b(0)
     early_in = exchange(turn(crossed), 1)
     late_in = exchange(turn(late_out), NEAR)
-    sp = partner(after(s[last], *crossed), base + last)
+    u = run.named(
+        fwd_last,
+        {"a": a, "sp": sp, "ph": parts[f"far{last}h"], "pl": parts[f"far{last}l"]},
+        {"u": vec, "um": shape(h, kh), "us": shape(h, kh)},
+    )
     out = shape(levels, r // n, n * h)
     plan = [(m, (i, f), lv, m + NEAR * f) for m in nears for f in fars for i, lv in enumerate(early)]
     element_grad = place(run, early_in, plan, out)
@@ -398,11 +405,6 @@
         results_kernel,
         [v for q in range(levels) for v in (s[q], st[q], gms[q], gts[q])],
         [shape(levels, h, k), shape(levels, h, k)],
-    )
-    u = run.named(
-        fwd_last,
-        {"a": a, "sp": sp, "ph": parts[f"far{last}h"], "pl": parts[f"far{last}l"]},
-        {"u": vec, "um": shape(h, kh), "us": shape(h, kh)},
     )
     top_update, = run(join_kernel, [u["um"], both(u["us"])], [shape(h, k)])
     plan = [(f, (i, m), lv, m + NEAR * f) for m in nears for f in fars for i, lv in enumerate(late)]

time: 110 us -> 105 us (0.955)
  starting transfers between devices: 37.5 us -> 33.9 us
  blocking collectives: 10.5 us -> 8.31 us
    ppermute x8, waiting for transfers between devices: 5.31 us -> 10.1 us  [partner(): lax.ppermute(x, 'cube', [(i, i ^ 1 << distance) for i in range(lax.axis_s...]
    ppermute x12, waiting for transfers between devices: 24.4 us -> 20 us  [exchange(): lax.ppermute(v, 'cube', [(i, i ^ j * step) for i in range(n)])]
    all_gather x5 -> x4, blocking collectives: 10.5 us -> 8.31 us  [both(): return lax.all_gather(x, 'cores')]
    ppermute x12, starting transfers between devices: 20 us -> 18 us  [exchange(): lax.ppermute(v, 'cube', [(i, i ^ j * step) for i in range(n)])]
    pallas_call x21 -> x25, Pallas kernels: 19.9 us -> 20.6 us  [__call__(): pl.pallas_call(kernel, out_shape=tuple(outs), in_specs=[pl.BlockSpec(memo...]
    ppermute x12 -> x13, starting transfers between devices: 2.95 us -> 2.45 us  [swap(): return lax.ppermute(x, 'cores', [(0, 1), (1, 0)])]
    ppermute x12 -> x13, waiting for transfers between devices: 8.07 us -> 8.07 us  [swap(): return lax.ppermute(x, 'cores', [(0, 1), (1, 0)])]
  transfers between devices with their start and end apart: 32 -> 33, of which waited for: 11 -> 11; matrix products, arithmetic and copies ran while one was open for 0% -> 0% of each run, Pallas kernels for 19% -> 21%
where the time goes in v2:
time: 105 us
  waiting for transfers between devices  38.2 us (36%)
  starting transfers between devices  33.9 us (32%)
  Pallas kernels  23.1 us (22%)
  blocking collectives  8.31 us (8%)
  between operations  1.08 us (1%)
    pallas_call x25, Pallas kernels, __call__(): pl.pallas_call(kernel, out_shape=tuple(outs), in_specs=[pl.BlockSpec(memo...  20.6 us
    ppermute x12, waiting for transfers between devices, exchange(): lax.ppermute(v, 'cube', [(i, i ^ j * step) for i in range(n)])  20 us
    ppermute x12, starting transfers between devices, exchange(): lax.ppermute(v, 'cube', [(i, i ^ j * step) for i in range(n)])  18 us
    ppermute x8, starting transfers between devices, partner(): lax.ppermute(x, 'cube', [(i, i ^ 1 << distance) for i in range(lax.axis_s...  13.4 us
    ppermute x8, waiting for transfers between devices, partner(): lax.ppermute(x, 'cube', [(i, i ^ 1 << distance) for i in range(lax.axis_s...  10.1 us
    all_gather x4, blocking collectives, both(): return lax.all_gather(x, 'cores')  8.31 us
    ppermute x13, waiting for transfers between devices, swap(): return lax.ppermute(x, 'cores', [(0, 1), (1, 0)])  8.07 us
    pallas_call x2, Pallas kernels, place(): pl.pallas_call(functools.partial(place_kernel, plan), out_shape=out, in_s...  2.45 us
  transfers between devices with their start and end apart: 33, of which 11 were waited for; matrix products, arithmetic and copies ran while one was open for 0% of the time, Pallas kernels for 21%

profile of v2, /device:TPU:8, one launch (start us, length us, event | category | flops | bytes accessed | tf_op | source)
XLA Modules:
  0.0 104.7 jit_solution(3002261115709297407)
XLA Ops:
  0.7 0.5 collective-permute-start.4
  1.2 1.3 %shard_map.102 = (f32[256,512]{1,0:T(8,128)S(1)}, f32[256,512]{1,0:T(8,128)S(1)}) custom-call(f32[4,256,512]{2,1,0:T(8,128)} %refs_3_.1, f32[4,256,512]{2,1,0:T(8,128)} %refs_5_.1), custom_call_target="tpu_custom_call" | custom-call | tf_op jit(solution)/shard_map/pallas_call | solution.py:65
  2.7 0.5 collective-permute-start.1
  3.2 3.5 %collective-permute-done.2.refs_5_ = f32[256,256]{1,0:T(8,128)S(1)} collective-permute-done((f32[256,256]{1,0:T(8,128)S(1)}, f32[256,256]{1,0:T(8,128)S(1)}, u32[]{:S(2)}, u32[]{:S(2)}) %collective-permute-start.2) | collective-permute-done | bytes 262176 | tf_op jit(solution)/shard_map/ppermute | solution.py:21
  6.8 0.2 collective-permute-start.5
  7.0 0.4 collective-permute-start.6
  7.5 1.0 shard_map.103
  8.5 1.6 %collective-permute-start.8 = (f32[512,128]{1,0:T(8,128)S(1)}, f32[512,128]{1,0:T(8,128)S(1)}, u32[]{:S(2)}, u32[]{:S(2)}) collective-permute-start(f32[512,128]{1,0:T(8,128)S(1)} %get-tuple-element.171.refs_0_), channel_id=1, source_target_pairs={{0,2},{2,0},{4,6},{6,4},{8,10},{10,8},{12,14},{14,12},{16,18},{18,... | collective-permute-start | bytes 786440 | tf_op jit(solution)/shard_map/ppermute | solution.py:17
  10.1 2.6 %collective-permute-start.9 = (f32[128,512]{1,0:T(8,128)S(1)}, f32[128,512]{1,0:T(8,128)S(1)}, u32[]{:S(2)}, u32[]{:S(2)}) collective-permute-start(f32[128,512]{1,0:T(8,128)S(1)} %get-tuple-element.114), channel_id=1, source_target_pairs={{0,16},{2,18},{4,20},{6,22},{8,24},{10,26},{12,28},{14,30},{16,0},... | collective-permute-start | bytes 786440 | tf_op jit(solution)/shard_map/ppermute | solution.py:17
  12.7 1.5 %collective-permute-done.6.refs_1_ = f32[4,256,512]{2,1,0:T(8,128)S(1)} collective-permute-done((f32[4,256,512]{2,1,0:T(8,128)}, f32[4,256,512]{2,1,0:T(8,128)S(1)}, u32[]{:S(2)}, u32[]{:S(2)}) %collective-permute-start.6) | collective-permute-done | bytes 2097184 | tf_op jit(solution)/shard_map/ppermute | solution.py:21
  14.2 3.0 %collective-permute-done.7.refs_2_ = f32[4,256,512]{2,1,0:T(8,128)S(1)} collective-permute-done((f32[4,256,512]{2,1,0:T(8,128)}, f32[4,256,512]{2,1,0:T(8,128)S(1)}, u32[]{:S(2)}, u32[]{:S(2)}) %collective-permute-start.7) | collective-permute-done | bytes 2097184 | tf_op jit(solution)/shard_map/ppermute | solution.py:21
  17.2 3.0 %shard_map.104 = (bf16[512,512]{1,0:T(8,128)(2,1)S(1)}, bf16[512,512]{1,0:T(8,128)(2,1)S(1)}, bf16[512,512]{1,0:T(8,128)(2,1)S(1)}, bf16[512,512]{1,0:T(8,128)(2...) custom-call(f32[4,256,512]{2,1,0:T(8,128)S(1)} %collective-permute-d, ...), custom_call_target="tpu_custom_call" | custom-call | tf_op jit(solution)/shard_map/pallas_call | solution.py:65
  20.2 0.4 shard_map.105.refs_0_
  20.7 0.8 shard_map.106.refs_0_.refs_4_
  21.5 1.6 %collective-permute-start.10 = (f32[512,128]{1,0:T(8,128)S(1)}, f32[512,128]{1,0:T(8,128)S(1)}, u32[]{:S(2)}, u32[]{:S(2)}) collective-permute-start(f32[512,128]{1,0:T(8,128)S(1)} %shard_map.106.refs_0_.refs_4_), channel_id=1, source_target_pairs={{0,4},{2,6},{4,0},{6,2},{8,12},{10,14},{12,8},{14,10},{16,20},{18,... | collective-permute-start | bytes 786440 | tf_op jit(solution)/shard_map/ppermute | solution.py:17
  23.1 0.4 shard_map.107.refs_0_
  23.5 0.5 collective-permute-done.9.refs_1_
  24.0 0.8 shard_map.108
  24.8 1.4 %collective-permute-start.11 = (f32[128,512]{1,0:T(8,128)S(1)}, f32[128,512]{1,0:T(8,128)S(1)}, u32[]{:S(2)}, u32[]{:S(2)}) collective-permute-start(f32[128,512]{1,0:T(8,128)S(1)} %get-tuple-element.130), channel_id=1, source_target_pairs={{0,8},{2,10},{4,12},{6,14},{8,0},{10,2},{12,4},{14,6},{16,24},{18,... | collective-permute-start | bytes 786440 | tf_op jit(solution)/shard_map/ppermute | solution.py:17
  26.2 0.4 shard_map.109.refs_0_
  26.7 3.3 %collective-permute-done.10.refs_1_ = f32[512,128]{1,0:T(8,128)S(1)} collective-permute-done((f32[512,128]{1,0:T(8,128)S(1)}, f32[512,128]{1,0:T(8,128)S(1)}, u32[]{:S(2)}, u32[]{:S(2)}) %collective-permute-start.10) | collective-permute-done | bytes 262176 | tf_op jit(solution)/shard_map/ppermute | solution.py:17
  29.9 0.8 shard_map.110.refs_4_.refs_0_.refs_8_
  30.8 0.3 collective-permute-start.16
  31.1 0.2 collective-permute-start.15
  31.3 0.4 shard_map.111.refs_0_
  31.7 1.4 %collective-permute-done.11.refs_1_ = f32[128,512]{1,0:T(8,128)S(1)} collective-permute-done((f32[128,512]{1,0:T(8,128)S(1)}, f32[128,512]{1,0:T(8,128)S(1)}, u32[]{:S(2)}, u32[]{:S(2)}) %collective-permute-start.11) | collective-permute-done | bytes 262176 | tf_op jit(solution)/shard_map/ppermute | solution.py:17
  33.1 0.8 shard_map.112
  34.0 1.6 %collective-permute-start.17 = (f32[128,512]{1,0:T(8,128)S(1)}, f32[128,512]{1,0:T(8,128)S(1)}, u32[]{:S(2)}, u32[]{:S(2)}) collective-permute-start(f32[128,512]{1,0:T(8,128)S(1)} %get-tuple-element.139), channel_id=1, source_target_pairs={{0,4},{2,6},{4,0},{6,2},{8,12},{10,14},{12,8},{14,10},{16,20},{18,... | collective-permute-start | bytes 786440 | tf_op jit(solution)/shard_map/ppermute | solution.py:17
  35.7 1.3 %shard_map.113 = (f32[2,4,32,256]{3,2,1,0:T(8,128)S(1)}, f32[2,4,32,256]{3,2,1,0:T(8,128)S(1)}, f32[2,4,32,256]{3,2,1,0:T(8,128)S(1)}, f32[2,4,32,256]{3,2,1,0:T(8,128)S(1)}) custom-call(s32[1,512]{1,0:T(1,128)S(1)} %copy-done.3, f32[512,128]{1,0:T(8,128)S(1)} %shard_map.106.refs_0_.refs_4_, f32[512,128]{1,0:T(8,128)S(1)} %collective-permute-done.12.refs_1_.refs_5_, ...), custom_call_target="tpu_custom_call" | custom-call | tf_op jit(solution)/shard_map/pallas_call | solution.py:65
  37.0 2.3 %collective-permute-start.21 = (f32[2,4,32,256]{3,2,1,0:T(8,128)S(1)}, f32[2,4,32,256]{3,2,1,0:T(8,128)S(1)}, u32[]{:S(2)}, u32[]{:S(2)}) collective-permute-start(f32[2,4,32,256]{3,2,1,0:T(8,128)S(1)} %get-tuple-element.136), channel_id=1, source_target_pairs={{0,24},{2,26},{4,28},{6,30},{8,16},{10,18},{12,20},{14,22},{16,8},... | collective-permute-start | bytes 786440 | tf_op jit(solution)/shard_map/ppermute | solution.py:327
  39.3 0.4 shard_map.114.refs_0_
  39.7 0.8 shard_map.115.refs_4_.refs_0_.refs_12_
  40.5 2.2 %all-gather.1 = f32[1024,128]{1,0:T(8,128)S(1)} all-gather(f32[512,128]{1,0:T(8,128)S(1)} %shard_map.115.refs_4_.refs_0_.refs_12_), channel_id=3, replica_groups=mesh['cube'=16,'cores'=2] {'cores'}, dimensions={0}, use_global_device_ids=true | all-gather | bytes 786432 | tf_op jit(solution)/shard_map/all_gather | solution.py:25
  42.7 2.6 %collective-permute-start.19 = (f32[2,4,32,256]{3,2,1,0:T(8,128)S(1)}, f32[2,4,32,256]{3,2,1,0:T(8,128)S(1)}, u32[]{:S(2)}, u32[]{:S(2)}) collective-permute-start(f32[2,4,32,256]{3,2,1,0:T(8,128)S(1)} %get-tuple-element.151), channel_id=1, source_target_pairs={{0,8},{2,10},{4,12},{6,14},{8,0},{10,2},{12,4},{14,6},{16,24},{18,... | collective-permute-start | bytes 786440 | tf_op jit(solution)/shard_map/ppermute | solution.py:327
  45.3 0.4 shard_map.116.refs_0_
  45.7 0.8 shard_map.117
  46.5 0.4 collective-permute-start.20
  46.9 2.2 %all-gather = f32[256,256]{1,0:T(8,128)S(1)} all-gather(f32[128,256]{1,0:T(8,128)S(1)} %get-tuple-element.141), channel_id=2, replica_groups=mesh['cube'=16,'cores'=2] {'cores'}, dimensions={0}, use_global_device_ids=true | all-gather | bytes 393216 | tf_op jit(solution)/shard_map/all_gather | solution.py:25
  49.0 1.3 %shard_map.118 = (f32[2,4,32,256]{3,2,1,0:T(8,128)S(1)}, f32[2,4,32,256]{3,2,1,0:T(8,128)S(1)}, f32[2,4,32,256]{3,2,1,0:T(8,128)S(1)}, f32[2,4,32,256]{3,2,1,0:T(8,128)S(1)}) custom-call(s32[1,512]{1,0:T(1,128)S(1)} %copy-done.3, f32[512,128]{1,0:T(8,128)S(1)} %get-tuple-element.171.refs_0_, f32[512,128]{1,0:T(8,128)S(1)} %collective-permute-done.18.refs_1_, ...), custom_call_target="tpu_custom_call" | custom-call | tf_op jit(solution)/shard_map/pallas_call | solution.py:65
  50.3 1.5 %collective-permute-start.22 = (f32[2,4,32,256]{3,2,1,0:T(8,128)S(1)}, f32[2,4,32,256]{3,2,1,0:T(8,128)S(1)}, u32[]{:S(2)}, u32[]{:S(2)}) collective-permute-start(f32[2,4,32,256]{3,2,1,0:T(8,128)S(1)} %get-tuple-element.157), channel_id=1, source_target_pairs={{0,2},{2,0},{4,6},{6,4},{8,10},{10,8},{12,14},{14,12},{16,18},{18,... | collective-permute-start | bytes 786440 | tf_op jit(solution)/shard_map/ppermute | solution.py:327
  51.8 1.7 %collective-permute-start.23 = (f32[2,4,32,256]{3,2,1,0:T(8,128)S(1)}, f32[2,4,32,256]{3,2,1,0:T(8,128)S(1)}, u32[]{:S(2)}, u32[]{:S(2)}) collective-permute-start(f32[2,4,32,256]{3,2,1,0:T(8,128)S(1)} %get-tuple-element.158), channel_id=1, source_target_pairs={{0,4},{2,6},{4,0},{6,2},{8,12},{10,14},{12,8},{14,10},{16,20},{18,... | collective-permute-start | bytes 786440 | tf_op jit(solution)/shard_map/ppermute | solution.py:327
  53.5 1.2 %collective-permute-done.19.refs_1_ = f32[2,4,32,256]{3,2,1,0:T(8,128)S(1)} collective-permute-done((f32[2,4,32,256]{3,2,1,0:T(8,128)S(1)}, f32[2,4,32,256]{3,2,1,0:T(8,128)S(1)}, u32[]{:S(2)}, u32[]{:S(2)}) %collective-permute-start.19) | collective-permute-done | bytes 262176 | tf_op jit(solution)/shard_map/ppermute | solution.py:327
  54.7 1.1 %collective-permute-start.24 = (f32[2,4,32,256]{3,2,1,0:T(8,128)S(1)}, f32[2,4,32,256]{3,2,1,0:T(8,128)S(1)}, u32[]{:S(2)}, u32[]{:S(2)}) collective-permute-start(f32[2,4,32,256]{3,2,1,0:T(8,128)S(1)} %get-tuple-element.146), channel_id=1, source_target_pairs={{0,6},{2,4},{4,2},{6,0},{8,14},{10,12},{12,10},{14,8},{16,22},{18,... | collective-permute-start | bytes 786440 | tf_op jit(solution)/shard_map/ppermute | solution.py:327
  55.7 0.4 shard_map.119.refs_0_
  56.2 0.4 shard_map.120.refs_0_
  56.6 5.7 %collective-permute-done.20.refs_2_ = f32[2,4,32,256]{3,2,1,0:T(8,128)S(1)} collective-permute-done((f32[2,4,32,256]{3,2,1,0:T(8,128)S(1)}, f32[2,4,32,256]{3,2,1,0:T(8,128)S(1)}, u32[]{:S(2)}, u32[]{:S(2)}) %collective-permute-start.20) | collective-permute-done | bytes 262176 | tf_op jit(solution)/shard_map/ppermute | solution.py:327
  62.2 3.4 %collective-permute-start.25 = (f32[512,128]{1,0:T(8,128)S(1)}, f32[512,128]{1,0:T(8,128)S(1)}, u32[]{:S(2)}, u32[]{:S(2)}) collective-permute-start(f32[512,128]{1,0:T(8,128)S(1)} %shard_map.115.refs_4_.refs_0_.refs_12_), channel_id=1, source_target_pairs={{0,16},{2,18},{4,20},{6,22},{8,24},{10,26},{12,28},{14,30},{16,0},... | collective-permute-start | bytes 786440 | tf_op jit(solution)/shard_map/ppermute | solution.py:17
  65.7 1.1 %collective-permute-start.26 = (f32[2,4,32,256]{3,2,1,0:T(8,128)S(1)}, f32[2,4,32,256]{3,2,1,0:T(8,128)S(1)}, u32[]{:S(2)}, u32[]{:S(2)}) collective-permute-start(f32[2,4,32,256]{3,2,1,0:T(8,128)S(1)} %get-tuple-element.165), channel_id=1, source_target_pairs={{0,2},{2,0},{4,6},{6,4},{8,10},{10,8},{12,14},{14,12},{16,18},{18,... | collective-permute-start | bytes 786440 | tf_op jit(solution)/shard_map/ppermute | solution.py:327
  66.8 0.8 collective-permute-start.27
  67.6 1.6 %collective-permute-start.28 = (f32[2,4,32,256]{3,2,1,0:T(8,128)S(1)}, f32[2,4,32,256]{3,2,1,0:T(8,128)S(1)}, u32[]{:S(2)}, u32[]{:S(2)}) collective-permute-start(f32[2,4,32,256]{3,2,1,0:T(8,128)S(1)} %get-tuple-element.155), channel_id=1, source_target_pairs={{0,6},{2,4},{4,2},{6,0},{8,14},{10,12},{12,10},{14,8},{16,22},{18,... | collective-permute-start | bytes 786440 | tf_op jit(solution)/shard_map/ppermute | solution.py:327
  69.3 1.0 collective-permute-start.29
  70.3 4.9 %collective-permute-done.25.refs_1_ = f32[512,128]{1,0:T(8,128)S(1)} collective-permute-done((f32[512,128]{1,0:T(8,128)S(1)}, f32[512,128]{1,0:T(8,128)S(1)}, u32[]{:S(2)}, u32[]{:S(2)}) %collective-permute-start.25) | collective-permute-done | bytes 262176 | tf_op jit(solution)/shard_map/ppermute | solution.py:17
  75.2 3.5 %collective-permute-start.30 = (f32[2,4,32,256]{3,2,1,0:T(8,128)S(1)}, f32[2,4,32,256]{3,2,1,0:T(8,128)S(1)}, u32[]{:S(2)}, u32[]{:S(2)}) collective-permute-start(f32[2,4,32,256]{3,2,1,0:T(8,128)S(1)} %get-tuple-element.179), channel_id=1, source_target_pairs={{0,8},{2,10},{4,12},{6,14},{8,0},{10,2},{12,4},{14,6},{16,24},{18,... | collective-permute-start | bytes 786440 | tf_op jit(solution)/shard_map/ppermute | solution.py:327
  78.7 1.5 %collective-permute-start.32 = (f32[2,4,32,256]{3,2,1,0:T(8,128)S(1)}, f32[2,4,32,256]{3,2,1,0:T(8,128)S(1)}, u32[]{:S(2)}, u32[]{:S(2)}) collective-permute-start(f32[2,4,32,256]{3,2,1,0:T(8,128)S(1)} %get-tuple-element.159), channel_id=1, source_target_pairs={{0,24},{2,26},{4,28},{6,30},{8,16},{10,18},{12,20},{14,22},{16,8},... | collective-permute-start | bytes 786440 | tf_op jit(solution)/shard_map/ppermute | solution.py:327
  80.2 1.2 %shard_map.123 = (f32[512,128]{1,0:T(8,128)}, f32[256,128]{1,0:T(8,128)S(1)}, f32[256,128]{1,0:T(8,128)S(1)}) custom-call(f32[512,128]{1,0:T(8,128)S(1)} %shard_map.119.refs_0_, f32[512,128]{1,0:T(8,128)S(1)} %collective-permute-done.25.refs_1_, bf16[512,512]{1,0:T(8,128)(2,1)S(1)} %get-tuple-element.161.refs_2_, bf16[512,512]{1,0:T(8,128)(2,1)S(1)} %get-tuple-element.162.refs_3_), custom_call_target="tpu_custom_call" | custom-call | tf_op jit(solution)/shard_map/pallas_call | solution.py:65
  81.4 2.0 %all-gather.3 = f32[512,128]{1,0:T(8,128)S(1)} all-gather(f32[256,128]{1,0:T(8,128)S(1)} %get-tuple-element.163), channel_id=5, replica_groups=mesh['cube'=16,'cores'=2] {'cores'}, dimensions={0}, use_global_device_ids=true | all-gather | bytes 393216 | tf_op jit(solution)/shard_map/all_gather | solution.py:25
  83.4 1.2 %shard_map.124.refs_4_ = f32[4,32,4096]{2,1,0:T(8,128)} custom-call(f32[2,4,32,256]{3,2,1,0:T(8,128)S(1)} %get-tuple-element.164.refs_0_, f32[2,4,32,256]{3,2,1,0:T(8,128)S(1)} %collective-permute-done.26.refs_1_, f32[2,4,32,256]{3,2,1,0:T(8,128)S(1)} %collective-permute-done.27.refs_2_, f32[2,4,32,256]{3,2,1,0:T(8,128)S(1)} %collective-permute-done.28.refs_3_), custom_call_target="tpu_custom_call" | custom-call | tf_op jit(solution)/shard_map/pallas_call | solution.py:265
  84.6 1.1 %shard_map.125 = (f32[128,512]{1,0:T(8,128)}, f32[128,256]{1,0:T(8,128)S(1)}, f32[128,256]{1,0:T(8,128)S(1)}) custom-call(f32[128,512]{1,0:T(8,128)S(1)} %shard_map.120.refs_0_, f32[128,512]{1,0:T(8,128)S(1)} %collective-permute-done.29.refs_1_, bf16[512,512]{1,0:T(8,128)(2,1)S(1)} %get-tuple-element.169.refs_2_, bf16[512,512]{1,0:T(8,128)(2,1)S(1)} %get-tuple-element.98.refs_3_), custom_call_target="tpu_custom_call" | custom-call | tf_op jit(solution)/shard_map/pallas_call | solution.py:65
  85.7 2.0 %all-gather.2 = f32[256,256]{1,0:T(8,128)S(1)} all-gather(f32[128,256]{1,0:T(8,128)S(1)} %get-tuple-element.170), channel_id=4, replica_groups=mesh['cube'=16,'cores'=2] {'cores'}, dimensions={0}, use_global_device_ids=true | all-gather | bytes 393216 | tf_op jit(solution)/shard_map/all_gather | solution.py:25
  87.7 1.6 %shard_map.126 = (f32[4,256,256]{2,1,0:T(8,128)}, f32[4,256,256]{2,1,0:T(8,128)}) custom-call(f32[512,128]{1,0:T(8,128)S(1)} %get-tuple-element.171.refs_0_, f32[512,128]{1,0:T(8,128)S(1)} %collective-permute-done.18.refs_1_, f32[128,256]{1,0:T(8,128)S(1)} %get-tuple-element.172.refs_2_, f32[2,128,256]{2,1,0:T(8,128)S(1)} %bitcast.8, ...), custom_call_target="tpu_custom_call" | custom-call | tf_op jit(solution)/shard_map/pallas_call | solution.py:65
  89.3 0.7 shard_map.127
  90.1 6.6 %collective-permute-done.31.refs_2_ = f32[2,4,32,256]{3,2,1,0:T(8,128)S(1)} collective-permute-done((f32[2,4,32,256]{3,2,1,0:T(8,128)S(1)}, f32[2,4,32,256]{3,2,1,0:T(8,128)S(1)}, u32[]{:S(2)}, u32[]{:S(2)}) %collective-permute-start.31) | collective-permute-done | bytes 262176 | tf_op jit(solution)/shard_map/ppermute | solution.py:327
  96.7 6.6 %collective-permute-done.32.refs_3_ = f32[2,4,32,256]{3,2,1,0:T(8,128)S(1)} collective-permute-done((f32[2,4,32,256]{3,2,1,0:T(8,128)S(1)}, f32[2,4,32,256]{3,2,1,0:T(8,128)S(1)}, u32[]{:S(2)}, u32[]{:S(2)}) %collective-permute-start.32) | collective-permute-done | bytes 262176 | tf_op jit(solution)/shard_map/ppermute | solution.py:327
  103.3 1.2 %shard_map.128 = f32[4,32,4096]{2,1,0:T(8,128)} custom-call(f32[2,4,32,256]{3,2,1,0:T(8,128)S(1)} %get-tuple-element.178.refs_0_, f32[2,4,32,256]{3,2,1,0:T(8,128)S(1)} %collective-permute-done.30.refs_1_, f32[2,4,32,256]{3,2,1,0:T(8,128)S(1)} %collective-permute-done.31.refs_2_, ...), custom_call_target="tpu_custom_call", output_to_operand_aliasing={{}: (4, {})} | custom-call | tf_op jit(solution)/shard_map/pallas_call | solution.py:265
  (43 shorter events, 0.9 us)
Async XLA Ops:
  0.6 6.9 %copy-start.1 = (f32[4,256,256]{2,1,0:T(8,128)S(1)}, f32[4,256,256]{2,1,0:T(8,128)}, u32[]{:S(2)}) copy-start(f32[4,256,256]{2,1,0:T(8,128)} %refs_6_.1) | copy-start | bytes 3145732
  0.6 6.1 %copy-start.4 = (f32[4,256,512]{2,1,0:T(8,128)S(1)}, f32[4,256,512]{2,1,0:T(8,128)}, u32[]{:S(2)}) copy-start(f32[4,256,512]{2,1,0:T(8,128)} %refs_3_.1) | copy-start | bytes 6291460
  0.7 2.5 %copy-start.2 = (f32[256,256]{1,0:T(8,128)S(1)}, f32[256,256]{1,0:T(8,128)}, u32[]{:S(2)}) copy-start(f32[256,256]{1,0:T(8,128)} %refs_4_.2) | copy-start | bytes 786436
  0.7 6.1 %collective-permute-start.3 = (f32[4,256,256]{2,1,0:T(8,128)}, f32[4,256,256]{2,1,0:T(8,128)S(1)}, u32[]{:S(2)}, u32[]{:S(2)}) collective-permute-start(f32[4,256,256]{2,1,0:T(8,128)} %refs_6_.1), channel_id=1, source_target_pairs={{0,1},{1,0},{2,3},{3,2},{4,5},{5,4},{6,7},{7,6},{8,9},{9,8},{10,11... | collective-permute-start | bytes 3145736 | tf_op jit(solution)/shard_map/ppermute | solution.py:21
  0.7 6.0 %collective-permute-start.4 = (f32[4,256,256]{2,1,0:T(8,128)}, f32[4,256,256]{2,1,0:T(8,128)S(1)}, u32[]{:S(2)}, u32[]{:S(2)}) collective-permute-start(f32[4,256,256]{2,1,0:T(8,128)} %refs_1_.7), channel_id=1, source_target_pairs={{0,1},{1,0},{2,3},{3,2},{4,5},{5,4},{6,7},{7,6},{8,9},{9,8},{10,11... | collective-permute-start | bytes 3145736 | tf_op jit(solution)/shard_map/ppermute | solution.py:21
  2.6 4.2 %collective-permute-start = (f32[256,512]{1,0:T(8,128)S(1)}, f32[256,512]{1,0:T(8,128)S(1)}, u32[]{:S(2)}, u32[]{:S(2)}) collective-permute-start(f32[256,512]{1,0:T(8,128)S(1)} %get-tuple-element.93.refs_0_), channel_id=1, source_target_pairs={{0,1},{1,0},{2,3},{3,2},{4,5},{5,4},{6,7},{7,6},{8,9},{9,8},{10,11... | collective-permute-start | bytes 1572872 | tf_op jit(solution)/shard_map/ppermute | solution.py:21
  2.7 4.1 %collective-permute-start.1 = (f32[256,512]{1,0:T(8,128)S(1)}, f32[256,512]{1,0:T(8,128)S(1)}, u32[]{:S(2)}, u32[]{:S(2)}) collective-permute-start(f32[256,512]{1,0:T(8,128)S(1)} %get-tuple-element.94.refs_2_), channel_id=1, source_target_pairs={{0,1},{1,0},{2,3},{3,2},{4,5},{5,4},{6,7},{7,6},{8,9},{9,8},{10,11... | collective-permute-start | bytes 1572872 | tf_op jit(solution)/shard_map/ppermute | solution.py:21
  3.2 3.6 %collective-permute-start.2 = (f32[256,256]{1,0:T(8,128)S(1)}, f32[256,256]{1,0:T(8,128)S(1)}, u32[]{:S(2)}, u32[]{:S(2)}) collective-permute-start(f32[256,256]{1,0:T(8,128)S(1)} %copy-done.2), channel_id=1, source_target_pairs={{0,1},{1,0},{2,3},{3,2},{4,5},{5,4},{6,7},{7,6},{8,9},{9,8},{10,11... | collective-permute-start | bytes 786440 | tf_op jit(solution)/shard_map/ppermute | solution.py:21
  6.8 5.9 %collective-permute-start.5 = (f32[4,256,512]{2,1,0:T(8,128)S(1)}, f32[4,256,512]{2,1,0:T(8,128)S(1)}, u32[]{:S(2)}, u32[]{:S(2)}) collective-permute-start(f32[4,256,512]{2,1,0:T(8,128)S(1)} %copy-done.4), channel_id=1, source_target_pairs={{0,1},{1,0},{2,3},{3,2},{4,5},{5,4},{6,7},{7,6},{8,9},{9,8},{10,11... | collective-permute-start | bytes 6291464 | tf_op jit(solution)/shard_map/ppermute | solution.py:21
  7.0 7.2 %collective-permute-start.6 = (f32[4,256,512]{2,1,0:T(8,128)}, f32[4,256,512]{2,1,0:T(8,128)S(1)}, u32[]{:S(2)}, u32[]{:S(2)}) collective-permute-start(f32[4,256,512]{2,1,0:T(8,128)} %refs_4_.3), channel_id=1, source_target_pairs={{0,1},{1,0},{2,3},{3,2},{4,5},{5,4},{6,7},{7,6},{8,9},{9,8},{10,11... | collective-permute-start | bytes 6291464 | tf_op jit(solution)/shard_map/ppermute | solution.py:21
  7.4 9.9 %collective-permute-start.7 = (f32[4,256,512]{2,1,0:T(8,128)}, f32[4,256,512]{2,1,0:T(8,128)S(1)}, u32[]{:S(2)}, u32[]{:S(2)}) collective-permute-start(f32[4,256,512]{2,1,0:T(8,128)} %refs_5_.1), channel_id=1, source_target_pairs={{0,1},{1,0},{2,3},{3,2},{4,5},{5,4},{6,7},{7,6},{8,9},{9,8},{10,11... | collective-permute-start | bytes 6291464 | tf_op jit(solution)/shard_map/ppermute | solution.py:21
  8.5 12.2 %collective-permute-start.8 = (f32[512,128]{1,0:T(8,128)S(1)}, f32[512,128]{1,0:T(8,128)S(1)}, u32[]{:S(2)}, u32[]{:S(2)}) collective-permute-start(f32[512,128]{1,0:T(8,128)S(1)} %get-tuple-element.171.refs_0_), channel_id=1, source_target_pairs={{0,2},{2,0},{4,6},{6,4},{8,10},{10,8},{12,14},{14,12},{16,18},{18,... | collective-permute-start | bytes 786440 | tf_op jit(solution)/shard_map/ppermute | solution.py:17
  10.1 13.9 %collective-permute-start.9 = (f32[128,512]{1,0:T(8,128)S(1)}, f32[128,512]{1,0:T(8,128)S(1)}, u32[]{:S(2)}, u32[]{:S(2)}) collective-permute-start(f32[128,512]{1,0:T(8,128)S(1)} %get-tuple-element.114), channel_id=1, source_target_pairs={{0,16},{2,18},{4,20},{6,22},{8,24},{10,26},{12,28},{14,30},{16,0},... | collective-permute-start | bytes 786440 | tf_op jit(solution)/shard_map/ppermute | solution.py:17
  20.7 2.4 %copy-start = (f32[4,256,256]{2,1,0:T(8,128)S(1)}, f32[4,256,256]{2,1,0:T(8,128)}, u32[]{:S(2)}) copy-start(f32[4,256,256]{2,1,0:T(8,128)} %refs_1_.7) | copy-start | bytes 3145732
  21.5 8.4 %collective-permute-start.10 = (f32[512,128]{1,0:T(8,128)S(1)}, f32[512,128]{1,0:T(8,128)S(1)}, u32[]{:S(2)}, u32[]{:S(2)}) collective-permute-start(f32[512,128]{1,0:T(8,128)S(1)} %shard_map.106.refs_0_.refs_4_), channel_id=1, source_target_pairs={{0,4},{2,6},{4,0},{6,2},{8,12},{10,14},{12,8},{14,10},{16,20},{18,... | collective-permute-start | bytes 786440 | tf_op jit(solution)/shard_map/ppermute | solution.py:17
  24.8 8.3 %collective-permute-start.11 = (f32[128,512]{1,0:T(8,128)S(1)}, f32[128,512]{1,0:T(8,128)S(1)}, u32[]{:S(2)}, u32[]{:S(2)}) collective-permute-start(f32[128,512]{1,0:T(8,128)S(1)} %get-tuple-element.130), channel_id=1, source_target_pairs={{0,8},{2,10},{4,12},{6,14},{8,0},{10,2},{12,4},{14,6},{16,24},{18,... | collective-permute-start | bytes 786440 | tf_op jit(solution)/shard_map/ppermute | solution.py:17
  26.2 9.3 %collective-permute-start.12 = (f32[512,128]{1,0:T(8,128)S(1)}, f32[512,128]{1,0:T(8,128)S(1)}, u32[]{:S(2)}, u32[]{:S(2)}) collective-permute-start(f32[512,128]{1,0:T(8,128)S(1)} %shard_map.106.refs_0_.refs_4_), channel_id=1, source_target_pairs={{0,1},{1,0},{2,3},{3,2},{4,5},{5,4},{6,7},{7,6},{8,9},{9,8},{10,11... | collective-permute-start | bytes 786440 | tf_op jit(solution)/shard_map/ppermute | solution.py:21
  30.7 5.0 %collective-permute-start.14 = (f32[512,128]{1,0:T(8,128)S(1)}, f32[512,128]{1,0:T(8,128)S(1)}, u32[]{:S(2)}, u32[]{:S(2)}) collective-permute-start(f32[512,128]{1,0:T(8,128)S(1)} %shard_map.110.refs_4_.refs_0_.refs_8_), channel_id=1, source_target_pairs={{0,1},{1,0},{2,3},{3,2},{4,5},{5,4},{6,7},{7,6},{8,9},{9,8},{10,11... | collective-permute-start | bytes 786440 | tf_op jit(solution)/shard_map/ppermute | solution.py:21
  30.8 8.9 %collective-permute-start.16 = (f32[512,128]{1,0:T(8,128)S(1)}, f32[512,128]{1,0:T(8,128)S(1)}, u32[]{:S(2)}, u32[]{:S(2)}) collective-permute-start(f32[512,128]{1,0:T(8,128)S(1)} %shard_map.110.refs_4_.refs_0_.refs_8_), channel_id=1, source_target_pairs={{0,8},{2,10},{4,12},{6,14},{8,0},{10,2},{12,4},{14,6},{16,24},{18,... | collective-permute-start | bytes 786440 | tf_op jit(solution)/shard_map/ppermute | solution.py:17
  31.1 2.8 %collective-permute-start.15 = (f32[128,256]{1,0:T(8,128)S(1)}, f32[128,256]{1,0:T(8,128)S(1)}, u32[]{:S(2)}, u32[]{:S(2)}) collective-permute-start(f32[128,256]{1,0:T(8,128)S(1)} %get-tuple-element.119), channel_id=1, source_target_pairs={{0,1},{1,0},{2,3},{3,2},{4,5},{5,4},{6,7},{7,6},{8,9},{9,8},{10,11... | collective-permute-start | bytes 393224 | tf_op jit(solution)/shard_map/ppermute | solution.py:21
  31.7 4.0 %copy-start.3 = (s32[1,512]{1,0:T(1,128)S(1)}, s32[1,512]{1,0:T(1,128)}, u32[]{:S(2)}) copy-start(s32[1,512]{1,0:T(1,128)} %map_ref.1) | copy-start | bytes 6148
  33.9 1.8 %collective-permute-start.13 = (f32[128,256]{1,0:T(8,128)S(1)}, f32[128,256]{1,0:T(8,128)S(1)}, u32[]{:S(2)}, u32[]{:S(2)}) collective-permute-start(f32[128,256]{1,0:T(8,128)S(1)} %get-tuple-element.132), channel_id=1, source_target_pairs={{0,1},{1,0},{2,3},{3,2},{4,5},{5,4},{6,7},{7,6},{8,9},{9,8},{10,11... | collective-permute-start | bytes 393224 | tf_op jit(solution)/shard_map/ppermute | solution.py:21
  34.0 11.8 %collective-permute-start.17 = (f32[128,512]{1,0:T(8,128)S(1)}, f32[128,512]{1,0:T(8,128)S(1)}, u32[]{:S(2)}, u32[]{:S(2)}) collective-permute-start(f32[128,512]{1,0:T(8,128)S(1)} %get-tuple-element.139), channel_id=1, source_target_pairs={{0,4},{2,6},{4,0},{6,2},{8,12},{10,14},{12,8},{14,10},{16,20},{18,... | collective-permute-start | bytes 786440 | tf_op jit(solution)/shard_map/ppermute | solution.py:17
  35.5 13.5 %collective-permute-start.18 = (f32[512,128]{1,0:T(8,128)S(1)}, f32[512,128]{1,0:T(8,128)S(1)}, u32[]{:S(2)}, u32[]{:S(2)}) collective-permute-start(f32[512,128]{1,0:T(8,128)S(1)} %get-tuple-element.171.refs_0_), channel_id=1, source_target_pairs={{0,1},{1,0},{2,3},{3,2},{4,5},{5,4},{6,7},{7,6},{8,9},{9,8},{10,11... | collective-permute-start | bytes 786440 | tf_op jit(solution)/shard_map/ppermute | solution.py:21
  37.0 28.6 %collective-permute-start.21 = (f32[2,4,32,256]{3,2,1,0:T(8,128)S(1)}, f32[2,4,32,256]{3,2,1,0:T(8,128)S(1)}, u32[]{:S(2)}, u32[]{:S(2)}) collective-permute-start(f32[2,4,32,256]{3,2,1,0:T(8,128)S(1)} %get-tuple-element.136), channel_id=1, source_target_pairs={{0,24},{2,26},{4,28},{6,30},{8,16},{10,18},{12,20},{14,22},{16,8},... | collective-permute-start | bytes 786440 | tf_op jit(solution)/shard_map/ppermute | solution.py:327
  42.7 12.0 %collective-permute-start.19 = (f32[2,4,32,256]{3,2,1,0:T(8,128)S(1)}, f32[2,4,32,256]{3,2,1,0:T(8,128)S(1)}, u32[]{:S(2)}, u32[]{:S(2)}) collective-permute-start(f32[2,4,32,256]{3,2,1,0:T(8,128)S(1)} %get-tuple-element.151), channel_id=1, source_target_pairs={{0,8},{2,10},{4,12},{6,14},{8,0},{10,2},{12,4},{14,6},{16,24},{18,... | collective-permute-start | bytes 786440 | tf_op jit(solution)/shard_map/ppermute | solution.py:327
  46.5 15.7 %collective-permute-start.20 = (f32[2,4,32,256]{3,2,1,0:T(8,128)S(1)}, f32[2,4,32,256]{3,2,1,0:T(8,128)S(1)}, u32[]{:S(2)}, u32[]{:S(2)}) collective-permute-start(f32[2,4,32,256]{3,2,1,0:T(8,128)S(1)} %get-tuple-element.152), channel_id=1, source_target_pairs={{0,16},{2,18},{4,20},{6,22},{8,24},{10,26},{12,28},{14,30},{16,0},... | collective-permute-start | bytes 786440 | tf_op jit(solution)/shard_map/ppermute | solution.py:327
  50.3 16.5 %collective-permute-start.22 = (f32[2,4,32,256]{3,2,1,0:T(8,128)S(1)}, f32[2,4,32,256]{3,2,1,0:T(8,128)S(1)}, u32[]{:S(2)}, u32[]{:S(2)}) collective-permute-start(f32[2,4,32,256]{3,2,1,0:T(8,128)S(1)} %get-tuple-element.157), channel_id=1, source_target_pairs={{0,2},{2,0},{4,6},{6,4},{8,10},{10,8},{12,14},{14,12},{16,18},{18,... | collective-permute-start | bytes 786440 | tf_op jit(solution)/shard_map/ppermute | solution.py:327
  51.8 15.8 %collective-permute-start.23 = (f32[2,4,32,256]{3,2,1,0:T(8,128)S(1)}, f32[2,4,32,256]{3,2,1,0:T(8,128)S(1)}, u32[]{:S(2)}, u32[]{:S(2)}) collective-permute-start(f32[2,4,32,256]{3,2,1,0:T(8,128)S(1)} %get-tuple-element.158), channel_id=1, source_target_pairs={{0,4},{2,6},{4,0},{6,2},{8,12},{10,14},{12,8},{14,10},{16,20},{18,... | collective-permute-start | bytes 786440 | tf_op jit(solution)/shard_map/ppermute | solution.py:327
  54.7 14.6 %collective-permute-start.24 = (f32[2,4,32,256]{3,2,1,0:T(8,128)S(1)}, f32[2,4,32,256]{3,2,1,0:T(8,128)S(1)}, u32[]{:S(2)}, u32[]{:S(2)}) collective-permute-start(f32[2,4,32,256]{3,2,1,0:T(8,128)S(1)} %get-tuple-element.146), channel_id=1, source_target_pairs={{0,6},{2,4},{4,2},{6,0},{8,14},{10,12},{12,10},{14,8},{16,22},{18,... | collective-permute-start | bytes 786440 | tf_op jit(solution)/shard_map/ppermute | solution.py:327
  62.2 13.0 %collective-permute-start.25 = (f32[512,128]{1,0:T(8,128)S(1)}, f32[512,128]{1,0:T(8,128)S(1)}, u32[]{:S(2)}, u32[]{:S(2)}) collective-permute-start(f32[512,128]{1,0:T(8,128)S(1)} %shard_map.115.refs_4_.refs_0_.refs_12_), channel_id=1, source_target_pairs={{0,16},{2,18},{4,20},{6,22},{8,24},{10,26},{12,28},{14,30},{16,0},... | collective-permute-start | bytes 786440 | tf_op jit(solution)/shard_map/ppermute | solution.py:17
  65.7 13.0 %collective-permute-start.26 = (f32[2,4,32,256]{3,2,1,0:T(8,128)S(1)}, f32[2,4,32,256]{3,2,1,0:T(8,128)S(1)}, u32[]{:S(2)}, u32[]{:S(2)}) collective-permute-start(f32[2,4,32,256]{3,2,1,0:T(8,128)S(1)} %get-tuple-element.165), channel_id=1, source_target_pairs={{0,2},{2,0},{4,6},{6,4},{8,10},{10,8},{12,14},{14,12},{16,18},{18,... | collective-permute-start | bytes 786440 | tf_op jit(solution)/shard_map/ppermute | solution.py:327
  66.8 11.9 %collective-permute-start.27 = (f32[2,4,32,256]{3,2,1,0:T(8,128)S(1)}, f32[2,4,32,256]{3,2,1,0:T(8,128)S(1)}, u32[]{:S(2)}, u32[]{:S(2)}) collective-permute-start(f32[2,4,32,256]{3,2,1,0:T(8,128)S(1)} %get-tuple-element.166), channel_id=1, source_target_pairs={{0,4},{2,6},{4,0},{6,2},{8,12},{10,14},{12,8},{14,10},{16,20},{18,... | collective-permute-start | bytes 786440 | tf_op jit(solution)/shard_map/ppermute | solution.py:327
  67.6 15.8 %collective-permute-start.28 = (f32[2,4,32,256]{3,2,1,0:T(8,128)S(1)}, f32[2,4,32,256]{3,2,1,0:T(8,128)S(1)}, u32[]{:S(2)}, u32[]{:S(2)}) collective-permute-start(f32[2,4,32,256]{3,2,1,0:T(8,128)S(1)} %get-tuple-element.155), channel_id=1, source_target_pairs={{0,6},{2,4},{4,2},{6,0},{8,14},{10,12},{12,10},{14,8},{16,22},{18,... | collective-permute-start | bytes 786440 | tf_op jit(solution)/shard_map/ppermute | solution.py:327
  69.3 15.3 %collective-permute-start.29 = (f32[128,512]{1,0:T(8,128)S(1)}, f32[128,512]{1,0:T(8,128)S(1)}, u32[]{:S(2)}, u32[]{:S(2)}) collective-permute-start(f32[128,512]{1,0:T(8,128)S(1)} %get-tuple-element.168), channel_id=1, source_target_pairs={{0,2},{2,0},{4,6},{6,4},{8,10},{10,8},{12,14},{14,12},{16,18},{18,... | collective-permute-start | bytes 786440 | tf_op jit(solution)/shard_map/ppermute | solution.py:17
  75.2 14.8 %collective-permute-start.30 = (f32[2,4,32,256]{3,2,1,0:T(8,128)S(1)}, f32[2,4,32,256]{3,2,1,0:T(8,128)S(1)}, u32[]{:S(2)}, u32[]{:S(2)}) collective-permute-start(f32[2,4,32,256]{3,2,1,0:T(8,128)S(1)} %get-tuple-element.179), channel_id=1, source_target_pairs={{0,8},{2,10},{4,12},{6,14},{8,0},{10,2},{12,4},{14,6},{16,24},{18,... | collective-permute-start | bytes 786440 | tf_op jit(solution)/shard_map/ppermute | solution.py:327
  78.7 18.0 %collective-permute-start.31 = (f32[2,4,32,256]{3,2,1,0:T(8,128)S(1)}, f32[2,4,32,256]{3,2,1,0:T(8,128)S(1)}, u32[]{:S(2)}, u32[]{:S(2)}) collective-permute-start(f32[2,4,32,256]{3,2,1,0:T(8,128)S(1)} %get-tuple-element.180), channel_id=1, source_target_pairs={{0,16},{2,18},{4,20},{6,22},{8,24},{10,26},{12,28},{14,30},{16,0},... | collective-permute-start | bytes 786440 | tf_op jit(solution)/shard_map/ppermute | solution.py:327
  78.7 24.6 %collective-permute-start.32 = (f32[2,4,32,256]{3,2,1,0:T(8,128)S(1)}, f32[2,4,32,256]{3,2,1,0:T(8,128)S(1)}, u32[]{:S(2)}, u32[]{:S(2)}) collective-permute-start(f32[2,4,32,256]{3,2,1,0:T(8,128)S(1)} %get-tuple-element.159), channel_id=1, source_target_pairs={{0,24},{2,26},{4,28},{6,30},{8,16},{10,18},{12,20},{14,22},{16,8},... | collective-permute-start | bytes 786440 | tf_op jit(solution)/shard_map/ppermute | solution.py:327

commit v3 on v2

--- a/solution.py
+++ b/solution.py
@@ -407,8 +407,11 @@
         [shape(levels, h, k), shape(levels, h, k)],
     )
     top_update, = run(join_kernel, [u["um"], both(u["us"])], [shape(h, k)])
-    plan = [(f, (i, m), lv, m + NEAR * f) for m in nears for f in fars for i, lv in enumerate(late)]
-    element_grad = place(run, late_in, plan, out, element_grad)
+    for part in (fars[: len(fars) // 2], fars[len(fars) // 2 :]):
+        plan = [
+            (f - part[0], (i, m), lv, m + NEAR * f) for m in nears for f in part for i, lv in enumerate(late)
+        ]
+        element_grad = place(run, [late_in[f] for f in part], plan, out, element_grad)
     return solved, top_update, grads, element_grad
 
 

time: 105 us -> 105 us (level)
    pallas_call x2 -> x3, Pallas kernels: 2.45 us -> 3.06 us  [place(): pl.pallas_call(functools.partial(place_kernel, plan), out_shape=out, in_s...]
  transfers between devices with their start and end apart: 33 -> 33, of which waited for: 11 -> 11; matrix products, arithmetic and copies ran while one was open for 0% -> 0% of each run, Pallas kernels for 21% -> 22%
where the time goes in v3:
time: 105 us; the launch traced here: 104 us
  waiting for transfers between devices  37.9 us (36%)
  starting transfers between devices  33.3 us (32%)
  Pallas kernels  23.7 us (23%)
  blocking collectives  8.31 us (8%)
  between operations  1.08 us (1%)
    pallas_call x25, Pallas kernels, __call__(): pl.pallas_call(kernel, out_shape=tuple(outs), in_specs=[pl.BlockSpec(memo...  20.7 us
    ppermute x12, waiting for transfers between devices, exchange(): lax.ppermute(v, 'cube', [(i, i ^ j * step) for i in range(n)])  19.8 us
    ppermute x12, starting transfers between devices, exchange(): lax.ppermute(v, 'cube', [(i, i ^ j * step) for i in range(n)])  17.4 us
    ppermute x8, starting transfers between devices, partner(): lax.ppermute(x, 'cube', [(i, i ^ 1 << distance) for i in range(lax.axis_s...  13.4 us
    ppermute x8, waiting for transfers between devices, partner(): lax.ppermute(x, 'cube', [(i, i ^ 1 << distance) for i in range(lax.axis_s...  10.1 us
    all_gather x4, blocking collectives, both(): return lax.all_gather(x, 'cores')  8.31 us
    ppermute x13, waiting for transfers between devices, swap(): return lax.ppermute(x, 'cores', [(0, 1), (1, 0)])  8.07 us
    pallas_call x3, Pallas kernels, place(): pl.pallas_call(functools.partial(place_kernel, plan), out_shape=out, in_s...  3.06 us
  transfers between devices with their start and end apart: 33, of which 11 were waited for; matrix products, arithmetic and copies ran while one was open for 0% of the time, Pallas kernels for 22%

profile of v3, /device:TPU:8, one launch (start us, length us, event | category | flops | bytes accessed | tf_op | source)
XLA Modules:
  0.0 104.4 jit_solution(7930166724379267015)
XLA Ops:
  0.7 0.5 collective-permute-start.4
  1.2 1.3 %shard_map.102 = (f32[256,512]{1,0:T(8,128)S(1)}, f32[256,512]{1,0:T(8,128)S(1)}) custom-call(f32[4,256,512]{2,1,0:T(8,128)} %refs_3_.1, f32[4,256,512]{2,1,0:T(8,128)} %refs_5_.1), custom_call_target="tpu_custom_call" | custom-call | tf_op jit(solution)/shard_map/pallas_call | solution.py:65
  2.7 0.5 collective-permute-start.1
  3.2 3.5 %collective-permute-done.2.refs_5_ = f32[256,256]{1,0:T(8,128)S(1)} collective-permute-done((f32[256,256]{1,0:T(8,128)S(1)}, f32[256,256]{1,0:T(8,128)S(1)}, u32[]{:S(2)}, u32[]{:S(2)}) %collective-permute-start.2) | collective-permute-done | bytes 262176 | tf_op jit(solution)/shard_map/ppermute | solution.py:21
  7.0 0.4 collective-permute-start.6
  7.5 1.0 shard_map.103
  8.5 1.6 %collective-permute-start.8 = (f32[512,128]{1,0:T(8,128)S(1)}, f32[512,128]{1,0:T(8,128)S(1)}, u32[]{:S(2)}, u32[]{:S(2)}) collective-permute-start(f32[512,128]{1,0:T(8,128)S(1)} %get-tuple-element.172.refs_0_), channel_id=1, source_target_pairs={{0,2},{2,0},{4,6},{6,4},{8,10},{10,8},{12,14},{14,12},{16,18},{18,... | collective-permute-start | bytes 786440 | tf_op jit(solution)/shard_map/ppermute | solution.py:17
  10.1 2.6 %collective-permute-start.9 = (f32[128,512]{1,0:T(8,128)S(1)}, f32[128,512]{1,0:T(8,128)S(1)}, u32[]{:S(2)}, u32[]{:S(2)}) collective-permute-start(f32[128,512]{1,0:T(8,128)S(1)} %get-tuple-element.115), channel_id=1, source_target_pairs={{0,16},{2,18},{4,20},{6,22},{8,24},{10,26},{12,28},{14,30},{16,0},... | collective-permute-start | bytes 786440 | tf_op jit(solution)/shard_map/ppermute | solution.py:17
  12.7 1.5 %collective-permute-done.6.refs_1_ = f32[4,256,512]{2,1,0:T(8,128)S(1)} collective-permute-done((f32[4,256,512]{2,1,0:T(8,128)}, f32[4,256,512]{2,1,0:T(8,128)S(1)}, u32[]{:S(2)}, u32[]{:S(2)}) %collective-permute-start.6) | collective-permute-done | bytes 2097184 | tf_op jit(solution)/shard_map/ppermute | solution.py:21
  14.2 3.0 %collective-permute-done.7.refs_2_ = f32[4,256,512]{2,1,0:T(8,128)S(1)} collective-permute-done((f32[4,256,512]{2,1,0:T(8,128)}, f32[4,256,512]{2,1,0:T(8,128)S(1)}, u32[]{:S(2)}, u32[]{:S(2)}) %collective-permute-start.7) | collective-permute-done | bytes 2097184 | tf_op jit(solution)/shard_map/ppermute | solution.py:21
  17.2 3.0 %shard_map.104 = (bf16[512,512]{1,0:T(8,128)(2,1)S(1)}, bf16[512,512]{1,0:T(8,128)(2,1)S(1)}, bf16[512,512]{1,0:T(8,128)(2,1)S(1)}, bf16[512,512]{1,0:T(8,128)(2...) custom-call(f32[4,256,512]{2,1,0:T(8,128)S(1)} %collective-permute-d, ...), custom_call_target="tpu_custom_call" | custom-call | tf_op jit(solution)/shard_map/pallas_call | solution.py:65
  20.2 0.4 shard_map.105.refs_0_
  20.7 0.8 shard_map.106.refs_0_.refs_4_
  21.5 1.6 %collective-permute-start.10 = (f32[512,128]{1,0:T(8,128)S(1)}, f32[512,128]{1,0:T(8,128)S(1)}, u32[]{:S(2)}, u32[]{:S(2)}) collective-permute-start(f32[512,128]{1,0:T(8,128)S(1)} %shard_map.106.refs_0_.refs_4_), channel_id=1, source_target_pairs={{0,4},{2,6},{4,0},{6,2},{8,12},{10,14},{12,8},{14,10},{16,20},{18,... | collective-permute-start | bytes 786440 | tf_op jit(solution)/shard_map/ppermute | solution.py:17
  23.1 0.4 shard_map.107.refs_0_
  23.5 0.5 collective-permute-done.9.refs_1_
  24.0 0.8 shard_map.108
  24.8 1.4 %collective-permute-start.11 = (f32[128,512]{1,0:T(8,128)S(1)}, f32[128,512]{1,0:T(8,128)S(1)}, u32[]{:S(2)}, u32[]{:S(2)}) collective-permute-start(f32[128,512]{1,0:T(8,128)S(1)} %get-tuple-element.131), channel_id=1, source_target_pairs={{0,8},{2,10},{4,12},{6,14},{8,0},{10,2},{12,4},{14,6},{16,24},{18,... | collective-permute-start | bytes 786440 | tf_op jit(solution)/shard_map/ppermute | solution.py:17
  26.2 0.4 shard_map.109.refs_0_
  26.7 3.3 %collective-permute-done.10.refs_1_ = f32[512,128]{1,0:T(8,128)S(1)} collective-permute-done((f32[512,128]{1,0:T(8,128)S(1)}, f32[512,128]{1,0:T(8,128)S(1)}, u32[]{:S(2)}, u32[]{:S(2)}) %collective-permute-start.10) | collective-permute-done | bytes 262176 | tf_op jit(solution)/shard_map/ppermute | solution.py:17
  29.9 0.8 shard_map.110.refs_4_.refs_0_.refs_8_
  30.8 0.3 collective-permute-start.16
  31.1 0.2 collective-permute-start.15
  31.3 0.4 shard_map.111.refs_0_
  31.7 1.4 %collective-permute-done.11.refs_1_ = f32[128,512]{1,0:T(8,128)S(1)} collective-permute-done((f32[128,512]{1,0:T(8,128)S(1)}, f32[128,512]{1,0:T(8,128)S(1)}, u32[]{:S(2)}, u32[]{:S(2)}) %collective-permute-start.11) | collective-permute-done | bytes 262176 | tf_op jit(solution)/shard_map/ppermute | solution.py:17
  33.1 0.8 shard_map.112
  34.0 1.6 %collective-permute-start.17 = (f32[128,512]{1,0:T(8,128)S(1)}, f32[128,512]{1,0:T(8,128)S(1)}, u32[]{:S(2)}, u32[]{:S(2)}) collective-permute-start(f32[128,512]{1,0:T(8,128)S(1)} %get-tuple-element.140), channel_id=1, source_target_pairs={{0,4},{2,6},{4,0},{6,2},{8,12},{10,14},{12,8},{14,10},{16,20},{18,... | collective-permute-start | bytes 786440 | tf_op jit(solution)/shard_map/ppermute | solution.py:17
  35.7 1.3 %shard_map.113 = (f32[2,4,32,256]{3,2,1,0:T(8,128)S(1)}, f32[2,4,32,256]{3,2,1,0:T(8,128)S(1)}, f32[2,4,32,256]{3,2,1,0:T(8,128)S(1)}, f32[2,4,32,256]{3,2,1,0:T(8,128)S(1)}) custom-call(s32[1,512]{1,0:T(1,128)S(1)} %copy-done.3, f32[512,128]{1,0:T(8,128)S(1)} %shard_map.106.refs_0_.refs_4_, f32[512,128]{1,0:T(8,128)S(1)} %collective-permute-done.12.refs_1_.refs_5_, ...), custom_call_target="tpu_custom_call" | custom-call | tf_op jit(solution)/shard_map/pallas_call | solution.py:65
  37.0 2.3 %collective-permute-start.21 = (f32[2,4,32,256]{3,2,1,0:T(8,128)S(1)}, f32[2,4,32,256]{3,2,1,0:T(8,128)S(1)}, u32[]{:S(2)}, u32[]{:S(2)}) collective-permute-start(f32[2,4,32,256]{3,2,1,0:T(8,128)S(1)} %get-tuple-element.137), channel_id=1, source_target_pairs={{0,24},{2,26},{4,28},{6,30},{8,16},{10,18},{12,20},{14,22},{16,8},... | collective-permute-start | bytes 786440 | tf_op jit(solution)/shard_map/ppermute | solution.py:327
  39.3 0.4 shard_map.114.refs_0_
  39.7 2.7 %collective-permute-start.19 = (f32[2,4,32,256]{3,2,1,0:T(8,128)S(1)}, f32[2,4,32,256]{3,2,1,0:T(8,128)S(1)}, u32[]{:S(2)}, u32[]{:S(2)}) collective-permute-start(f32[2,4,32,256]{3,2,1,0:T(8,128)S(1)} %get-tuple-element.152), channel_id=1, source_target_pairs={{0,8},{2,10},{4,12},{6,14},{8,0},{10,2},{12,4},{14,6},{16,24},{18,... | collective-permute-start | bytes 786440 | tf_op jit(solution)/shard_map/ppermute | solution.py:327
  42.4 0.8 shard_map.115.refs_4_.refs_0_.refs_12_
  43.2 2.2 %all-gather.1 = f32[1024,128]{1,0:T(8,128)S(1)} all-gather(f32[512,128]{1,0:T(8,128)S(1)} %shard_map.115.refs_4_.refs_0_.refs_12_), channel_id=3, replica_groups=mesh['cube'=16,'cores'=2] {'cores'}, dimensions={0}, use_global_device_ids=true | all-gather | bytes 786432 | tf_op jit(solution)/shard_map/all_gather | solution.py:25
  45.4 0.4 shard_map.116.refs_0_
  45.8 0.8 shard_map.117
  46.6 0.3 collective-permute-start.20
  46.9 2.2 %all-gather = f32[256,256]{1,0:T(8,128)S(1)} all-gather(f32[128,256]{1,0:T(8,128)S(1)} %get-tuple-element.142), channel_id=2, replica_groups=mesh['cube'=16,'cores'=2] {'cores'}, dimensions={0}, use_global_device_ids=true | all-gather | bytes 393216 | tf_op jit(solution)/shard_map/all_gather | solution.py:25
  49.0 1.3 %shard_map.118 = (f32[2,4,32,256]{3,2,1,0:T(8,128)S(1)}, f32[2,4,32,256]{3,2,1,0:T(8,128)S(1)}, f32[2,4,32,256]{3,2,1,0:T(8,128)S(1)}, f32[2,4,32,256]{3,2,1,0:T(8,128)S(1)}) custom-call(s32[1,512]{1,0:T(1,128)S(1)} %copy-done.3, f32[512,128]{1,0:T(8,128)S(1)} %get-tuple-element.172.refs_0_, f32[512,128]{1,0:T(8,128)S(1)} %collective-permute-done.18.refs_1_, ...), custom_call_target="tpu_custom_call" | custom-call | tf_op jit(solution)/shard_map/pallas_call | solution.py:65
  50.3 1.0 collective-permute-start.22
  51.3 1.5 %collective-permute-start.23 = (f32[2,4,32,256]{3,2,1,0:T(8,128)S(1)}, f32[2,4,32,256]{3,2,1,0:T(8,128)S(1)}, u32[]{:S(2)}, u32[]{:S(2)}) collective-permute-start(f32[2,4,32,256]{3,2,1,0:T(8,128)S(1)} %get-tuple-element.159), channel_id=1, source_target_pairs={{0,4},{2,6},{4,0},{6,2},{8,12},{10,14},{12,8},{14,10},{16,20},{18,... | collective-permute-start | bytes 786440 | tf_op jit(solution)/shard_map/ppermute | solution.py:327
  52.8 1.8 %collective-permute-done.19.refs_1_ = f32[2,4,32,256]{3,2,1,0:T(8,128)S(1)} collective-permute-done((f32[2,4,32,256]{3,2,1,0:T(8,128)S(1)}, f32[2,4,32,256]{3,2,1,0:T(8,128)S(1)}, u32[]{:S(2)}, u32[]{:S(2)}) %collective-permute-start.19) | collective-permute-done | bytes 262176 | tf_op jit(solution)/shard_map/ppermute | solution.py:327
  54.7 1.1 %collective-permute-start.24 = (f32[2,4,32,256]{3,2,1,0:T(8,128)S(1)}, f32[2,4,32,256]{3,2,1,0:T(8,128)S(1)}, u32[]{:S(2)}, u32[]{:S(2)}) collective-permute-start(f32[2,4,32,256]{3,2,1,0:T(8,128)S(1)} %get-tuple-element.147), channel_id=1, source_target_pairs={{0,6},{2,4},{4,2},{6,0},{8,14},{10,12},{12,10},{14,8},{16,22},{18,... | collective-permute-start | bytes 786440 | tf_op jit(solution)/shard_map/ppermute | solution.py:327
  55.7 0.4 shard_map.119.refs_0_
  56.2 0.4 shard_map.120.refs_0_
  56.6 5.7 %collective-permute-done.20.refs_2_ = f32[2,4,32,256]{3,2,1,0:T(8,128)S(1)} collective-permute-done((f32[2,4,32,256]{3,2,1,0:T(8,128)S(1)}, f32[2,4,32,256]{3,2,1,0:T(8,128)S(1)}, u32[]{:S(2)}, u32[]{:S(2)}) %collective-permute-start.20) | collective-permute-done | bytes 262176 | tf_op jit(solution)/shard_map/ppermute | solution.py:327
  62.2 3.4 %collective-permute-start.25 = (f32[512,128]{1,0:T(8,128)S(1)}, f32[512,128]{1,0:T(8,128)S(1)}, u32[]{:S(2)}, u32[]{:S(2)}) collective-permute-start(f32[512,128]{1,0:T(8,128)S(1)} %shard_map.115.refs_4_.refs_0_.refs_12_), channel_id=1, source_target_pairs={{0,16},{2,18},{4,20},{6,22},{8,24},{10,26},{12,28},{14,30},{16,0},... | collective-permute-start | bytes 786440 | tf_op jit(solution)/shard_map/ppermute | solution.py:17
  65.7 1.1 %collective-permute-start.26 = (f32[2,4,32,256]{3,2,1,0:T(8,128)S(1)}, f32[2,4,32,256]{3,2,1,0:T(8,128)S(1)}, u32[]{:S(2)}, u32[]{:S(2)}) collective-permute-start(f32[2,4,32,256]{3,2,1,0:T(8,128)S(1)} %get-tuple-element.166), channel_id=1, source_target_pairs={{0,2},{2,0},{4,6},{6,4},{8,10},{10,8},{12,14},{14,12},{16,18},{18,... | collective-permute-start | bytes 786440 | tf_op jit(solution)/shard_map/ppermute | solution.py:327
  66.8 0.8 collective-permute-start.27
  67.6 1.6 %collective-permute-start.28 = (f32[2,4,32,256]{3,2,1,0:T(8,128)S(1)}, f32[2,4,32,256]{3,2,1,0:T(8,128)S(1)}, u32[]{:S(2)}, u32[]{:S(2)}) collective-permute-start(f32[2,4,32,256]{3,2,1,0:T(8,128)S(1)} %get-tuple-element.156), channel_id=1, source_target_pairs={{0,6},{2,4},{4,2},{6,0},{8,14},{10,12},{12,10},{14,8},{16,22},{18,... | collective-permute-start | bytes 786440 | tf_op jit(solution)/shard_map/ppermute | solution.py:327
  69.3 1.0 collective-permute-start.29
  70.3 4.9 %collective-permute-done.25.refs_1_ = f32[512,128]{1,0:T(8,128)S(1)} collective-permute-done((f32[512,128]{1,0:T(8,128)S(1)}, f32[512,128]{1,0:T(8,128)S(1)}, u32[]{:S(2)}, u32[]{:S(2)}) %collective-permute-start.25) | collective-permute-done | bytes 262176 | tf_op jit(solution)/shard_map/ppermute | solution.py:17
  75.2 3.5 %collective-permute-start.31 = (f32[2,4,32,256]{3,2,1,0:T(8,128)S(1)}, f32[2,4,32,256]{3,2,1,0:T(8,128)S(1)}, u32[]{:S(2)}, u32[]{:S(2)}) collective-permute-start(f32[2,4,32,256]{3,2,1,0:T(8,128)S(1)} %get-tuple-element.181), channel_id=1, source_target_pairs={{0,8},{2,10},{4,12},{6,14},{8,0},{10,2},{12,4},{14,6},{16,24},{18,... | collective-permute-start | bytes 786440 | tf_op jit(solution)/shard_map/ppermute | solution.py:327
  78.7 1.5 %collective-permute-start.32 = (f32[2,4,32,256]{3,2,1,0:T(8,128)S(1)}, f32[2,4,32,256]{3,2,1,0:T(8,128)S(1)}, u32[]{:S(2)}, u32[]{:S(2)}) collective-permute-start(f32[2,4,32,256]{3,2,1,0:T(8,128)S(1)} %get-tuple-element.160), channel_id=1, source_target_pairs={{0,24},{2,26},{4,28},{6,30},{8,16},{10,18},{12,20},{14,22},{16,8},... | collective-permute-start | bytes 786440 | tf_op jit(solution)/shard_map/ppermute | solution.py:327
  80.2 1.2 %shard_map.123 = (f32[512,128]{1,0:T(8,128)}, f32[256,128]{1,0:T(8,128)S(1)}, f32[256,128]{1,0:T(8,128)S(1)}) custom-call(f32[512,128]{1,0:T(8,128)S(1)} %shard_map.119.refs_0_, f32[512,128]{1,0:T(8,128)S(1)} %collective-permute-done.25.refs_1_, bf16[512,512]{1,0:T(8,128)(2,1)S(1)} %get-tuple-element.162.refs_2_, bf16[512,512]{1,0:T(8,128)(2,1)S(1)} %get-tuple-element.163.refs_3_), custom_call_target="tpu_custom_call" | custom-call | tf_op jit(solution)/shard_map/pallas_call | solution.py:65
  81.4 2.0 %all-gather.3 = f32[512,128]{1,0:T(8,128)S(1)} all-gather(f32[256,128]{1,0:T(8,128)S(1)} %get-tuple-element.164), channel_id=5, replica_groups=mesh['cube'=16,'cores'=2] {'cores'}, dimensions={0}, use_global_device_ids=true | all-gather | bytes 393216 | tf_op jit(solution)/shard_map/all_gather | solution.py:25
  83.4 1.2 %shard_map.124.refs_2_ = f32[4,32,4096]{2,1,0:T(8,128)} custom-call(f32[2,4,32,256]{3,2,1,0:T(8,128)S(1)} %get-tuple-element.165.refs_0_, f32[2,4,32,256]{3,2,1,0:T(8,128)S(1)} %collective-permute-done.26.refs_1_, f32[2,4,32,256]{3,2,1,0:T(8,128)S(1)} %collective-permute-done.27.refs_2_, f32[2,4,32,256]{3,2,1,0:T(8,128)S(1)} %collective-permute-done.28.refs_3_), custom_call_target="tpu_custom_call" | custom-call | tf_op jit(solution)/shard_map/pallas_call | solution.py:265
  84.6 1.1 %shard_map.125 = (f32[128,512]{1,0:T(8,128)}, f32[128,256]{1,0:T(8,128)S(1)}, f32[128,256]{1,0:T(8,128)S(1)}) custom-call(f32[128,512]{1,0:T(8,128)S(1)} %shard_map.120.refs_0_, f32[128,512]{1,0:T(8,128)S(1)} %collective-permute-done.29.refs_1_, bf16[512,512]{1,0:T(8,128)(2,1)S(1)} %get-tuple-element.170.refs_2_, bf16[512,512]{1,0:T(8,128)(2,1)S(1)} %get-tuple-element.99.refs_3_), custom_call_target="tpu_custom_call" | custom-call | tf_op jit(solution)/shard_map/pallas_call | solution.py:65
  85.7 2.0 %all-gather.2 = f32[256,256]{1,0:T(8,128)S(1)} all-gather(f32[128,256]{1,0:T(8,128)S(1)} %get-tuple-element.171), channel_id=4, replica_groups=mesh['cube'=16,'cores'=2] {'cores'}, dimensions={0}, use_global_device_ids=true | all-gather | bytes 393216 | tf_op jit(solution)/shard_map/all_gather | solution.py:25
  87.7 1.6 %shard_map.126 = (f32[4,256,256]{2,1,0:T(8,128)}, f32[4,256,256]{2,1,0:T(8,128)}) custom-call(f32[512,128]{1,0:T(8,128)S(1)} %get-tuple-element.172.refs_0_, f32[512,128]{1,0:T(8,128)S(1)} %collective-permute-done.18.refs_1_, f32[128,256]{1,0:T(8,128)S(1)} %get-tuple-element.173.refs_2_, f32[2,128,256]{2,1,0:T(8,128)S(1)} %bitcast.8, ...), custom_call_target="tpu_custom_call" | custom-call | tf_op jit(solution)/shard_map/pallas_call | solution.py:65
  89.3 0.7 shard_map.127
  90.1 0.9 shard_map.128.refs_2_
  91.0 5.7 %collective-permute-done.30.refs_0_ = f32[2,4,32,256]{3,2,1,0:T(8,128)S(1)} collective-permute-done((f32[2,4,32,256]{3,2,1,0:T(8,128)S(1)}, f32[2,4,32,256]{3,2,1,0:T(8,128)S(1)}, u32[]{:S(2)}, u32[]{:S(2)}) %collective-permute-start.30) | collective-permute-done | bytes 262176 | tf_op jit(solution)/shard_map/ppermute | solution.py:327
  96.7 6.6 %collective-permute-done.32.refs_1_ = f32[2,4,32,256]{3,2,1,0:T(8,128)S(1)} collective-permute-done((f32[2,4,32,256]{3,2,1,0:T(8,128)S(1)}, f32[2,4,32,256]{3,2,1,0:T(8,128)S(1)}, u32[]{:S(2)}, u32[]{:S(2)}) %collective-permute-start.32) | collective-permute-done | bytes 262176 | tf_op jit(solution)/shard_map/ppermute | solution.py:327
  103.3 0.9 shard_map.129
  (44 shorter events, 1.1 us)
Async XLA Ops:
  0.6 6.9 %copy-start.1 = (f32[4,256,256]{2,1,0:T(8,128)S(1)}, f32[4,256,256]{2,1,0:T(8,128)}, u32[]{:S(2)}) copy-start(f32[4,256,256]{2,1,0:T(8,128)} %refs_6_.1) | copy-start | bytes 3145732
  0.6 6.1 %copy-start.4 = (f32[4,256,512]{2,1,0:T(8,128)S(1)}, f32[4,256,512]{2,1,0:T(8,128)}, u32[]{:S(2)}) copy-start(f32[4,256,512]{2,1,0:T(8,128)} %refs_3_.1) | copy-start | bytes 6291460
  0.7 2.5 %copy-start.2 = (f32[256,256]{1,0:T(8,128)S(1)}, f32[256,256]{1,0:T(8,128)}, u32[]{:S(2)}) copy-start(f32[256,256]{1,0:T(8,128)} %refs_4_.2) | copy-start | bytes 786436
  0.7 6.1 %collective-permute-start.3 = (f32[4,256,256]{2,1,0:T(8,128)}, f32[4,256,256]{2,1,0:T(8,128)S(1)}, u32[]{:S(2)}, u32[]{:S(2)}) collective-permute-start(f32[4,256,256]{2,1,0:T(8,128)} %refs_6_.1), channel_id=1, source_target_pairs={{0,1},{1,0},{2,3},{3,2},{4,5},{5,4},{6,7},{7,6},{8,9},{9,8},{10,11... | collective-permute-start | bytes 3145736 | tf_op jit(solution)/shard_map/ppermute | solution.py:21
  0.7 6.0 %collective-permute-start.4 = (f32[4,256,256]{2,1,0:T(8,128)}, f32[4,256,256]{2,1,0:T(8,128)S(1)}, u32[]{:S(2)}, u32[]{:S(2)}) collective-permute-start(f32[4,256,256]{2,1,0:T(8,128)} %refs_1_.7), channel_id=1, source_target_pairs={{0,1},{1,0},{2,3},{3,2},{4,5},{5,4},{6,7},{7,6},{8,9},{9,8},{10,11... | collective-permute-start | bytes 3145736 | tf_op jit(solution)/shard_map/ppermute | solution.py:21
  2.6 4.2 %collective-permute-start = (f32[256,512]{1,0:T(8,128)S(1)}, f32[256,512]{1,0:T(8,128)S(1)}, u32[]{:S(2)}, u32[]{:S(2)}) collective-permute-start(f32[256,512]{1,0:T(8,128)S(1)} %get-tuple-element.94.refs_0_), channel_id=1, source_target_pairs={{0,1},{1,0},{2,3},{3,2},{4,5},{5,4},{6,7},{7,6},{8,9},{9,8},{10,11... | collective-permute-start | bytes 1572872 | tf_op jit(solution)/shard_map/ppermute | solution.py:21
  2.7 4.1 %collective-permute-start.1 = (f32[256,512]{1,0:T(8,128)S(1)}, f32[256,512]{1,0:T(8,128)S(1)}, u32[]{:S(2)}, u32[]{:S(2)}) collective-permute-start(f32[256,512]{1,0:T(8,128)S(1)} %get-tuple-element.95.refs_2_), channel_id=1, source_target_pairs={{0,1},{1,0},{2,3},{3,2},{4,5},{5,4},{6,7},{7,6},{8,9},{9,8},{10,11... | collective-permute-start | bytes 1572872 | tf_op jit(solution)/shard_map/ppermute | solution.py:21
  3.2 3.6 %collective-permute-start.2 = (f32[256,256]{1,0:T(8,128)S(1)}, f32[256,256]{1,0:T(8,128)S(1)}, u32[]{:S(2)}, u32[]{:S(2)}) collective-permute-start(f32[256,256]{1,0:T(8,128)S(1)} %copy-done.2), channel_id=1, source_target_pairs={{0,1},{1,0},{2,3},{3,2},{4,5},{5,4},{6,7},{7,6},{8,9},{9,8},{10,11... | collective-permute-start | bytes 786440 | tf_op jit(solution)/shard_map/ppermute | solution.py:21
  6.8 5.9 %collective-permute-start.5 = (f32[4,256,512]{2,1,0:T(8,128)S(1)}, f32[4,256,512]{2,1,0:T(8,128)S(1)}, u32[]{:S(2)}, u32[]{:S(2)}) collective-permute-start(f32[4,256,512]{2,1,0:T(8,128)S(1)} %copy-done.4), channel_id=1, source_target_pairs={{0,1},{1,0},{2,3},{3,2},{4,5},{5,4},{6,7},{7,6},{8,9},{9,8},{10,11... | collective-permute-start | bytes 6291464 | tf_op jit(solution)/shard_map/ppermute | solution.py:21
  7.0 7.2 %collective-permute-start.6 = (f32[4,256,512]{2,1,0:T(8,128)}, f32[4,256,512]{2,1,0:T(8,128)S(1)}, u32[]{:S(2)}, u32[]{:S(2)}) collective-permute-start(f32[4,256,512]{2,1,0:T(8,128)} %refs_4_.3), channel_id=1, source_target_pairs={{0,1},{1,0},{2,3},{3,2},{4,5},{5,4},{6,7},{7,6},{8,9},{9,8},{10,11... | collective-permute-start | bytes 6291464 | tf_op jit(solution)/shard_map/ppermute | solution.py:21
  7.4 9.9 %collective-permute-start.7 = (f32[4,256,512]{2,1,0:T(8,128)}, f32[4,256,512]{2,1,0:T(8,128)S(1)}, u32[]{:S(2)}, u32[]{:S(2)}) collective-permute-start(f32[4,256,512]{2,1,0:T(8,128)} %refs_5_.1), channel_id=1, source_target_pairs={{0,1},{1,0},{2,3},{3,2},{4,5},{5,4},{6,7},{7,6},{8,9},{9,8},{10,11... | collective-permute-start | bytes 6291464 | tf_op jit(solution)/shard_map/ppermute | solution.py:21
  8.5 12.2 %collective-permute-start.8 = (f32[512,128]{1,0:T(8,128)S(1)}, f32[512,128]{1,0:T(8,128)S(1)}, u32[]{:S(2)}, u32[]{:S(2)}) collective-permute-start(f32[512,128]{1,0:T(8,128)S(1)} %get-tuple-element.172.refs_0_), channel_id=1, source_target_pairs={{0,2},{2,0},{4,6},{6,4},{8,10},{10,8},{12,14},{14,12},{16,18},{18,... | collective-permute-start | bytes 786440 | tf_op jit(solution)/shard_map/ppermute | solution.py:17
  10.1 13.9 %collective-permute-start.9 = (f32[128,512]{1,0:T(8,128)S(1)}, f32[128,512]{1,0:T(8,128)S(1)}, u32[]{:S(2)}, u32[]{:S(2)}) collective-permute-start(f32[128,512]{1,0:T(8,128)S(1)} %get-tuple-element.115), channel_id=1, source_target_pairs={{0,16},{2,18},{4,20},{6,22},{8,24},{10,26},{12,28},{14,30},{16,0},... | collective-permute-start | bytes 786440 | tf_op jit(solution)/shard_map/ppermute | solution.py:17
  20.7 2.4 %copy-start = (f32[4,256,256]{2,1,0:T(8,128)S(1)}, f32[4,256,256]{2,1,0:T(8,128)}, u32[]{:S(2)}) copy-start(f32[4,256,256]{2,1,0:T(8,128)} %refs_1_.7) | copy-start | bytes 3145732
  21.5 8.4 %collective-permute-start.10 = (f32[512,128]{1,0:T(8,128)S(1)}, f32[512,128]{1,0:T(8,128)S(1)}, u32[]{:S(2)}, u32[]{:S(2)}) collective-permute-start(f32[512,128]{1,0:T(8,128)S(1)} %shard_map.106.refs_0_.refs_4_), channel_id=1, source_target_pairs={{0,4},{2,6},{4,0},{6,2},{8,12},{10,14},{12,8},{14,10},{16,20},{18,... | collective-permute-start | bytes 786440 | tf_op jit(solution)/shard_map/ppermute | solution.py:17
  24.8 8.3 %collective-permute-start.11 = (f32[128,512]{1,0:T(8,128)S(1)}, f32[128,512]{1,0:T(8,128)S(1)}, u32[]{:S(2)}, u32[]{:S(2)}) collective-permute-start(f32[128,512]{1,0:T(8,128)S(1)} %get-tuple-element.131), channel_id=1, source_target_pairs={{0,8},{2,10},{4,12},{6,14},{8,0},{10,2},{12,4},{14,6},{16,24},{18,... | collective-permute-start | bytes 786440 | tf_op jit(solution)/shard_map/ppermute | solution.py:17
  26.2 9.3 %collective-permute-start.12 = (f32[512,128]{1,0:T(8,128)S(1)}, f32[512,128]{1,0:T(8,128)S(1)}, u32[]{:S(2)}, u32[]{:S(2)}) collective-permute-start(f32[512,128]{1,0:T(8,128)S(1)} %shard_map.106.refs_0_.refs_4_), channel_id=1, source_target_pairs={{0,1},{1,0},{2,3},{3,2},{4,5},{5,4},{6,7},{7,6},{8,9},{9,8},{10,11... | collective-permute-start | bytes 786440 | tf_op jit(solution)/shard_map/ppermute | solution.py:21
  30.7 5.0 %collective-permute-start.14 = (f32[512,128]{1,0:T(8,128)S(1)}, f32[512,128]{1,0:T(8,128)S(1)}, u32[]{:S(2)}, u32[]{:S(2)}) collective-permute-start(f32[512,128]{1,0:T(8,128)S(1)} %shard_map.110.refs_4_.refs_0_.refs_8_), channel_id=1, source_target_pairs={{0,1},{1,0},{2,3},{3,2},{4,5},{5,4},{6,7},{7,6},{8,9},{9,8},{10,11... | collective-permute-start | bytes 786440 | tf_op jit(solution)/shard_map/ppermute | solution.py:21
  30.8 11.6 %collective-permute-start.16 = (f32[512,128]{1,0:T(8,128)S(1)}, f32[512,128]{1,0:T(8,128)S(1)}, u32[]{:S(2)}, u32[]{:S(2)}) collective-permute-start(f32[512,128]{1,0:T(8,128)S(1)} %shard_map.110.refs_4_.refs_0_.refs_8_), channel_id=1, source_target_pairs={{0,8},{2,10},{4,12},{6,14},{8,0},{10,2},{12,4},{14,6},{16,24},{18,... | collective-permute-start | bytes 786440 | tf_op jit(solution)/shard_map/ppermute | solution.py:17
  31.1 2.8 %collective-permute-start.15 = (f32[128,256]{1,0:T(8,128)S(1)}, f32[128,256]{1,0:T(8,128)S(1)}, u32[]{:S(2)}, u32[]{:S(2)}) collective-permute-start(f32[128,256]{1,0:T(8,128)S(1)} %get-tuple-element.120), channel_id=1, source_target_pairs={{0,1},{1,0},{2,3},{3,2},{4,5},{5,4},{6,7},{7,6},{8,9},{9,8},{10,11... | collective-permute-start | bytes 393224 | tf_op jit(solution)/shard_map/ppermute | solution.py:21
  31.7 4.0 %copy-start.3 = (s32[1,512]{1,0:T(1,128)S(1)}, s32[1,512]{1,0:T(1,128)}, u32[]{:S(2)}) copy-start(s32[1,512]{1,0:T(1,128)} %map_ref.1) | copy-start | bytes 6148
  33.9 1.8 %collective-permute-start.13 = (f32[128,256]{1,0:T(8,128)S(1)}, f32[128,256]{1,0:T(8,128)S(1)}, u32[]{:S(2)}, u32[]{:S(2)}) collective-permute-start(f32[128,256]{1,0:T(8,128)S(1)} %get-tuple-element.133), channel_id=1, source_target_pairs={{0,1},{1,0},{2,3},{3,2},{4,5},{5,4},{6,7},{7,6},{8,9},{9,8},{10,11... | collective-permute-start | bytes 393224 | tf_op jit(solution)/shard_map/ppermute | solution.py:21
  34.0 11.8 %collective-permute-start.17 = (f32[128,512]{1,0:T(8,128)S(1)}, f32[128,512]{1,0:T(8,128)S(1)}, u32[]{:S(2)}, u32[]{:S(2)}) collective-permute-start(f32[128,512]{1,0:T(8,128)S(1)} %get-tuple-element.140), channel_id=1, source_target_pairs={{0,4},{2,6},{4,0},{6,2},{8,12},{10,14},{12,8},{14,10},{16,20},{18,... | collective-permute-start | bytes 786440 | tf_op jit(solution)/shard_map/ppermute | solution.py:17
  35.5 13.5 %collective-permute-start.18 = (f32[512,128]{1,0:T(8,128)S(1)}, f32[512,128]{1,0:T(8,128)S(1)}, u32[]{:S(2)}, u32[]{:S(2)}) collective-permute-start(f32[512,128]{1,0:T(8,128)S(1)} %get-tuple-element.172.refs_0_), channel_id=1, source_target_pairs={{0,1},{1,0},{2,3},{3,2},{4,5},{5,4},{6,7},{7,6},{8,9},{9,8},{10,11... | collective-permute-start | bytes 786440 | tf_op jit(solution)/shard_map/ppermute | solution.py:21
  37.0 28.6 %collective-permute-start.21 = (f32[2,4,32,256]{3,2,1,0:T(8,128)S(1)}, f32[2,4,32,256]{3,2,1,0:T(8,128)S(1)}, u32[]{:S(2)}, u32[]{:S(2)}) collective-permute-start(f32[2,4,32,256]{3,2,1,0:T(8,128)S(1)} %get-tuple-element.137), channel_id=1, source_target_pairs={{0,24},{2,26},{4,28},{6,30},{8,16},{10,18},{12,20},{14,22},{16,8},... | collective-permute-start | bytes 786440 | tf_op jit(solution)/shard_map/ppermute | solution.py:327
  39.7 15.0 %collective-permute-start.19 = (f32[2,4,32,256]{3,2,1,0:T(8,128)S(1)}, f32[2,4,32,256]{3,2,1,0:T(8,128)S(1)}, u32[]{:S(2)}, u32[]{:S(2)}) collective-permute-start(f32[2,4,32,256]{3,2,1,0:T(8,128)S(1)} %get-tuple-element.152), channel_id=1, source_target_pairs={{0,8},{2,10},{4,12},{6,14},{8,0},{10,2},{12,4},{14,6},{16,24},{18,... | collective-permute-start | bytes 786440 | tf_op jit(solution)/shard_map/ppermute | solution.py:327
  46.6 15.7 %collective-permute-start.20 = (f32[2,4,32,256]{3,2,1,0:T(8,128)S(1)}, f32[2,4,32,256]{3,2,1,0:T(8,128)S(1)}, u32[]{:S(2)}, u32[]{:S(2)}) collective-permute-start(f32[2,4,32,256]{3,2,1,0:T(8,128)S(1)} %get-tuple-element.153), channel_id=1, source_target_pairs={{0,16},{2,18},{4,20},{6,22},{8,24},{10,26},{12,28},{14,30},{16,0},... | collective-permute-start | bytes 786440 | tf_op jit(solution)/shard_map/ppermute | solution.py:327
  50.3 16.5 %collective-permute-start.22 = (f32[2,4,32,256]{3,2,1,0:T(8,128)S(1)}, f32[2,4,32,256]{3,2,1,0:T(8,128)S(1)}, u32[]{:S(2)}, u32[]{:S(2)}) collective-permute-start(f32[2,4,32,256]{3,2,1,0:T(8,128)S(1)} %get-tuple-element.158), channel_id=1, source_target_pairs={{0,2},{2,0},{4,6},{6,4},{8,10},{10,8},{12,14},{14,12},{16,18},{18,... | collective-permute-start | bytes 786440 | tf_op jit(solution)/shard_map/ppermute | solution.py:327
  51.3 16.3 %collective-permute-start.23 = (f32[2,4,32,256]{3,2,1,0:T(8,128)S(1)}, f32[2,4,32,256]{3,2,1,0:T(8,128)S(1)}, u32[]{:S(2)}, u32[]{:S(2)}) collective-permute-start(f32[2,4,32,256]{3,2,1,0:T(8,128)S(1)} %get-tuple-element.159), channel_id=1, source_target_pairs={{0,4},{2,6},{4,0},{6,2},{8,12},{10,14},{12,8},{14,10},{16,20},{18,... | collective-permute-start | bytes 786440 | tf_op jit(solution)/shard_map/ppermute | solution.py:327
  54.7 14.6 %collective-permute-start.24 = (f32[2,4,32,256]{3,2,1,0:T(8,128)S(1)}, f32[2,4,32,256]{3,2,1,0:T(8,128)S(1)}, u32[]{:S(2)}, u32[]{:S(2)}) collective-permute-start(f32[2,4,32,256]{3,2,1,0:T(8,128)S(1)} %get-tuple-element.147), channel_id=1, source_target_pairs={{0,6},{2,4},{4,2},{6,0},{8,14},{10,12},{12,10},{14,8},{16,22},{18,... | collective-permute-start | bytes 786440 | tf_op jit(solution)/shard_map/ppermute | solution.py:327
  62.2 13.0 %collective-permute-start.25 = (f32[512,128]{1,0:T(8,128)S(1)}, f32[512,128]{1,0:T(8,128)S(1)}, u32[]{:S(2)}, u32[]{:S(2)}) collective-permute-start(f32[512,128]{1,0:T(8,128)S(1)} %shard_map.115.refs_4_.refs_0_.refs_12_), channel_id=1, source_target_pairs={{0,16},{2,18},{4,20},{6,22},{8,24},{10,26},{12,28},{14,30},{16,0},... | collective-permute-start | bytes 786440 | tf_op jit(solution)/shard_map/ppermute | solution.py:17
  65.7 13.0 %collective-permute-start.26 = (f32[2,4,32,256]{3,2,1,0:T(8,128)S(1)}, f32[2,4,32,256]{3,2,1,0:T(8,128)S(1)}, u32[]{:S(2)}, u32[]{:S(2)}) collective-permute-start(f32[2,4,32,256]{3,2,1,0:T(8,128)S(1)} %get-tuple-element.166), channel_id=1, source_target_pairs={{0,2},{2,0},{4,6},{6,4},{8,10},{10,8},{12,14},{14,12},{16,18},{18,... | collective-permute-start | bytes 786440 | tf_op jit(solution)/shard_map/ppermute | solution.py:327
  66.8 11.9 %collective-permute-start.27 = (f32[2,4,32,256]{3,2,1,0:T(8,128)S(1)}, f32[2,4,32,256]{3,2,1,0:T(8,128)S(1)}, u32[]{:S(2)}, u32[]{:S(2)}) collective-permute-start(f32[2,4,32,256]{3,2,1,0:T(8,128)S(1)} %get-tuple-element.167), channel_id=1, source_target_pairs={{0,4},{2,6},{4,0},{6,2},{8,12},{10,14},{12,8},{14,10},{16,20},{18,... | collective-permute-start | bytes 786440 | tf_op jit(solution)/shard_map/ppermute | solution.py:327
  67.6 15.8 %collective-permute-start.28 = (f32[2,4,32,256]{3,2,1,0:T(8,128)S(1)}, f32[2,4,32,256]{3,2,1,0:T(8,128)S(1)}, u32[]{:S(2)}, u32[]{:S(2)}) collective-permute-start(f32[2,4,32,256]{3,2,1,0:T(8,128)S(1)} %get-tuple-element.156), channel_id=1, source_target_pairs={{0,6},{2,4},{4,2},{6,0},{8,14},{10,12},{12,10},{14,8},{16,22},{18,... | collective-permute-start | bytes 786440 | tf_op jit(solution)/shard_map/ppermute | solution.py:327
  69.3 15.3 %collective-permute-start.29 = (f32[128,512]{1,0:T(8,128)S(1)}, f32[128,512]{1,0:T(8,128)S(1)}, u32[]{:S(2)}, u32[]{:S(2)}) collective-permute-start(f32[128,512]{1,0:T(8,128)S(1)} %get-tuple-element.169), channel_id=1, source_target_pairs={{0,2},{2,0},{4,6},{6,4},{8,10},{10,8},{12,14},{14,12},{16,18},{18,... | collective-permute-start | bytes 786440 | tf_op jit(solution)/shard_map/ppermute | solution.py:17
  75.2 14.8 %collective-permute-start.31 = (f32[2,4,32,256]{3,2,1,0:T(8,128)S(1)}, f32[2,4,32,256]{3,2,1,0:T(8,128)S(1)}, u32[]{:S(2)}, u32[]{:S(2)}) collective-permute-start(f32[2,4,32,256]{3,2,1,0:T(8,128)S(1)} %get-tuple-element.181), channel_id=1, source_target_pairs={{0,8},{2,10},{4,12},{6,14},{8,0},{10,2},{12,4},{14,6},{16,24},{18,... | collective-permute-start | bytes 786440 | tf_op jit(solution)/shard_map/ppermute | solution.py:327
  78.7 18.0 %collective-permute-start.30 = (f32[2,4,32,256]{3,2,1,0:T(8,128)S(1)}, f32[2,4,32,256]{3,2,1,0:T(8,128)S(1)}, u32[]{:S(2)}, u32[]{:S(2)}) collective-permute-start(f32[2,4,32,256]{3,2,1,0:T(8,128)S(1)} %get-tuple-element.178), channel_id=1, source_target_pairs={{0,16},{2,18},{4,20},{6,22},{8,24},{10,26},{12,28},{14,30},{16,0},... | collective-permute-start | bytes 786440 | tf_op jit(solution)/shard_map/ppermute | solution.py:327
  78.7 24.6 %collective-permute-start.32 = (f32[2,4,32,256]{3,2,1,0:T(8,128)S(1)}, f32[2,4,32,256]{3,2,1,0:T(8,128)S(1)}, u32[]{:S(2)}, u32[]{:S(2)}) collective-permute-start(f32[2,4,32,256]{3,2,1,0:T(8,128)S(1)} %get-tuple-element.160), channel_id=1, source_target_pairs={{0,24},{2,26},{4,28},{6,30},{8,16},{10,18},{12,20},{14,22},{16,8},... | collective-permute-start | bytes 786440 | tf_op jit(solution)/shard_map/ppermute | solution.py:327

commit v4 on v3

--- a/solution.py
+++ b/solution.py
@@ -356,7 +356,8 @@
 
     def own_a(t):
         fronts = {e: parts[f"own{t}{e}"] for e in "hl"}
-        return run.named(fwd_own, {"s": s[t], **fronts}, {"a": vec})["a"]
+        mine = after(s[t], st[0]) if t == 1 else s[t]
+        return run.named(fwd_own, {"s": mine, **fronts}, {"a": vec})["a"]
 
     def own_b(t):
         fronts = {e: parts[f"own{t}{e}"] for e in "hl"}

time: 105 us -> 104 us (level)
  waiting for transfers between devices: 37.9 us -> 36.8 us
where the time goes in v4:
time: 104 us
  waiting for transfers between devices  36.8 us (35%)
  starting transfers between devices  33.9 us (33%)
  Pallas kernels  23.7 us (23%)
  blocking collectives  8.31 us (8%)
  between operations  1.09 us (1%)
    pallas_call x25, Pallas kernels, __call__(): pl.pallas_call(kernel, out_shape=tuple(outs), in_specs=[pl.BlockSpec(memo...  20.6 us
    ppermute x12, waiting for transfers between devices, exchange(): lax.ppermute(v, 'cube', [(i, i ^ j * step) for i in range(n)])  18.9 us
    ppermute x12, starting transfers between devices, exchange(): lax.ppermute(v, 'cube', [(i, i ^ j * step) for i in range(n)])  17.9 us
    ppermute x8, starting transfers between devices, partner(): lax.ppermute(x, 'cube', [(i, i ^ 1 << distance) for i in range(lax.axis_s...  13.6 us
    ppermute x8, waiting for transfers between devices, partner(): lax.ppermute(x, 'cube', [(i, i ^ 1 << distance) for i in range(lax.axis_s...  9.51 us
    ppermute x13, waiting for transfers between devices, swap(): return lax.ppermute(x, 'cores', [(0, 1), (1, 0)])  8.36 us
    all_gather x4, blocking collectives, both(): return lax.all_gather(x, 'cores')  8.31 us
    pallas_call x3, Pallas kernels, place(): pl.pallas_call(functools.partial(place_kernel, plan), out_shape=out, in_s...  3.06 us
  transfers between devices with their start and end apart: 33, of which 11 were waited for; matrix products, arithmetic and copies ran while one was open for 0% of the time, Pallas kernels for 22%

profile of v4, /device:TPU:8, one launch (start us, length us, event | category | flops | bytes accessed | tf_op | source)
XLA Modules:
  0.0 103.7 jit_solution(2074987195206678977)
XLA Ops:
  0.7 0.5 collective-permute-start.4
  1.2 1.3 %shard_map.102 = (f32[256,512]{1,0:T(8,128)S(1)}, f32[256,512]{1,0:T(8,128)S(1)}) custom-call(f32[4,256,512]{2,1,0:T(8,128)} %refs_3_.1, f32[4,256,512]{2,1,0:T(8,128)} %refs_5_.1), custom_call_target="tpu_custom_call" | custom-call | tf_op jit(solution)/shard_map/pallas_call | solution.py:65
  2.7 0.5 collective-permute-start.1
  3.2 3.5 %collective-permute-done.2.refs_5_ = f32[256,256]{1,0:T(8,128)S(1)} collective-permute-done((f32[256,256]{1,0:T(8,128)S(1)}, f32[256,256]{1,0:T(8,128)S(1)}, u32[]{:S(2)}, u32[]{:S(2)}) %collective-permute-start.2) | collective-permute-done | bytes 262176 | tf_op jit(solution)/shard_map/ppermute | solution.py:21
  6.8 0.2 collective-permute-start.5
  7.0 0.4 collective-permute-start.6
  7.5 1.0 shard_map.103
  8.5 1.6 %collective-permute-start.8 = (f32[512,128]{1,0:T(8,128)S(1)}, f32[512,128]{1,0:T(8,128)S(1)}, u32[]{:S(2)}, u32[]{:S(2)}) collective-permute-start(f32[512,128]{1,0:T(8,128)S(1)} %get-tuple-element.174.refs_0_), channel_id=1, source_target_pairs={{0,2},{2,0},{4,6},{6,4},{8,10},{10,8},{12,14},{14,12},{16,18},{18,... | collective-permute-start | bytes 786440 | tf_op jit(solution)/shard_map/ppermute | solution.py:17
  10.1 2.6 %collective-permute-start.9 = (f32[128,512]{1,0:T(8,128)S(1)}, f32[128,512]{1,0:T(8,128)S(1)}, u32[]{:S(2)}, u32[]{:S(2)}) collective-permute-start(f32[128,512]{1,0:T(8,128)S(1)} %get-tuple-element.116), channel_id=1, source_target_pairs={{0,16},{2,18},{4,20},{6,22},{8,24},{10,26},{12,28},{14,30},{16,0},... | collective-permute-start | bytes 786440 | tf_op jit(solution)/shard_map/ppermute | solution.py:17
  12.8 1.4 %collective-permute-done.6.refs_1_ = f32[4,256,512]{2,1,0:T(8,128)S(1)} collective-permute-done((f32[4,256,512]{2,1,0:T(8,128)}, f32[4,256,512]{2,1,0:T(8,128)S(1)}, u32[]{:S(2)}, u32[]{:S(2)}) %collective-permute-start.6) | collective-permute-done | bytes 2097184 | tf_op jit(solution)/shard_map/ppermute | solution.py:21
  14.2 3.4 %collective-permute-done.7.refs_2_ = f32[4,256,512]{2,1,0:T(8,128)S(1)} collective-permute-done((f32[4,256,512]{2,1,0:T(8,128)}, f32[4,256,512]{2,1,0:T(8,128)S(1)}, u32[]{:S(2)}, u32[]{:S(2)}) %collective-permute-start.7) | collective-permute-done | bytes 2097184 | tf_op jit(solution)/shard_map/ppermute | solution.py:21
  17.6 3.0 %shard_map.104 = (bf16[512,512]{1,0:T(8,128)(2,1)S(1)}, bf16[512,512]{1,0:T(8,128)(2,1)S(1)}, bf16[512,512]{1,0:T(8,128)(2,1)S(1)}, bf16[512,512]{1,0:T(8,128)(2...) custom-call(f32[4,256,512]{2,1,0:T(8,128)S(1)} %collective-permute-d, ...), custom_call_target="tpu_custom_call" | custom-call | tf_op jit(solution)/shard_map/pallas_call | solution.py:65
  20.6 0.4 shard_map.105.refs_0_
  21.1 0.8 shard_map.106.refs_0_.refs_4_
  21.9 1.6 %collective-permute-start.11 = (f32[512,128]{1,0:T(8,128)S(1)}, f32[512,128]{1,0:T(8,128)S(1)}, u32[]{:S(2)}, u32[]{:S(2)}) collective-permute-start(f32[512,128]{1,0:T(8,128)S(1)} %shard_map.106.refs_0_.refs_4_), channel_id=1, source_target_pairs={{0,4},{2,6},{4,0},{6,2},{8,12},{10,14},{12,8},{14,10},{16,20},{18,... | collective-permute-start | bytes 786440 | tf_op jit(solution)/shard_map/ppermute | solution.py:17
  23.5 0.4 shard_map.107.refs_0_
  24.0 0.8 shard_map.108
  24.8 1.4 %collective-permute-start.12 = (f32[128,512]{1,0:T(8,128)S(1)}, f32[128,512]{1,0:T(8,128)S(1)}, u32[]{:S(2)}, u32[]{:S(2)}) collective-permute-start(f32[128,512]{1,0:T(8,128)S(1)} %get-tuple-element.133), channel_id=1, source_target_pairs={{0,8},{2,10},{4,12},{6,14},{8,0},{10,2},{12,4},{14,6},{16,24},{18,... | collective-permute-start | bytes 786440 | tf_op jit(solution)/shard_map/ppermute | solution.py:17
  26.2 0.4 shard_map.109.refs_0_
  26.7 3.6 %collective-permute-done.11.refs_1_ = f32[512,128]{1,0:T(8,128)S(1)} collective-permute-done((f32[512,128]{1,0:T(8,128)S(1)}, f32[512,128]{1,0:T(8,128)S(1)}, u32[]{:S(2)}, u32[]{:S(2)}) %collective-permute-start.11) | collective-permute-done | bytes 262176 | tf_op jit(solution)/shard_map/ppermute | solution.py:17
  30.3 0.8 shard_map.110.refs_4_.refs_0_.refs_8_
  31.2 0.3 collective-permute-start.17
  31.5 0.2 collective-permute-start.16
  31.7 0.4 shard_map.111.refs_0_
  32.1 1.0 collective-permute-done.12.refs_1_
  33.1 0.8 shard_map.112
  34.0 1.6 %collective-permute-start.18 = (f32[128,512]{1,0:T(8,128)S(1)}, f32[128,512]{1,0:T(8,128)S(1)}, u32[]{:S(2)}, u32[]{:S(2)}) collective-permute-start(f32[128,512]{1,0:T(8,128)S(1)} %get-tuple-element.142), channel_id=1, source_target_pairs={{0,4},{2,6},{4,0},{6,2},{8,12},{10,14},{12,8},{14,10},{16,20},{18,... | collective-permute-start | bytes 786440 | tf_op jit(solution)/shard_map/ppermute | solution.py:17
  35.6 1.3 %shard_map.113 = (f32[2,4,32,256]{3,2,1,0:T(8,128)S(1)}, f32[2,4,32,256]{3,2,1,0:T(8,128)S(1)}, f32[2,4,32,256]{3,2,1,0:T(8,128)S(1)}, f32[2,4,32,256]{3,2,1,0:T(8,128)S(1)}) custom-call(s32[1,512]{1,0:T(1,128)S(1)} %copy-done.3, f32[512,128]{1,0:T(8,128)S(1)} %shard_map.106.refs_0_.refs_4_, f32[512,128]{1,0:T(8,128)S(1)} %collective-permute-done.13.refs_1_.refs_5_, ...), custom_call_target="tpu_custom_call" | custom-call | tf_op jit(solution)/shard_map/pallas_call | solution.py:65
  36.8 2.3 %collective-permute-start.21 = (f32[2,4,32,256]{3,2,1,0:T(8,128)S(1)}, f32[2,4,32,256]{3,2,1,0:T(8,128)S(1)}, u32[]{:S(2)}, u32[]{:S(2)}) collective-permute-start(f32[2,4,32,256]{3,2,1,0:T(8,128)S(1)} %get-tuple-element.139), channel_id=1, source_target_pairs={{0,24},{2,26},{4,28},{6,30},{8,16},{10,18},{12,20},{14,22},{16,8},... | collective-permute-start | bytes 786440 | tf_op jit(solution)/shard_map/ppermute | solution.py:327
  39.1 0.4 shard_map.114.refs_0_
  39.6 2.7 %collective-permute-start.19 = (f32[2,4,32,256]{3,2,1,0:T(8,128)S(1)}, f32[2,4,32,256]{3,2,1,0:T(8,128)S(1)}, u32[]{:S(2)}, u32[]{:S(2)}) collective-permute-start(f32[2,4,32,256]{3,2,1,0:T(8,128)S(1)} %get-tuple-element.154), channel_id=1, source_target_pairs={{0,8},{2,10},{4,12},{6,14},{8,0},{10,2},{12,4},{14,6},{16,24},{18,... | collective-permute-start | bytes 786440 | tf_op jit(solution)/shard_map/ppermute | solution.py:327
  42.3 0.8 shard_map.115.refs_4_.refs_0_.refs_12_
  43.1 2.2 %all-gather.1 = f32[1024,128]{1,0:T(8,128)S(1)} all-gather(f32[512,128]{1,0:T(8,128)S(1)} %shard_map.115.refs_4_.refs_0_.refs_12_), channel_id=3, replica_groups=mesh['cube'=16,'cores'=2] {'cores'}, dimensions={0}, use_global_device_ids=true | all-gather | bytes 786432 | tf_op jit(solution)/shard_map/all_gather | solution.py:25
  45.2 0.4 shard_map.116.refs_0_
  45.6 0.8 shard_map.117
  46.4 0.5 collective-permute-start.20
  46.9 2.2 %all-gather = f32[256,256]{1,0:T(8,128)S(1)} all-gather(f32[128,256]{1,0:T(8,128)S(1)} %get-tuple-element.144), channel_id=2, replica_groups=mesh['cube'=16,'cores'=2] {'cores'}, dimensions={0}, use_global_device_ids=true | all-gather | bytes 393216 | tf_op jit(solution)/shard_map/all_gather | solution.py:25
  49.0 1.3 %shard_map.118 = (f32[2,4,32,256]{3,2,1,0:T(8,128)S(1)}, f32[2,4,32,256]{3,2,1,0:T(8,128)S(1)}, f32[2,4,32,256]{3,2,1,0:T(8,128)S(1)}, f32[2,4,32,256]{3,2,1,0:T(8,128)S(1)}) custom-call(s32[1,512]{1,0:T(1,128)S(1)} %copy-done.3, f32[512,128]{1,0:T(8,128)S(1)} %get-tuple-element.174.refs_0_, f32[512,128]{1,0:T(8,128)S(1)} %collective-permute-done.10.refs_1_, ...), custom_call_target="tpu_custom_call" | custom-call | tf_op jit(solution)/shard_map/pallas_call | solution.py:65
  50.3 1.4 %collective-permute-start.22 = (f32[2,4,32,256]{3,2,1,0:T(8,128)S(1)}, f32[2,4,32,256]{3,2,1,0:T(8,128)S(1)}, u32[]{:S(2)}, u32[]{:S(2)}) collective-permute-start(f32[2,4,32,256]{3,2,1,0:T(8,128)S(1)} %get-tuple-element.160), channel_id=1, source_target_pairs={{0,2},{2,0},{4,6},{6,4},{8,10},{10,8},{12,14},{14,12},{16,18},{18,... | collective-permute-start | bytes 786440 | tf_op jit(solution)/shard_map/ppermute | solution.py:327
  51.7 1.5 %collective-permute-start.23 = (f32[2,4,32,256]{3,2,1,0:T(8,128)S(1)}, f32[2,4,32,256]{3,2,1,0:T(8,128)S(1)}, u32[]{:S(2)}, u32[]{:S(2)}) collective-permute-start(f32[2,4,32,256]{3,2,1,0:T(8,128)S(1)} %get-tuple-element.161), channel_id=1, source_target_pairs={{0,4},{2,6},{4,0},{6,2},{8,12},{10,14},{12,8},{14,10},{16,20},{18,... | collective-permute-start | bytes 786440 | tf_op jit(solution)/shard_map/ppermute | solution.py:327
  53.2 1.3 %collective-permute-done.19.refs_1_ = f32[2,4,32,256]{3,2,1,0:T(8,128)S(1)} collective-permute-done((f32[2,4,32,256]{3,2,1,0:T(8,128)S(1)}, f32[2,4,32,256]{3,2,1,0:T(8,128)S(1)}, u32[]{:S(2)}, u32[]{:S(2)}) %collective-permute-start.19) | collective-permute-done | bytes 262176 | tf_op jit(solution)/shard_map/ppermute | solution.py:327
  54.5 1.2 %collective-permute-start.24 = (f32[2,4,32,256]{3,2,1,0:T(8,128)S(1)}, f32[2,4,32,256]{3,2,1,0:T(8,128)S(1)}, u32[]{:S(2)}, u32[]{:S(2)}) collective-permute-start(f32[2,4,32,256]{3,2,1,0:T(8,128)S(1)} %get-tuple-element.149), channel_id=1, source_target_pairs={{0,6},{2,4},{4,2},{6,0},{8,14},{10,12},{12,10},{14,8},{16,22},{18,... | collective-permute-start | bytes 786440 | tf_op jit(solution)/shard_map/ppermute | solution.py:327
  55.7 0.4 shard_map.119.refs_0_
  56.2 0.4 shard_map.120.refs_0_
  56.6 5.3 %collective-permute-done.20.refs_2_ = f32[2,4,32,256]{3,2,1,0:T(8,128)S(1)} collective-permute-done((f32[2,4,32,256]{3,2,1,0:T(8,128)S(1)}, f32[2,4,32,256]{3,2,1,0:T(8,128)S(1)}, u32[]{:S(2)}, u32[]{:S(2)}) %collective-permute-start.20) | collective-permute-done | bytes 262176 | tf_op jit(solution)/shard_map/ppermute | solution.py:327
  61.8 3.4 %collective-permute-start.25 = (f32[512,128]{1,0:T(8,128)S(1)}, f32[512,128]{1,0:T(8,128)S(1)}, u32[]{:S(2)}, u32[]{:S(2)}) collective-permute-start(f32[512,128]{1,0:T(8,128)S(1)} %shard_map.115.refs_4_.refs_0_.refs_12_), channel_id=1, source_target_pairs={{0,16},{2,18},{4,20},{6,22},{8,24},{10,26},{12,28},{14,30},{16,0},... | collective-permute-start | bytes 786440 | tf_op jit(solution)/shard_map/ppermute | solution.py:17
  65.3 1.2 %collective-permute-start.26 = (f32[2,4,32,256]{3,2,1,0:T(8,128)S(1)}, f32[2,4,32,256]{3,2,1,0:T(8,128)S(1)}, u32[]{:S(2)}, u32[]{:S(2)}) collective-permute-start(f32[2,4,32,256]{3,2,1,0:T(8,128)S(1)} %get-tuple-element.168), channel_id=1, source_target_pairs={{0,2},{2,0},{4,6},{6,4},{8,10},{10,8},{12,14},{14,12},{16,18},{18,... | collective-permute-start | bytes 786440 | tf_op jit(solution)/shard_map/ppermute | solution.py:327
  66.5 1.4 %collective-permute-start.27 = (f32[2,4,32,256]{3,2,1,0:T(8,128)S(1)}, f32[2,4,32,256]{3,2,1,0:T(8,128)S(1)}, u32[]{:S(2)}, u32[]{:S(2)}) collective-permute-start(f32[2,4,32,256]{3,2,1,0:T(8,128)S(1)} %get-tuple-element.169), channel_id=1, source_target_pairs={{0,4},{2,6},{4,0},{6,2},{8,12},{10,14},{12,8},{14,10},{16,20},{18,... | collective-permute-start | bytes 786440 | tf_op jit(solution)/shard_map/ppermute | solution.py:327
  68.0 0.9 collective-permute-start.28
  68.9 1.1 %collective-permute-start.29 = (f32[128,512]{1,0:T(8,128)S(1)}, f32[128,512]{1,0:T(8,128)S(1)}, u32[]{:S(2)}, u32[]{:S(2)}) collective-permute-start(f32[128,512]{1,0:T(8,128)S(1)} %get-tuple-element.171), channel_id=1, source_target_pairs={{0,2},{2,0},{4,6},{6,4},{8,10},{10,8},{12,14},{14,12},{16,18},{18,... | collective-permute-start | bytes 786440 | tf_op jit(solution)/shard_map/ppermute | solution.py:17
  70.1 4.7 %collective-permute-done.25.refs_1_ = f32[512,128]{1,0:T(8,128)S(1)} collective-permute-done((f32[512,128]{1,0:T(8,128)S(1)}, f32[512,128]{1,0:T(8,128)S(1)}, u32[]{:S(2)}, u32[]{:S(2)}) %collective-permute-start.25) | collective-permute-done | bytes 262176 | tf_op jit(solution)/shard_map/ppermute | solution.py:17
  74.8 3.3 %collective-permute-start.31 = (f32[2,4,32,256]{3,2,1,0:T(8,128)S(1)}, f32[2,4,32,256]{3,2,1,0:T(8,128)S(1)}, u32[]{:S(2)}, u32[]{:S(2)}) collective-permute-start(f32[2,4,32,256]{3,2,1,0:T(8,128)S(1)} %get-tuple-element.183), channel_id=1, source_target_pairs={{0,8},{2,10},{4,12},{6,14},{8,0},{10,2},{12,4},{14,6},{16,24},{18,... | collective-permute-start | bytes 786440 | tf_op jit(solution)/shard_map/ppermute | solution.py:327
  78.2 1.4 %collective-permute-start.32 = (f32[2,4,32,256]{3,2,1,0:T(8,128)S(1)}, f32[2,4,32,256]{3,2,1,0:T(8,128)S(1)}, u32[]{:S(2)}, u32[]{:S(2)}) collective-permute-start(f32[2,4,32,256]{3,2,1,0:T(8,128)S(1)} %get-tuple-element.162), channel_id=1, source_target_pairs={{0,24},{2,26},{4,28},{6,30},{8,16},{10,18},{12,20},{14,22},{16,8},... | collective-permute-start | bytes 786440 | tf_op jit(solution)/shard_map/ppermute | solution.py:327
  79.6 1.2 %shard_map.123 = (f32[512,128]{1,0:T(8,128)}, f32[256,128]{1,0:T(8,128)S(1)}, f32[256,128]{1,0:T(8,128)S(1)}) custom-call(f32[512,128]{1,0:T(8,128)S(1)} %shard_map.119.refs_0_, f32[512,128]{1,0:T(8,128)S(1)} %collective-permute-done.25.refs_1_, bf16[512,512]{1,0:T(8,128)(2,1)S(1)} %get-tuple-element.164.refs_2_, bf16[512,512]{1,0:T(8,128)(2,1)S(1)} %get-tuple-element.165.refs_3_), custom_call_target="tpu_custom_call" | custom-call | tf_op jit(solution)/shard_map/pallas_call | solution.py:65
  80.8 2.0 %all-gather.3 = f32[512,128]{1,0:T(8,128)S(1)} all-gather(f32[256,128]{1,0:T(8,128)S(1)} %get-tuple-element.166), channel_id=5, replica_groups=mesh['cube'=16,'cores'=2] {'cores'}, dimensions={0}, use_global_device_ids=true | all-gather | bytes 393216 | tf_op jit(solution)/shard_map/all_gather | solution.py:25
  82.7 1.2 %shard_map.124.refs_2_ = f32[4,32,4096]{2,1,0:T(8,128)} custom-call(f32[2,4,32,256]{3,2,1,0:T(8,128)S(1)} %get-tuple-element.167.refs_0_, f32[2,4,32,256]{3,2,1,0:T(8,128)S(1)} %collective-permute-done.26.refs_1_, f32[2,4,32,256]{3,2,1,0:T(8,128)S(1)} %collective-permute-done.27.refs_2_, f32[2,4,32,256]{3,2,1,0:T(8,128)S(1)} %collective-permute-done.28.refs_3_), custom_call_target="tpu_custom_call" | custom-call | tf_op jit(solution)/shard_map/pallas_call | solution.py:265
  84.0 1.1 %shard_map.125 = (f32[128,512]{1,0:T(8,128)}, f32[128,256]{1,0:T(8,128)S(1)}, f32[128,256]{1,0:T(8,128)S(1)}) custom-call(f32[128,512]{1,0:T(8,128)S(1)} %shard_map.120.refs_0_, f32[128,512]{1,0:T(8,128)S(1)} %collective-permute-done.29.refs_1_, bf16[512,512]{1,0:T(8,128)(2,1)S(1)} %get-tuple-element.172.refs_2_, bf16[512,512]{1,0:T(8,128)(2,1)S(1)} %get-tuple-element.100.refs_3_), custom_call_target="tpu_custom_call" | custom-call | tf_op jit(solution)/shard_map/pallas_call | solution.py:65
  85.1 2.0 %all-gather.2 = f32[256,256]{1,0:T(8,128)S(1)} all-gather(f32[128,256]{1,0:T(8,128)S(1)} %get-tuple-element.173), channel_id=4, replica_groups=mesh['cube'=16,'cores'=2] {'cores'}, dimensions={0}, use_global_device_ids=true | all-gather | bytes 393216 | tf_op jit(solution)/shard_map/all_gather | solution.py:25
  87.1 1.6 %shard_map.126 = (f32[4,256,256]{2,1,0:T(8,128)}, f32[4,256,256]{2,1,0:T(8,128)}) custom-call(f32[512,128]{1,0:T(8,128)S(1)} %get-tuple-element.174.refs_0_, f32[512,128]{1,0:T(8,128)S(1)} %collective-permute-done.10.refs_1_, f32[128,256]{1,0:T(8,128)S(1)} %get-tuple-element.175.refs_2_, f32[2,128,256]{2,1,0:T(8,128)S(1)} %bitcast.8, ...), custom_call_target="tpu_custom_call" | custom-call | tf_op jit(solution)/shard_map/pallas_call | solution.py:65
  88.7 0.7 shard_map.127
  89.5 0.9 shard_map.128.refs_2_
  90.4 5.7 %collective-permute-done.30.refs_0_ = f32[2,4,32,256]{3,2,1,0:T(8,128)S(1)} collective-permute-done((f32[2,4,32,256]{3,2,1,0:T(8,128)S(1)}, f32[2,4,32,256]{3,2,1,0:T(8,128)S(1)}, u32[]{:S(2)}, u32[]{:S(2)}) %collective-permute-start.30) | collective-permute-done | bytes 262176 | tf_op jit(solution)/shard_map/ppermute | solution.py:327
  96.1 6.6 %collective-permute-done.32.refs_1_ = f32[2,4,32,256]{3,2,1,0:T(8,128)S(1)} collective-permute-done((f32[2,4,32,256]{3,2,1,0:T(8,128)S(1)}, f32[2,4,32,256]{3,2,1,0:T(8,128)S(1)}, u32[]{:S(2)}, u32[]{:S(2)}) %collective-permute-start.32) | collective-permute-done | bytes 262176 | tf_op jit(solution)/shard_map/ppermute | solution.py:327
  102.7 0.9 shard_map.129
  (44 shorter events, 1.0 us)
Async XLA Ops:
  0.6 6.9 %copy-start.1 = (f32[4,256,256]{2,1,0:T(8,128)S(1)}, f32[4,256,256]{2,1,0:T(8,128)}, u32[]{:S(2)}) copy-start(f32[4,256,256]{2,1,0:T(8,128)} %refs_6_.1) | copy-start | bytes 3145732
  0.6 6.1 %copy-start.4 = (f32[4,256,512]{2,1,0:T(8,128)S(1)}, f32[4,256,512]{2,1,0:T(8,128)}, u32[]{:S(2)}) copy-start(f32[4,256,512]{2,1,0:T(8,128)} %refs_3_.1) | copy-start | bytes 6291460
  0.7 2.5 %copy-start.2 = (f32[256,256]{1,0:T(8,128)S(1)}, f32[256,256]{1,0:T(8,128)}, u32[]{:S(2)}) copy-start(f32[256,256]{1,0:T(8,128)} %refs_4_.2) | copy-start | bytes 786436
  0.7 6.1 %collective-permute-start.3 = (f32[4,256,256]{2,1,0:T(8,128)}, f32[4,256,256]{2,1,0:T(8,128)S(1)}, u32[]{:S(2)}, u32[]{:S(2)}) collective-permute-start(f32[4,256,256]{2,1,0:T(8,128)} %refs_6_.1), channel_id=1, source_target_pairs={{0,1},{1,0},{2,3},{3,2},{4,5},{5,4},{6,7},{7,6},{8,9},{9,8},{10,11... | collective-permute-start | bytes 3145736 | tf_op jit(solution)/shard_map/ppermute | solution.py:21
  0.7 6.0 %collective-permute-start.4 = (f32[4,256,256]{2,1,0:T(8,128)}, f32[4,256,256]{2,1,0:T(8,128)S(1)}, u32[]{:S(2)}, u32[]{:S(2)}) collective-permute-start(f32[4,256,256]{2,1,0:T(8,128)} %refs_1_.7), channel_id=1, source_target_pairs={{0,1},{1,0},{2,3},{3,2},{4,5},{5,4},{6,7},{7,6},{8,9},{9,8},{10,11... | collective-permute-start | bytes 3145736 | tf_op jit(solution)/shard_map/ppermute | solution.py:21
  2.6 4.2 %collective-permute-start = (f32[256,512]{1,0:T(8,128)S(1)}, f32[256,512]{1,0:T(8,128)S(1)}, u32[]{:S(2)}, u32[]{:S(2)}) collective-permute-start(f32[256,512]{1,0:T(8,128)S(1)} %get-tuple-element.95.refs_0_), channel_id=1, source_target_pairs={{0,1},{1,0},{2,3},{3,2},{4,5},{5,4},{6,7},{7,6},{8,9},{9,8},{10,11... | collective-permute-start | bytes 1572872 | tf_op jit(solution)/shard_map/ppermute | solution.py:21
  2.7 4.1 %collective-permute-start.1 = (f32[256,512]{1,0:T(8,128)S(1)}, f32[256,512]{1,0:T(8,128)S(1)}, u32[]{:S(2)}, u32[]{:S(2)}) collective-permute-start(f32[256,512]{1,0:T(8,128)S(1)} %get-tuple-element.96.refs_2_), channel_id=1, source_target_pairs={{0,1},{1,0},{2,3},{3,2},{4,5},{5,4},{6,7},{7,6},{8,9},{9,8},{10,11... | collective-permute-start | bytes 1572872 | tf_op jit(solution)/shard_map/ppermute | solution.py:21
  3.2 3.6 %collective-permute-start.2 = (f32[256,256]{1,0:T(8,128)S(1)}, f32[256,256]{1,0:T(8,128)S(1)}, u32[]{:S(2)}, u32[]{:S(2)}) collective-permute-start(f32[256,256]{1,0:T(8,128)S(1)} %copy-done.2), channel_id=1, source_target_pairs={{0,1},{1,0},{2,3},{3,2},{4,5},{5,4},{6,7},{7,6},{8,9},{9,8},{10,11... | collective-permute-start | bytes 786440 | tf_op jit(solution)/shard_map/ppermute | solution.py:21
  6.8 5.9 %collective-permute-start.5 = (f32[4,256,512]{2,1,0:T(8,128)S(1)}, f32[4,256,512]{2,1,0:T(8,128)S(1)}, u32[]{:S(2)}, u32[]{:S(2)}) collective-permute-start(f32[4,256,512]{2,1,0:T(8,128)S(1)} %copy-done.4), channel_id=1, source_target_pairs={{0,1},{1,0},{2,3},{3,2},{4,5},{5,4},{6,7},{7,6},{8,9},{9,8},{10,11... | collective-permute-start | bytes 6291464 | tf_op jit(solution)/shard_map/ppermute | solution.py:21
  7.0 7.2 %collective-permute-start.6 = (f32[4,256,512]{2,1,0:T(8,128)}, f32[4,256,512]{2,1,0:T(8,128)S(1)}, u32[]{:S(2)}, u32[]{:S(2)}) collective-permute-start(f32[4,256,512]{2,1,0:T(8,128)} %refs_4_.3), channel_id=1, source_target_pairs={{0,1},{1,0},{2,3},{3,2},{4,5},{5,4},{6,7},{7,6},{8,9},{9,8},{10,11... | collective-permute-start | bytes 6291464 | tf_op jit(solution)/shard_map/ppermute | solution.py:21
  7.4 10.2 %collective-permute-start.7 = (f32[4,256,512]{2,1,0:T(8,128)}, f32[4,256,512]{2,1,0:T(8,128)S(1)}, u32[]{:S(2)}, u32[]{:S(2)}) collective-permute-start(f32[4,256,512]{2,1,0:T(8,128)} %refs_5_.1), channel_id=1, source_target_pairs={{0,1},{1,0},{2,3},{3,2},{4,5},{5,4},{6,7},{7,6},{8,9},{9,8},{10,11... | collective-permute-start | bytes 6291464 | tf_op jit(solution)/shard_map/ppermute | solution.py:21
  8.5 12.5 %collective-permute-start.8 = (f32[512,128]{1,0:T(8,128)S(1)}, f32[512,128]{1,0:T(8,128)S(1)}, u32[]{:S(2)}, u32[]{:S(2)}) collective-permute-start(f32[512,128]{1,0:T(8,128)S(1)} %get-tuple-element.174.refs_0_), channel_id=1, source_target_pairs={{0,2},{2,0},{4,6},{6,4},{8,10},{10,8},{12,14},{14,12},{16,18},{18,... | collective-permute-start | bytes 786440 | tf_op jit(solution)/shard_map/ppermute | solution.py:17
  10.1 13.9 %collective-permute-start.9 = (f32[128,512]{1,0:T(8,128)S(1)}, f32[128,512]{1,0:T(8,128)S(1)}, u32[]{:S(2)}, u32[]{:S(2)}) collective-permute-start(f32[128,512]{1,0:T(8,128)S(1)} %get-tuple-element.116), channel_id=1, source_target_pairs={{0,16},{2,18},{4,20},{6,22},{8,24},{10,26},{12,28},{14,30},{16,0},... | collective-permute-start | bytes 786440 | tf_op jit(solution)/shard_map/ppermute | solution.py:17
  12.7 13.5 %collective-permute-start.10 = (f32[512,128]{1,0:T(8,128)S(1)}, f32[512,128]{1,0:T(8,128)S(1)}, u32[]{:S(2)}, u32[]{:S(2)}) collective-permute-start(f32[512,128]{1,0:T(8,128)S(1)} %get-tuple-element.174.refs_0_), channel_id=1, source_target_pairs={{0,1},{1,0},{2,3},{3,2},{4,5},{5,4},{6,7},{7,6},{8,9},{9,8},{10,11... | collective-permute-start | bytes 786440 | tf_op jit(solution)/shard_map/ppermute | solution.py:21
  21.1 2.4 %copy-start = (f32[4,256,256]{2,1,0:T(8,128)S(1)}, f32[4,256,256]{2,1,0:T(8,128)}, u32[]{:S(2)}) copy-start(f32[4,256,256]{2,1,0:T(8,128)} %refs_1_.7) | copy-start | bytes 3145732
  21.9 8.4 %collective-permute-start.11 = (f32[512,128]{1,0:T(8,128)S(1)}, f32[512,128]{1,0:T(8,128)S(1)}, u32[]{:S(2)}, u32[]{:S(2)}) collective-permute-start(f32[512,128]{1,0:T(8,128)S(1)} %shard_map.106.refs_0_.refs_4_), channel_id=1, source_target_pairs={{0,4},{2,6},{4,0},{6,2},{8,12},{10,14},{12,8},{14,10},{16,20},{18,... | collective-permute-start | bytes 786440 | tf_op jit(solution)/shard_map/ppermute | solution.py:17
  24.8 8.3 %collective-permute-start.12 = (f32[128,512]{1,0:T(8,128)S(1)}, f32[128,512]{1,0:T(8,128)S(1)}, u32[]{:S(2)}, u32[]{:S(2)}) collective-permute-start(f32[128,512]{1,0:T(8,128)S(1)} %get-tuple-element.133), channel_id=1, source_target_pairs={{0,8},{2,10},{4,12},{6,14},{8,0},{10,2},{12,4},{14,6},{16,24},{18,... | collective-permute-start | bytes 786440 | tf_op jit(solution)/shard_map/ppermute | solution.py:17
  26.2 9.3 %collective-permute-start.13 = (f32[512,128]{1,0:T(8,128)S(1)}, f32[512,128]{1,0:T(8,128)S(1)}, u32[]{:S(2)}, u32[]{:S(2)}) collective-permute-start(f32[512,128]{1,0:T(8,128)S(1)} %shard_map.106.refs_0_.refs_4_), channel_id=1, source_target_pairs={{0,1},{1,0},{2,3},{3,2},{4,5},{5,4},{6,7},{7,6},{8,9},{9,8},{10,11... | collective-permute-start | bytes 786440 | tf_op jit(solution)/shard_map/ppermute | solution.py:21
  31.1 4.4 %collective-permute-start.15 = (f32[512,128]{1,0:T(8,128)S(1)}, f32[512,128]{1,0:T(8,128)S(1)}, u32[]{:S(2)}, u32[]{:S(2)}) collective-permute-start(f32[512,128]{1,0:T(8,128)S(1)} %shard_map.110.refs_4_.refs_0_.refs_8_), channel_id=1, source_target_pairs={{0,1},{1,0},{2,3},{3,2},{4,5},{5,4},{6,7},{7,6},{8,9},{9,8},{10,11... | collective-permute-start | bytes 786440 | tf_op jit(solution)/shard_map/ppermute | solution.py:21
  31.2 11.1 %collective-permute-start.17 = (f32[512,128]{1,0:T(8,128)S(1)}, f32[512,128]{1,0:T(8,128)S(1)}, u32[]{:S(2)}, u32[]{:S(2)}) collective-permute-start(f32[512,128]{1,0:T(8,128)S(1)} %shard_map.110.refs_4_.refs_0_.refs_8_), channel_id=1, source_target_pairs={{0,8},{2,10},{4,12},{6,14},{8,0},{10,2},{12,4},{14,6},{16,24},{18,... | collective-permute-start | bytes 786440 | tf_op jit(solution)/shard_map/ppermute | solution.py:17
  31.5 2.5 %collective-permute-start.16 = (f32[128,256]{1,0:T(8,128)S(1)}, f32[128,256]{1,0:T(8,128)S(1)}, u32[]{:S(2)}, u32[]{:S(2)}) collective-permute-start(f32[128,256]{1,0:T(8,128)S(1)} %get-tuple-element.122), channel_id=1, source_target_pairs={{0,1},{1,0},{2,3},{3,2},{4,5},{5,4},{6,7},{7,6},{8,9},{9,8},{10,11... | collective-permute-start | bytes 393224 | tf_op jit(solution)/shard_map/ppermute | solution.py:21
  32.1 3.5 %copy-start.3 = (s32[1,512]{1,0:T(1,128)S(1)}, s32[1,512]{1,0:T(1,128)}, u32[]{:S(2)}) copy-start(s32[1,512]{1,0:T(1,128)} %map_ref.1) | copy-start | bytes 6148
  33.9 1.7 %collective-permute-start.14 = (f32[128,256]{1,0:T(8,128)S(1)}, f32[128,256]{1,0:T(8,128)S(1)}, u32[]{:S(2)}, u32[]{:S(2)}) collective-permute-start(f32[128,256]{1,0:T(8,128)S(1)} %get-tuple-element.135), channel_id=1, source_target_pairs={{0,1},{1,0},{2,3},{3,2},{4,5},{5,4},{6,7},{7,6},{8,9},{9,8},{10,11... | collective-permute-start | bytes 393224 | tf_op jit(solution)/shard_map/ppermute | solution.py:21
  34.0 11.7 %collective-permute-start.18 = (f32[128,512]{1,0:T(8,128)S(1)}, f32[128,512]{1,0:T(8,128)S(1)}, u32[]{:S(2)}, u32[]{:S(2)}) collective-permute-start(f32[128,512]{1,0:T(8,128)S(1)} %get-tuple-element.142), channel_id=1, source_target_pairs={{0,4},{2,6},{4,0},{6,2},{8,12},{10,14},{12,8},{14,10},{16,20},{18,... | collective-permute-start | bytes 786440 | tf_op jit(solution)/shard_map/ppermute | solution.py:17
  36.8 28.4 %collective-permute-start.21 = (f32[2,4,32,256]{3,2,1,0:T(8,128)S(1)}, f32[2,4,32,256]{3,2,1,0:T(8,128)S(1)}, u32[]{:S(2)}, u32[]{:S(2)}) collective-permute-start(f32[2,4,32,256]{3,2,1,0:T(8,128)S(1)} %get-tuple-element.139), channel_id=1, source_target_pairs={{0,24},{2,26},{4,28},{6,30},{8,16},{10,18},{12,20},{14,22},{16,8},... | collective-permute-start | bytes 786440 | tf_op jit(solution)/shard_map/ppermute | solution.py:327
  39.6 15.0 %collective-permute-start.19 = (f32[2,4,32,256]{3,2,1,0:T(8,128)S(1)}, f32[2,4,32,256]{3,2,1,0:T(8,128)S(1)}, u32[]{:S(2)}, u32[]{:S(2)}) collective-permute-start(f32[2,4,32,256]{3,2,1,0:T(8,128)S(1)} %get-tuple-element.154), channel_id=1, source_target_pairs={{0,8},{2,10},{4,12},{6,14},{8,0},{10,2},{12,4},{14,6},{16,24},{18,... | collective-permute-start | bytes 786440 | tf_op jit(solution)/shard_map/ppermute | solution.py:327
  46.4 15.4 %collective-permute-start.20 = (f32[2,4,32,256]{3,2,1,0:T(8,128)S(1)}, f32[2,4,32,256]{3,2,1,0:T(8,128)S(1)}, u32[]{:S(2)}, u32[]{:S(2)}) collective-permute-start(f32[2,4,32,256]{3,2,1,0:T(8,128)S(1)} %get-tuple-element.155), channel_id=1, source_target_pairs={{0,16},{2,18},{4,20},{6,22},{8,24},{10,26},{12,28},{14,30},{16,0},... | collective-permute-start | bytes 786440 | tf_op jit(solution)/shard_map/ppermute | solution.py:327
  50.3 16.2 %collective-permute-start.22 = (f32[2,4,32,256]{3,2,1,0:T(8,128)S(1)}, f32[2,4,32,256]{3,2,1,0:T(8,128)S(1)}, u32[]{:S(2)}, u32[]{:S(2)}) collective-permute-start(f32[2,4,32,256]{3,2,1,0:T(8,128)S(1)} %get-tuple-element.160), channel_id=1, source_target_pairs={{0,2},{2,0},{4,6},{6,4},{8,10},{10,8},{12,14},{14,12},{16,18},{18,... | collective-permute-start | bytes 786440 | tf_op jit(solution)/shard_map/ppermute | solution.py:327
  51.7 16.3 %collective-permute-start.23 = (f32[2,4,32,256]{3,2,1,0:T(8,128)S(1)}, f32[2,4,32,256]{3,2,1,0:T(8,128)S(1)}, u32[]{:S(2)}, u32[]{:S(2)}) collective-permute-start(f32[2,4,32,256]{3,2,1,0:T(8,128)S(1)} %get-tuple-element.161), channel_id=1, source_target_pairs={{0,4},{2,6},{4,0},{6,2},{8,12},{10,14},{12,8},{14,10},{16,20},{18,... | collective-permute-start | bytes 786440 | tf_op jit(solution)/shard_map/ppermute | solution.py:327
  54.5 14.3 %collective-permute-start.24 = (f32[2,4,32,256]{3,2,1,0:T(8,128)S(1)}, f32[2,4,32,256]{3,2,1,0:T(8,128)S(1)}, u32[]{:S(2)}, u32[]{:S(2)}) collective-permute-start(f32[2,4,32,256]{3,2,1,0:T(8,128)S(1)} %get-tuple-element.149), channel_id=1, source_target_pairs={{0,6},{2,4},{4,2},{6,0},{8,14},{10,12},{12,10},{14,8},{16,22},{18,... | collective-permute-start | bytes 786440 | tf_op jit(solution)/shard_map/ppermute | solution.py:327
  61.8 12.9 %collective-permute-start.25 = (f32[512,128]{1,0:T(8,128)S(1)}, f32[512,128]{1,0:T(8,128)S(1)}, u32[]{:S(2)}, u32[]{:S(2)}) collective-permute-start(f32[512,128]{1,0:T(8,128)S(1)} %shard_map.115.refs_4_.refs_0_.refs_12_), channel_id=1, source_target_pairs={{0,16},{2,18},{4,20},{6,22},{8,24},{10,26},{12,28},{14,30},{16,0},... | collective-permute-start | bytes 786440 | tf_op jit(solution)/shard_map/ppermute | solution.py:17
  65.3 12.8 %collective-permute-start.26 = (f32[2,4,32,256]{3,2,1,0:T(8,128)S(1)}, f32[2,4,32,256]{3,2,1,0:T(8,128)S(1)}, u32[]{:S(2)}, u32[]{:S(2)}) collective-permute-start(f32[2,4,32,256]{3,2,1,0:T(8,128)S(1)} %get-tuple-element.168), channel_id=1, source_target_pairs={{0,2},{2,0},{4,6},{6,4},{8,10},{10,8},{12,14},{14,12},{16,18},{18,... | collective-permute-start | bytes 786440 | tf_op jit(solution)/shard_map/ppermute | solution.py:327
  66.5 11.6 %collective-permute-start.27 = (f32[2,4,32,256]{3,2,1,0:T(8,128)S(1)}, f32[2,4,32,256]{3,2,1,0:T(8,128)S(1)}, u32[]{:S(2)}, u32[]{:S(2)}) collective-permute-start(f32[2,4,32,256]{3,2,1,0:T(8,128)S(1)} %get-tuple-element.169), channel_id=1, source_target_pairs={{0,4},{2,6},{4,0},{6,2},{8,12},{10,14},{12,8},{14,10},{16,20},{18,... | collective-permute-start | bytes 786440 | tf_op jit(solution)/shard_map/ppermute | solution.py:327
  68.0 14.8 %collective-permute-start.28 = (f32[2,4,32,256]{3,2,1,0:T(8,128)S(1)}, f32[2,4,32,256]{3,2,1,0:T(8,128)S(1)}, u32[]{:S(2)}, u32[]{:S(2)}) collective-permute-start(f32[2,4,32,256]{3,2,1,0:T(8,128)S(1)} %get-tuple-element.158), channel_id=1, source_target_pairs={{0,6},{2,4},{4,2},{6,0},{8,14},{10,12},{12,10},{14,8},{16,22},{18,... | collective-permute-start | bytes 786440 | tf_op jit(solution)/shard_map/ppermute | solution.py:327
  68.9 15.1 %collective-permute-start.29 = (f32[128,512]{1,0:T(8,128)S(1)}, f32[128,512]{1,0:T(8,128)S(1)}, u32[]{:S(2)}, u32[]{:S(2)}) collective-permute-start(f32[128,512]{1,0:T(8,128)S(1)} %get-tuple-element.171), channel_id=1, source_target_pairs={{0,2},{2,0},{4,6},{6,4},{8,10},{10,8},{12,14},{14,12},{16,18},{18,... | collective-permute-start | bytes 786440 | tf_op jit(solution)/shard_map/ppermute | solution.py:17
  74.8 14.7 %collective-permute-start.31 = (f32[2,4,32,256]{3,2,1,0:T(8,128)S(1)}, f32[2,4,32,256]{3,2,1,0:T(8,128)S(1)}, u32[]{:S(2)}, u32[]{:S(2)}) collective-permute-start(f32[2,4,32,256]{3,2,1,0:T(8,128)S(1)} %get-tuple-element.183), channel_id=1, source_target_pairs={{0,8},{2,10},{4,12},{6,14},{8,0},{10,2},{12,4},{14,6},{16,24},{18,... | collective-permute-start | bytes 786440 | tf_op jit(solution)/shard_map/ppermute | solution.py:327
  78.1 18.0 %collective-permute-start.30 = (f32[2,4,32,256]{3,2,1,0:T(8,128)S(1)}, f32[2,4,32,256]{3,2,1,0:T(8,128)S(1)}, u32[]{:S(2)}, u32[]{:S(2)}) collective-permute-start(f32[2,4,32,256]{3,2,1,0:T(8,128)S(1)} %get-tuple-element.180), channel_id=1, source_target_pairs={{0,16},{2,18},{4,20},{6,22},{8,24},{10,26},{12,28},{14,30},{16,0},... | collective-permute-start | bytes 786440 | tf_op jit(solution)/shard_map/ppermute | solution.py:327
  78.2 24.5 %collective-permute-start.32 = (f32[2,4,32,256]{3,2,1,0:T(8,128)S(1)}, f32[2,4,32,256]{3,2,1,0:T(8,128)S(1)}, u32[]{:S(2)}, u32[]{:S(2)}) collective-permute-start(f32[2,4,32,256]{3,2,1,0:T(8,128)S(1)} %get-tuple-element.162), channel_id=1, source_target_pairs={{0,24},{2,26},{4,28},{6,30},{8,16},{10,18},{12,20},{14,22},{16,8},... | collective-permute-start | bytes 786440 | tf_op jit(solution)/shard_map/ppermute | solution.py:327
